TPU v7x, 32 devices: a whole 2x2x4 slice. The times are simulated.
32 devices in a mesh: dp: 8 (over y, x, core), tensor: 4 (over z).
Axes of the slice: x: 2, y: 2, z: 4, core: 2. Of those that a mesh axis runs over, the one named last changes fastest.
Arguments:
- tokens: bfloat16 [3072, 1536], P('dp'), may hold values from -6 to 6
- cotangent: bfloat16 [3072, 1536], P('dp'), may hold values from -6 to 6
- dest: int32 [3072], P('dp'), may hold values from 0 to 3071, as said below
- source: int32 [3072], P('dp'), may hold values from 0 to 3071, as said below
- lengths: int32 [24, 4], P('dp'), may hold values from 1 to 96, 128 in all within a row
- persist: bfloat16 [64, 1536], P(None, 'dp'), may hold values from -6 to 6
- gain_attn: bfloat16 [1536], P('dp'), may hold values from 0.5 to 1.5
- w_query_mem: bfloat16 [1536, 1536], P('tensor', 'dp'), may hold values from -0.15625 to 0.15625
- mem_in: bfloat16 [1536, 6144], P('dp', 'tensor'), may hold values from -0.15625 to 0.15625
- mem_out: bfloat16 [6144, 1536], P('tensor', 'dp'), may hold values from -0.078125 to 0.078125
- w_query: bfloat16 [1536, 1536], P('dp', 'tensor'), may hold values from -0.15625 to 0.15625
- w_key: bfloat16 [1536, 1536], P('dp', 'tensor'), may hold values from -0.15625 to 0.15625
- w_value: bfloat16 [1536, 1536], P('dp', 'tensor'), may hold values from -0.15625 to 0.15625
- w_output: bfloat16 [1536, 1536], P('tensor', 'dp'), may hold values from -0.4375 to 0.4375
- gain_mem: bfloat16 [1536], P('dp'), may hold values from 0.5 to 1.5
- w_key_mem: bfloat16 [1536, 1536], P('tensor', 'dp'), may hold values from -0.15625 to 0.15625
- w_value_mem: bfloat16 [1536, 1536], P('tensor', 'dp'), may hold values from -0.15625 to 0.15625
- w_rate: bfloat16 [1536], P('dp'), may hold values from -0.3125 to 0.3125
- gain_ffn: bfloat16 [1536], P('dp'), may hold values from 0.5 to 1.5
- w_gate: bfloat16 [1536, 4096], P('dp', 'tensor'), may hold values from -0.15625 to 0.15625
- w_up: bfloat16 [1536, 4096], P('dp', 'tensor'), may hold values from -0.15625 to 0.15625
- w_down: bfloat16 [4096, 1536], P('tensor', 'dp'), may hold values from -0.09375 to 0.09375
Outputs:
- output: bfloat16 [3072, 1536], P('dp')
- grad_tokens: bfloat16 [3072, 1536], P('dp')
- grad_persist: float32 [64, 1536], P(None, 'dp')
- grad_gain_attn: float32 [1536], P('dp')
- grad_w_query_mem: float32 [1536, 1536], P('tensor', 'dp')
- grad_mem_in: float32 [1536, 6144], P('dp', 'tensor')
- grad_mem_out: float32 [6144, 1536], P('tensor', 'dp')
- grad_w_query: float32 [1536, 1536], P('dp', 'tensor')
- grad_w_key: float32 [1536, 1536], P('dp', 'tensor')
- grad_w_value: float32 [1536, 1536], P('dp', 'tensor')
- grad_w_output: float32 [1536, 1536], P('tensor', 'dp')
- grad_gain_mem: float32 [1536], P('dp')
- grad_w_key_mem: float32 [1536, 1536], P('tensor', 'dp')
- grad_w_value_mem: float32 [1536, 1536], P('tensor', 'dp')
- grad_w_rate: float32 [1536], P('dp')
- grad_gain_ffn: float32 [1536], P('dp')
- grad_w_gate: float32 [1536, 4096], P('dp', 'tensor')
- grad_w_up: float32 [1536, 4096], P('dp', 'tensor')
- grad_w_down: float32 [4096, 1536], P('tensor', 'dp')
Inputs may be any that keep to these rules, and one draw needn't show every extreme that they name: A permutation of the 3072 positions: dest gives each token's place in the dealt order, in which index d of dp holds places d * 384 to (d + 1) * 384 - 1. The tokens that one index of dp holds go exactly 48 to each index of dp. `source`: the inverse permutation of dest. `lengths`: each row sums to 128; its longest sequence has exactly 96 tokens.
All inputs are finite; a program needn't handle non-finite values.
Results may differ from a plain program's by a relative error of at most 0.025.
Values may be sent and summed in bfloat16 or wider, within the bound.
A program may use at most 320 MiB of HBM per device.

v0:
```python
import functools

import jax
import jax.numpy as jnp
from jax import lax
from jax.sharding import PartitionSpec as P

HD = 96


EPSILON = 1e-06
RATE_SCALE = 4e-05
NEG_LARGE = -1e30
HIGH = lax.Precision.HIGHEST


def value_plain(operand):
    return lax.optimization_barrier(operand.astype(jnp.bfloat16)).astype(jnp.float32)


def same_value(operand):
    return operand


def value_keep(operand):
    return (value_plain(operand), None)


def value_pass(stored, incoming):
    return (incoming,)


def grad_keep(operand):
    return (operand, None)


def grad_lower(stored, incoming):
    return (value_plain(incoming),)


def value_round(operand):
    rounder = jax.custom_vjp(value_plain)
    rounder.defvjp(value_keep, value_pass)
    return rounder(operand)


def grad_round(operand):
    rounder = jax.custom_vjp(same_value)
    rounder.defvjp(grad_keep, grad_lower)
    return rounder(operand)


def round_both(operand):
    return value_round(grad_round(operand))


def matmul(left_side, right_side):
    return jnp.dot(left_side, right_side, precision=HIGH, preferred_element_type=jnp.float32)


def rounded_dot(left_side, right_side):
    return jnp.dot(left_side, right_side, preferred_element_type=jnp.float32)


def rms_norm(operand, scaling):
    return (
        operand * lax.rsqrt(jnp.mean(operand * operand, axis=-1, keepdims=True) + EPSILON) * scaling
    )


def silu_slope(operand):
    sigma = jax.nn.sigmoid(operand)
    return sigma * (1.0 + operand * (1.0 - sigma))


def causal_mask(lens_row, row_count):
    position = jnp.arange(row_count, dtype=jnp.int32)
    bounds = jnp.cumsum(lens_row)
    segment = jnp.sum((position[:, None] >= bounds[None, :]).astype(jnp.int32), axis=1)
    same = segment[:, None] == segment[None, :]
    return same & (position[None, :] <= position[:, None])


def tensor_sum(operand):
    return lax.psum(operand, "tensor")


def attend(normed_in, memory_tokens, persistent, w_query, w_key, w_value, w_output, causal):
    row_count = normed_in.shape[0]
    head_count = w_query.shape[1] // HD
    query = round_both(rounded_dot(normed_in, w_query)).reshape(row_count, head_count, HD)
    context = jnp.concatenate([persistent, memory_tokens, normed_in], axis=0)
    keys = round_both(rounded_dot(context, w_key)).reshape(-1, head_count, HD)
    values = round_both(rounded_dot(context, w_value)).reshape(-1, head_count, HD)
    allowed = jnp.concatenate(
        [jnp.ones((row_count, persistent.shape[0]), dtype=bool), causal, causal], axis=1
    )
    scores = jnp.einsum("qhd,khd->hqk", query, keys, preferred_element_type=jnp.float32) * HD ** (
        -0.5
    )
    scores = grad_round(scores)
    scores = jnp.where(allowed[None], scores, NEG_LARGE)
    weights = jax.nn.softmax(scores, axis=-1)
    mixed = jnp.einsum(
        "hqk,khd->qhd", value_round(weights), values, preferred_element_type=jnp.float32
    ).reshape(row_count, head_count * HD)
    return rounded_dot(round_both(mixed), w_output)


def micro_batch(inputs, upstream, lens_row, params, part_index):
    (
        persist,
        gain_attn,
        w_query_mem,
        mem_in,
        mem_out,
        w_query,
        w_key,
        w_value,
        w_output,
        gain_mem,
        w_key_mem,
        w_value_mem,
        w_rate,
        gain_ffn,
        w_gate,
        w_up,
        w_down,
    ) = params
    slice_width = w_query_mem.shape[0]
    causal = causal_mask(lens_row, inputs.shape[0])

    def own_columns(operand):
        return lax.dynamic_slice_in_dim(operand, part_index * slice_width, slice_width, 1)

    normed_pre, pull_first = jax.vjp(rms_norm, inputs, gain_attn)
    normed_in = value_round(normed_pre)

    def query_piece(normed_part, weight_part):
        return rounded_dot(own_columns(normed_part), weight_part)

    query_part, pull_query = jax.vjp(query_piece, normed_in, w_query_mem)
    query_mem = value_round(tensor_sum(query_part))

    def read_piece(query_low, weight_in, weight_out):
        hidden = value_round(jax.nn.silu(grad_round(rounded_dot(query_low, weight_in))))
        return rounded_dot(hidden, weight_out)

    read_part, pull_read = jax.vjp(read_piece, query_mem, mem_in, mem_out)
    memory_tokens = value_round(tensor_sum(read_part))
    persistent = value_round(persist)
    attn_part, pull_attn = jax.vjp(
        functools.partial(attend, causal=causal),
        normed_in,
        memory_tokens,
        persistent,
        w_query,
        w_key,
        w_value,
        w_output,
    )
    after_attn = inputs + tensor_sum(attn_part)

    def rate_piece(residual, scaling, rate_weight):
        normed_mid = rms_norm(residual, scaling)
        return (
            normed_mid,
            RATE_SCALE * 2.0 * jax.nn.sigmoid(jnp.dot(normed_mid, rate_weight, precision=HIGH)),
        )

    (normed_mid, rate), pull_mid = jax.vjp(rate_piece, after_attn, gain_mem, w_rate)
    normed_low = value_round(normed_mid)

    def pair_piece(normed_part, weight_key, weight_value):
        own_part = own_columns(normed_part)
        return (rounded_dot(own_part, weight_key), matmul(own_part, weight_value))

    (key_part, value_part), pull_pair = jax.vjp(pair_piece, normed_low, w_key_mem, w_value_mem)
    key_sum, value_mem = lax.psum((key_part, value_part), "tensor")
    key_mem = value_round(key_sum)

    def key_piece(key_low, weight_in, weight_out):
        key_hidden = grad_round(rounded_dot(key_low, weight_in))
        key_act = value_round(jax.nn.silu(key_hidden))
        return (key_hidden, key_act, matmul(key_act, weight_out))

    (key_hidden, key_act, predict_part), pull_key = jax.vjp(key_piece, key_mem, mem_in, mem_out)
    predicted = tensor_sum(predict_part)

    def error_piece(predict_sum, value_sum, rate_rows):
        return rate_rows[:, None] * (predict_sum - value_sum)

    error_pre, pull_error = jax.vjp(error_piece, predicted, value_mem, rate)
    error_step = value_round(error_pre)

    def update_piece(key_low, hidden_in, act_in, error_low, weight_out):
        back_hidden = round_both(matmul(error_low, weight_out.T) * silu_slope(hidden_in))
        gram = jnp.where(causal, matmul(key_low, key_low.T), 0.0)
        new_hidden = grad_round(hidden_in - matmul(gram, back_hidden))
        new_act = value_round(jax.nn.silu(new_hidden))
        pair_act = jnp.where(causal, matmul(new_act, act_in.T), 0.0)
        return rounded_dot(new_act, weight_out) - matmul(pair_act, error_low)

    update_part, pull_update = jax.vjp(
        update_piece, key_mem, key_hidden, key_act, error_step, mem_out
    )
    after_mem = after_attn + tensor_sum(update_part)
    normed_third, pull_third = jax.vjp(rms_norm, after_mem, gain_ffn)
    normed_ffn = value_round(normed_third)

    def ffn_piece(normed_part, weight_gate, weight_up, weight_down):
        gate = grad_round(rounded_dot(normed_part, weight_gate))
        up_part = grad_round(rounded_dot(normed_part, weight_up))
        return rounded_dot(value_round(jax.nn.silu(gate) * up_part), weight_down)

    ffn_part, pull_ffn = jax.vjp(ffn_piece, normed_ffn, w_gate, w_up, w_down)
    result = after_mem + tensor_sum(ffn_part)
    d_normed_ffn, g_gate, g_up, g_down = pull_ffn(value_round(upstream))
    d_mem_norm, g_gain_ffn = pull_third(tensor_sum(d_normed_ffn))
    d_after_mem = upstream + d_mem_norm
    d_key_update, d_hidden_update, d_act_update, d_error_part, g_out_update = pull_update(
        value_round(d_after_mem)
    )
    d_error = value_round(tensor_sum(d_error_part))
    d_predicted, d_value_mem, d_rate = pull_error(d_error)
    d_key_own, g_in_key, g_out_key = pull_key((d_hidden_update, d_act_update, d_predicted))
    d_key = value_round(tensor_sum(d_key_update + d_key_own))
    d_normed_low, g_key_mem, g_value_mem = pull_pair((d_key, d_value_mem))
    d_attn_norm, g_gain_mem, g_rate = pull_mid((tensor_sum(d_normed_low), d_rate))
    d_after_attn = d_after_mem + d_attn_norm
    d_normed_attn, d_memory, d_persist, g_query, g_key, g_value, g_output = pull_attn(
        value_round(d_after_attn)
    )
    d_query_low, g_in_read, g_out_read = pull_read(value_round(tensor_sum(d_memory)))
    d_normed_query, g_query_mem = pull_query(value_round(tensor_sum(d_query_low)))
    d_input_norm, g_gain_attn = pull_first(tensor_sum(d_normed_attn + d_normed_query))
    d_inputs = d_after_attn + d_input_norm
    gradients = (
        d_persist,
        g_gain_attn,
        g_query_mem,
        g_in_read + g_in_key,
        g_out_read + g_out_key + g_out_update,
        g_query,
        g_key,
        g_value,
        g_output,
        g_gain_mem,
        g_key_mem,
        g_value_mem,
        g_rate,
        g_gain_ffn,
        g_gate,
        g_up,
        g_down,
    )
    return (result, d_inputs, gradients)


def per_device(
    tokens,
    cotangent,
    dest,
    source,
    lengths,
    persist,
    gain_attn,
    w_query_mem,
    mem_in,
    mem_out,
    w_query,
    w_key,
    w_value,
    w_output,
    gain_mem,
    w_key_mem,
    w_value_mem,
    w_rate,
    gain_ffn,
    w_gate,
    w_up,
    w_down,
):
    tok_count = tokens.shape[0]
    send_order = jnp.argsort(dest // tok_count, stable=True)
    recv_order = jnp.argsort(source, stable=True)
    arrived_tokens, arrived_cot = (
        lax.all_to_all(tokens[send_order], "dp", split_axis=0, concat_axis=0, tiled=True),
        lax.all_to_all(cotangent[send_order], "dp", split_axis=0, concat_axis=0, tiled=True),
    )
    dealt_tokens = (
        jnp.zeros_like(arrived_tokens).at[recv_order].set(arrived_tokens).astype(jnp.float32)
    )
    dealt_cot = jnp.zeros_like(arrived_cot).at[recv_order].set(arrived_cot).astype(jnp.float32)
    batch_count = lengths.shape[0]
    row_count = tok_count // batch_count
    part_index = lax.axis_index("tensor")
    summed = None
    results = []
    input_grads = []
    for batch in range(batch_count):
        gathered = (
            lax.all_gather(persist, "dp", axis=1, tiled=True),
            lax.all_gather(gain_attn, "dp", axis=0, tiled=True),
            lax.all_gather(w_query_mem, "dp", axis=1, tiled=True),
            lax.all_gather(mem_in, "dp", axis=0, tiled=True),
            lax.all_gather(mem_out, "dp", axis=1, tiled=True),
            lax.all_gather(w_query, "dp", axis=0, tiled=True),
            lax.all_gather(w_key, "dp", axis=0, tiled=True),
            lax.all_gather(w_value, "dp", axis=0, tiled=True),
            lax.all_gather(w_output, "dp", axis=1, tiled=True),
            lax.all_gather(gain_mem, "dp", axis=0, tiled=True),
            lax.all_gather(w_key_mem, "dp", axis=1, tiled=True),
            lax.all_gather(w_value_mem, "dp", axis=1, tiled=True),
            lax.all_gather(w_rate, "dp", axis=0, tiled=True),
            lax.all_gather(gain_ffn, "dp", axis=0, tiled=True),
            lax.all_gather(w_gate, "dp", axis=0, tiled=True),
            lax.all_gather(w_up, "dp", axis=0, tiled=True),
            lax.all_gather(w_down, "dp", axis=1, tiled=True),
        )
        params = tuple((member.astype(jnp.float32) for member in gathered))
        lower = batch * row_count
        result, d_inputs, gradients = micro_batch(
            dealt_tokens[lower : lower + row_count],
            dealt_cot[lower : lower + row_count],
            lengths[batch],
            params,
            part_index,
        )
        results.append(result.astype(jnp.bfloat16))
        input_grads.append(d_inputs.astype(jnp.bfloat16))
        summed = gradients if summed is None else jax.tree.map(jnp.add, summed, gradients)
    (
        g_persist,
        g_gain_attn,
        g_query_mem,
        g_mem_in,
        g_mem_out,
        g_query,
        g_key,
        g_value,
        g_output,
        g_gain_mem,
        g_key_mem,
        g_value_mem,
        g_rate,
        g_gain_ffn,
        g_gate,
        g_up,
        g_down,
    ) = summed
    g_persist = tensor_sum(g_persist)
    shares = (
        lax.psum_scatter(
            g_persist.astype(jnp.bfloat16), "dp", scatter_dimension=1, tiled=True
        ).astype(jnp.float32),
        lax.psum_scatter(
            g_gain_attn.astype(jnp.bfloat16), "dp", scatter_dimension=0, tiled=True
        ).astype(jnp.float32),
        lax.psum_scatter(
            g_query_mem.astype(jnp.bfloat16), "dp", scatter_dimension=1, tiled=True
        ).astype(jnp.float32),
        lax.psum_scatter(
            g_mem_in.astype(jnp.bfloat16), "dp", scatter_dimension=0, tiled=True
        ).astype(jnp.float32),
        lax.psum_scatter(
            g_mem_out.astype(jnp.bfloat16), "dp", scatter_dimension=1, tiled=True
        ).astype(jnp.float32),
        lax.psum_scatter(
            g_query.astype(jnp.bfloat16), "dp", scatter_dimension=0, tiled=True
        ).astype(jnp.float32),
        lax.psum_scatter(g_key.astype(jnp.bfloat16), "dp", scatter_dimension=0, tiled=True).astype(
            jnp.float32
        ),
        lax.psum_scatter(
            g_value.astype(jnp.bfloat16), "dp", scatter_dimension=0, tiled=True
        ).astype(jnp.float32),
        lax.psum_scatter(
            g_output.astype(jnp.bfloat16), "dp", scatter_dimension=1, tiled=True
        ).astype(jnp.float32),
        lax.psum_scatter(
            g_gain_mem.astype(jnp.bfloat16), "dp", scatter_dimension=0, tiled=True
        ).astype(jnp.float32),
        lax.psum_scatter(
            g_key_mem.astype(jnp.bfloat16), "dp", scatter_dimension=1, tiled=True
        ).astype(jnp.float32),
        lax.psum_scatter(
            g_value_mem.astype(jnp.bfloat16), "dp", scatter_dimension=1, tiled=True
        ).astype(jnp.float32),
        lax.psum_scatter(g_rate.astype(jnp.bfloat16), "dp", scatter_dimension=0, tiled=True).astype(
            jnp.float32
        ),
        lax.psum_scatter(
            g_gain_ffn.astype(jnp.bfloat16), "dp", scatter_dimension=0, tiled=True
        ).astype(jnp.float32),
        lax.psum_scatter(g_gate.astype(jnp.bfloat16), "dp", scatter_dimension=0, tiled=True).astype(
            jnp.float32
        ),
        lax.psum_scatter(g_up.astype(jnp.bfloat16), "dp", scatter_dimension=0, tiled=True).astype(
            jnp.float32
        ),
        lax.psum_scatter(g_down.astype(jnp.bfloat16), "dp", scatter_dimension=1, tiled=True).astype(
            jnp.float32
        ),
    )
    dealt_out = jnp.concatenate(results, axis=0)
    dealt_grad = jnp.concatenate(input_grads, axis=0)
    back_out, back_grad = (
        lax.all_to_all(dealt_out[recv_order], "dp", split_axis=0, concat_axis=0, tiled=True),
        lax.all_to_all(dealt_grad[recv_order], "dp", split_axis=0, concat_axis=0, tiled=True),
    )
    output = jnp.zeros_like(back_out).at[send_order].set(back_out)
    grad_tokens = jnp.zeros_like(back_grad).at[send_order].set(back_grad)
    return (
        output,
        grad_tokens,
        shares[0],
        shares[1],
        shares[2],
        shares[3],
        shares[4],
        shares[5],
        shares[6],
        shares[7],
        shares[8],
        shares[9],
        shares[10],
        shares[11],
        shares[12],
        shares[13],
        shares[14],
        shares[15],
        shares[16],
    )


def solution(mesh):
    placed = (
        P("dp", None),
        P("dp", None),
        P("dp"),
        P("dp"),
        P("dp", None),
        P(None, "dp"),
        P("dp"),
        P("tensor", "dp"),
        P("dp", "tensor"),
        P("tensor", "dp"),
        P("dp", "tensor"),
        P("dp", "tensor"),
        P("dp", "tensor"),
        P("tensor", "dp"),
        P("dp"),
        P("tensor", "dp"),
        P("tensor", "dp"),
        P("dp"),
        P("dp"),
        P("dp", "tensor"),
        P("dp", "tensor"),
        P("tensor", "dp"),
    )
    return jax.shard_map(
        per_device,
        mesh=mesh,
        in_specs=placed,
        out_specs=(
            P("dp", None),
            P("dp", None),
            P(None, "dp"),
            P("dp"),
            P("tensor", "dp"),
            P("dp", "tensor"),
            P("tensor", "dp"),
            P("dp", "tensor"),
            P("dp", "tensor"),
            P("dp", "tensor"),
            P("tensor", "dp"),
            P("dp"),
            P("tensor", "dp"),
            P("tensor", "dp"),
            P("dp"),
            P("dp"),
            P("dp", "tensor"),
            P("dp", "tensor"),
            P("tensor", "dp"),
        ),
        check_vma=False,
    )
```

profile of v0, /device:TPU:0, one launch (start us, length us, event | category | flops | bytes accessed | tf_op | source)
XLA Modules:
  0.0 2408.2 jit_solution(17926963638653563303)
XLA Ops:
  95.8 82.0 %all-reduce.48 = (bf16[128,1536]{1,0:T(8,128)(2,1)}, bf16[128,1536]{1,0:T(8,128)(2,1)}, bf16[128,1536]{1,0:T(8,128)(2,1)}) all-reduce(f32[128,1536]{1,0:T(8,128)} %fusion.187, f32[128,1536]{1,0:T(8,128)} %fusion.190, f32[128,1536]{1,0:T(8,128)} %fusion.194), channel_id=1, replica_groups=mesh['dp'=8,'tensor'=4] {'tensor'}, use_global_device_ids=true, to_apply=%region_34.35 | all-reduce | flops 589824 | bytes 3538944 | tf_op jit(solution)/shard_map/psum | solution.py:85
  210.8 81.3 %all-reduce.49 = (bf16[128,1536]{1,0:T(8,128)(2,1)S(1)}, bf16[128,1536]{1,0:T(8,128)(2,1)}, bf16[128,1536]{1,0:T(8,128)(2,1)}) all-reduce(f32[128,1536]{1,0:T(8,128)} %fusion.314, f32[128,1536]{1,0:T(8,128)} %fusion.308, f32[128,1536]{1,0:T(8,128)} %fusion.302), channel_id=1, replica_groups=mesh['dp'=8,'tensor'=4] {'tensor'}, use_global_device_ids=true, to_apply=%region_35.36 | all-reduce | flops 589824 | bytes 3538944 | tf_op jit(solution)/shard_map/psum | solution.py:85
  336.1 98.9 %all-reduce.47.cloned.1.call-done = (f32[128,1536]{1,0:T(8,128)}, f32[128,1536]{1,0:T(8,128)}, f32[128,1536]{1,0:T(8,128)}) async-done(((f32[128,1536]{1,0:T(8,128)}, f32[128,1536]{1,0:T(8,128)}, f32[128,1536]{1,0:T(8,128)}), (f32[128,1536]{1,0:T(8,128)}, f32[128,1536]{1,0:T(8,128)}, f32[128,1536]{1,0:T(8,128)})) %all-reduce.47.cloned.1.call-update) | async-done | bytes 2359312 | tf_op jit(solution)/shard_map/psum | solution.py:85
  465.5 88.5 %all-reduce.50 = (bf16[128,1536]{1,0:T(8,128)(2,1)}, bf16[128,1536]{1,0:T(8,128)(2,1)S(1)}, bf16[128,1536]{1,0:T(8,128)(2,1)S(1)}) all-reduce(f32[128,1536]{1,0:T(8,128)} %fusion.203, f32[128,1536]{1,0:T(8,128)} %fusion.209, f32[128,1536]{1,0:T(8,128)} %fusion.216), channel_id=1, replica_groups=mesh['dp'=8,'tensor'=4] {'tensor'}, use_global_device_ids=true, to_apply=%region_42.43 | all-reduce | flops 589824 | bytes 3538944 | tf_op jit(solution)/shard_map/psum | solution.py:179
  589.2 161.2 %all-reduce.45.cloned.1.call-done = (f32[128,1536]{1,0:T(8,128)}, f32[128,1536]{1,0:T(8,128)}, f32[128,1536]{1,0:T(8,128)}, f32[128,1536]{1,0:T(8,128)}, f32[128,1536]{1,0:T(8,128)}, /*index=5*/f32[128,1536]{1,0:T(8,128)}) async-done(((f32[128,1536]{1,0:T(8,128)}, f32[128,1536]{1,0:T(8,128)}, f32[128,1536]{1,0:T(8,128)}, f32[128,1536]{1,0:T(8,128)}, f32[128,1536]{1,0:T(8,128)}, ...) | async-done | bytes 4718608 | tf_op jit(solution)/shard_map/psum | solution.py:85
  814.2 66.4 %all-reduce.43.cloned.1.call-done = (f32[128,1536]{1,0:T(8,128)}, f32[128,1536]{1,0:T(8,128)}, f32[128,1536]{1,0:T(8,128)}) async-done(((f32[128,1536]{1,0:T(8,128)}, f32[128,1536]{1,0:T(8,128)}, f32[128,1536]{1,0:T(8,128)}), (f32[128,1536]{1,0:T(8,128)}, f32[128,1536]{1,0:T(8,128)}, f32[128,1536]{1,0:T(8,128)})) %all-reduce.43.cloned.1.call-update) | async-done | bytes 2359312 | tf_op jit(solution)/shard_map/psum | solution.py:85
  917.1 30.5 %all-gather.32.cloned.1.call-done = bf16[1536,1024]{1,0:T(8,128)(2,1)} async-done(((bf16[192,1024]{1,0:T(8,128)(2,1)}), bf16[1536,1024]{1,0:T(8,128)(2,1)}) %all-gather.32.cloned.1.call-update) | async-done | bytes 3145744 | tf_op jit(solution)/shard_map/all_gather | solution.py:317
  972.2 90.0 %all-reduce.41.cloned.1.call-done = (f32[128,1536]{1,0:T(8,128)}, f32[128,1536]{1,0:T(8,128)}, f32[128,1536]{1,0:T(8,128)}) async-done(((f32[128,1536]{1,0:T(8,128)}, f32[128,1536]{1,0:T(8,128)}, f32[128,1536]{1,0:T(8,128)}), (f32[128,1536]{1,0:T(8,128)}, f32[128,1536]{1,0:T(8,128)}, f32[128,1536]{1,0:T(8,128)})) %all-reduce.41.cloned.1.call-update) | async-done | bytes 2359312 | tf_op jit(solution)/shard_map/psum | solution.py:85
  1104.2 86.1 %all-reduce.51 = (bf16[128,1536]{1,0:T(8,128)(2,1)S(1)}, bf16[128,1536]{1,0:T(8,128)(2,1)S(1)}, bf16[128,1536]{1,0:T(8,128)(2,1)S(1)}) all-reduce(f32[128,1536]{1,0:T(8,128)} %convolution_add_fusion.33, f32[128,1536]{1,0:T(8,128)} %convolution_add_fusion.38, ...), channel_id=1, replica_groups=mesh['dp'=8,'tensor'=4] {'tensor'}, use_global_device_ids=true, to_apply=%region_76.77 | all-reduce | flops 589824 | bytes 3538944 | tf_op jit(solution)/shard_map/psum | solution.py:85
  1216.7 82.9 %all-reduce.52 = (bf16[128,1536]{1,0:T(8,128)(2,1)}, bf16[128,1536]{1,0:T(8,128)(2,1)}, bf16[128,1536]{1,0:T(8,128)(2,1)}) all-reduce(f32[128,1536]{1,0:T(8,128)} %fusion.19, f32[128,1536]{1,0:T(8,128)} %fusion.20, f32[128,1536]{1,0:T(8,128)} %fusion.21), channel_id=1, replica_groups=mesh['dp'=8,'tensor'=4] {'tensor'}, use_global_device_ids=true, to_apply=%region_77.78 | all-reduce | flops 589824 | bytes 3538944 | tf_op jit(solution)/shard_map/psum | solution.py:85
  1316.1 84.0 %all-reduce.39.cloned.1.call-done = (f32[128,1536]{1,0:T(8,128)}, f32[128,1536]{1,0:T(8,128)}, f32[128,1536]{1,0:T(8,128)}) async-done(((f32[128,1536]{1,0:T(8,128)}, f32[128,1536]{1,0:T(8,128)}, f32[128,1536]{1,0:T(8,128)}), (f32[128,1536]{1,0:T(8,128)}, f32[128,1536]{1,0:T(8,128)}, f32[128,1536]{1,0:T(8,128)})) %all-reduce.39.cloned.1.call-update) | async-done | bytes 2359312 | tf_op jit(solution)/shard_map/psum | solution.py:85
  1436.7 85.7 %all-reduce.53 = (bf16[128,1536]{1,0:T(8,128)(2,1)S(1)}, bf16[128,1536]{1,0:T(8,128)(2,1)S(1)}, bf16[128,1536]{1,0:T(8,128)(2,1)}) all-reduce(f32[128,1536]{1,0:T(8,128)S(1)} %slice-done.26, f32[128,1536]{1,0:T(8,128)S(1)} %slice-done.27, f32[128,1536]{1,0:T(8,128)} %split.37), channel_id=1, replica_groups=mesh['dp'=8,'tensor'=4] {'tensor'}, use_global_device_ids=true, to_apply=%region_82.83 | all-reduce | flops 589824 | bytes 3538944 | tf_op jit(solution)/shard_map/psum | solution.py:85
  1536.7 95.2 %all-reduce.54 = (bf16[128,1536]{1,0:T(8,128)(2,1)}, bf16[128,1536]{1,0:T(8,128)(2,1)}, bf16[128,1536]{1,0:T(8,128)(2,1)}, bf16[64,1536]{1,0:T(8,128)(2,1)}) all-reduce(f32[128,1536]{1,0:T(8,128)S(1)} %fusion.340, f32[128,1536]{1,0:T(8,128)S(1)} %fusion.333, ...), channel_id=1, replica_groups=mesh['dp'=8,'tensor'=4] {'tensor'}, use_global_device_ids=true, to_apply=%region_83.84 | all-reduce | flops 688128 | bytes 4128768 | tf_op jit(solution)/shard_map/psum | solution.py:85
  1857.1 41.7 %reduce-scatter.32.cloned.1.call-done = bf16[384,192]{0,1:T(8,128)(2,1)} async-done(((bf16[384,1536]{0,1:T(8,128)(2,1)}), bf16[384,192]{0,1:T(8,128)(2,1)}) %reduce-scatter.32.cloned.1.call-update) | async-done | bytes 147472 | tf_op jit(solution)/shard_map/reduce_scatter | solution.py:387
  1900.5 47.8 %reduce-scatter.34.cloned.1.call-done = bf16[192,1024]{1,0:T(8,128)(2,1)} async-done(((bf16[1536,1024]{1,0:T(8,128)(2,1)}), bf16[192,1024]{1,0:T(8,128)(2,1)}) %reduce-scatter.34.cloned.1.call-update) | async-done | bytes 393232 | tf_op jit(solution)/shard_map/reduce_scatter | solution.py:396
  1950.3 47.5 %reduce-scatter.36.cloned.1.call-done = bf16[192,1024]{1,0:T(8,128)(2,1)} async-done(((bf16[1536,1024]{1,0:T(8,128)(2,1)}), bf16[192,1024]{1,0:T(8,128)(2,1)}) %reduce-scatter.36.cloned.1.call-update) | async-done | bytes 393232 | tf_op jit(solution)/shard_map/reduce_scatter | solution.py:399
  1999.8 47.5 %reduce-scatter.38.cloned.1.call-done = bf16[1024,192]{0,1:T(8,128)(2,1)} async-done(((bf16[1024,1536]{0,1:T(8,128)(2,1)}), bf16[1024,192]{0,1:T(8,128)(2,1)}) %reduce-scatter.38.cloned.1.call-update) | async-done | bytes 393232 | tf_op jit(solution)/shard_map/reduce_scatter | solution.py:402
  2049.3 34.9 %reduce-scatter.40.cloned.1.call-done = bf16[192,64]{1,0:T(8,128)(2,1)} async-done(((bf16[1536,64]{1,0:T(8,128)(2,1)}), bf16[192,64]{1,0:T(8,128)(2,1)}) %reduce-scatter.40.cloned.1.call-update) | async-done | bytes 24592
  2085.7 39.0 %reduce-scatter.16.cloned.1.call-done = bf16[384,192]{0,1:T(8,128)(2,1)} async-done(((bf16[384,1536]{0,1:T(8,128)(2,1)}), bf16[384,192]{0,1:T(8,128)(2,1)}) %reduce-scatter.16.cloned.1.call-update) | async-done | bytes 147472 | tf_op jit(solution)/shard_map/reduce_scatter | solution.py:360
  2126.3 38.7 %reduce-scatter.22.cloned.1.call-done = bf16[192,384]{1,0:T(8,128)(2,1)} async-done(((bf16[1536,384]{1,0:T(8,128)(2,1)}), bf16[192,384]{1,0:T(8,128)(2,1)}) %reduce-scatter.22.cloned.1.call-update) | async-done | bytes 147472 | tf_op jit(solution)/shard_map/reduce_scatter | solution.py:369
  2166.7 38.1 %reduce-scatter.24.cloned.1.call-done = bf16[192,384]{1,0:T(8,128)(2,1)} async-done(((bf16[1536,384]{1,0:T(8,128)(2,1)}), bf16[192,384]{1,0:T(8,128)(2,1)}) %reduce-scatter.24.cloned.1.call-update) | async-done | bytes 147472 | tf_op jit(solution)/shard_map/reduce_scatter | solution.py:372
  2206.4 38.3 %reduce-scatter.26.cloned.1.call-done = bf16[192,384]{1,0:T(8,128)(2,1)} async-done(((bf16[1536,384]{1,0:T(8,128)(2,1)}), bf16[192,384]{1,0:T(8,128)(2,1)}) %reduce-scatter.26.cloned.1.call-update) | async-done | bytes 147472 | tf_op jit(solution)/shard_map/reduce_scatter | solution.py:375
  2246.3 38.3 %reduce-scatter.28.cloned.1.call-done = bf16[384,192]{0,1:T(8,128)(2,1)} async-done(((bf16[384,1536]{0,1:T(8,128)(2,1)}), bf16[384,192]{0,1:T(8,128)(2,1)}) %reduce-scatter.28.cloned.1.call-update) | async-done | bytes 147472 | tf_op jit(solution)/shard_map/reduce_scatter | solution.py:378
  2343.9 55.1 %reduce-scatter.20.cloned.1.call-done = bf16[1536,192]{0,1:T(8,128)(2,1)} async-done(((bf16[1536,1536]{0,1:T(8,128)(2,1)}), bf16[1536,192]{0,1:T(8,128)(2,1)}) %reduce-scatter.20.cloned.1.call-update) | async-done | bytes 589840 | tf_op jit(solution)/shard_map/reduce_scatter | solution.py:366
  (1400 shorter events, 787.2 us)
Async XLA Ops:
  10.0 282.1 %all-gather.20.cloned.1.call-start = ((), (), s32[]{:S(2)}) async-start(), calls=%async_computation.20 | async-start | bytes 1327104 | tf_op jit(solution)/shard_map/all_gather | solution.py:310
  10.6 286.1 %all-gather.24.cloned.1.call-start = ((), (), s32[]{:S(2)}) async-start(), calls=%async_computation.22 | async-start | bytes 1327104 | tf_op jit(solution)/shard_map/all_gather | solution.py:309
  24.5 303.1 %all-gather.26.cloned.1.call-start = ((), (), s32[]{:S(2)}) async-start(), calls=%async_computation.23 | async-start | bytes 1327104 | tf_op jit(solution)/shard_map/all_gather | solution.py:311
  25.2 409.8 %all-reduce.47.cloned.1.call-start = ((), (), s32[]{:S(2)}) async-start(), calls=%async_computation.47 | async-start | bytes 4718592 | tf_op jit(solution)/shard_map/psum | solution.py:85
  334.9 227.5 %all-gather.30.cloned.1.call-start = ((), (), s32[]{:S(2)}) async-start(), calls=%async_computation.25 | async-start | bytes 1327104 | tf_op jit(solution)/shard_map/all_gather | solution.py:314
  335.5 414.9 %all-reduce.45.cloned.1.call-start = ((), (), s32[]{:S(2)}) async-start(), calls=%async_computation.46 | async-start | bytes 9437184 | tf_op jit(solution)/shard_map/psum | solution.py:85
  580.9 226.9 %all-gather.36.cloned.1.call-start = ((), (), s32[]{:S(2)}) async-start(), calls=%async_computation.28 | async-start | bytes 3538944 | tf_op jit(solution)/shard_map/all_gather | solution.py:319
  581.5 299.1 %all-reduce.43.cloned.1.call-start = ((), (), s32[]{:S(2)}) async-start(), calls=%async_computation.45 | async-start | bytes 4718592 | tf_op jit(solution)/shard_map/psum | solution.py:85
  785.5 276.7 %all-reduce.41.cloned.1.call-start = ((), (), s32[]{:S(2)}) async-start(), calls=%async_computation.44 | async-start | bytes 4718592 | tf_op jit(solution)/shard_map/psum | solution.py:85
  967.4 432.7 %all-reduce.39.cloned.1.call-start = ((), (), s32[]{:S(2)}) async-start(), calls=%async_computation.43 | async-start | bytes 4718592 | tf_op jit(solution)/shard_map/psum | solution.py:85
  1306.3 511.1 %all-reduce.37.cloned.1.call-start = ((), (), s32[]{:S(2)}) async-start(), calls=%async_computation.42 | async-start | bytes 9437184 | tf_op jit(solution)/shard_map/psum | solution.py:85
  1643.7 255.1 %reduce-scatter.32.cloned.1.call-start = ((), (), s32[]{:S(2)}) async-start(), calls=%async_computation.37 | async-start | bytes 1327104 | tf_op jit(solution)/shard_map/reduce_scatter | solution.py:387
  1648.9 299.4 %reduce-scatter.34.cloned.1.call-start = ((), (), s32[]{:S(2)}) async-start(), calls=%async_computation.38 | async-start | bytes 3538944 | tf_op jit(solution)/shard_map/reduce_scatter | solution.py:396
  1653.8 344.0 %reduce-scatter.36.cloned.1.call-start = ((), (), s32[]{:S(2)}) async-start(), calls=%async_computation.39 | async-start | bytes 3538944 | tf_op jit(solution)/shard_map/reduce_scatter | solution.py:399
  1659.6 387.8 %reduce-scatter.38.cloned.1.call-start = ((), (), s32[]{:S(2)}) async-start(), calls=%async_computation.40 | async-start | bytes 3538944 | tf_op jit(solution)/shard_map/reduce_scatter | solution.py:402
  1665.5 418.7 %reduce-scatter.40.cloned.1.call-start = ((), (), s32[]{:S(2)}) async-start(), calls=%async_computation.41 | async-start | bytes 442368
  1669.9 454.8 %reduce-scatter.16.cloned.1.call-start = ((), (), s32[]{:S(2)}) async-start(), calls=%async_computation.29 | async-start | bytes 1327104 | tf_op jit(solution)/shard_map/reduce_scatter | solution.py:360
  1673.2 491.8 %reduce-scatter.22.cloned.1.call-start = ((), (), s32[]{:S(2)}) async-start(), calls=%async_computation.32 | async-start | bytes 1327104 | tf_op jit(solution)/shard_map/reduce_scatter | solution.py:369
  1676.5 528.3 %reduce-scatter.24.cloned.1.call-start = ((), (), s32[]{:S(2)}) async-start(), calls=%async_computation.33 | async-start | bytes 1327104 | tf_op jit(solution)/shard_map/reduce_scatter | solution.py:372
  1685.8 558.9 %reduce-scatter.26.cloned.1.call-start = ((), (), s32[]{:S(2)}) async-start(), calls=%async_computation.34 | async-start | bytes 1327104 | tf_op jit(solution)/shard_map/reduce_scatter | solution.py:375
  1700.7 583.9 %reduce-scatter.28.cloned.1.call-start = ((), (), s32[]{:S(2)}) async-start(), calls=%async_computation.35 | async-start | bytes 1327104 | tf_op jit(solution)/shard_map/reduce_scatter | solution.py:378
  1715.8 625.9 %reduce-scatter.18.cloned.1.call-start = ((), (), s32[]{:S(2)}) async-start(), calls=%async_computation.30 | async-start | bytes 5308416 | tf_op jit(solution)/shard_map/reduce_scatter | solution.py:363
  1736.7 662.3 %reduce-scatter.20.cloned.1.call-start = ((), (), s32[]{:S(2)}) async-start(), calls=%async_computation.31 | async-start | bytes 5308416 | tf_op jit(solution)/shard_map/reduce_scatter | solution.py:366
  1846.8 469.3 %all-to-all-start.3 = ((bf16[8,48,1536]{2,1,0:T(8,128)(2,1)}), bf16[8,48,1536]{2,1,0:T(8,128)(2,1)S(1)}, u32[]{:S(2)}, u32[]{:S(2)}) async-start(bf16[8,48,1536]{2,1,0:T(8,128)(2,1)} %bitcast.61), calls=%async_computation.3 | async-start | bytes 2359296 | tf_op jit(solution)/shard_map/all_to_all | solution.py:410
  (485 other events, 11153.8 us)
Sparse Core Ops, SparseCore 0:
  9.9 32.1 all-gather.13
  70.9 40.4 all-gather.15
  113.1 38.7 all-gather.17
  334.3 100.7 all-reduce.46
  581.0 169.3 all-reduce.44
  785.9 94.6 all-reduce.42
  882.3 31.1 all-gather.33
  915.3 32.1 all-gather.31
  967.5 94.6 all-reduce.40
  1306.5 93.6 all-reduce.38
  1640.0 171.9 all-reduce.36
  1815.2 40.2 reduce-scatter.29
  1858.6 40.2 reduce-scatter.31
  1902.2 46.0 reduce-scatter.33
  1951.7 46.0 reduce-scatter.35
  2001.2 46.0 reduce-scatter.37
  2050.2 33.9 reduce-scatter.39
  2088.0 36.6 reduce-scatter.15
  2128.3 36.6 reduce-scatter.21
  2168.1 36.6 reduce-scatter.23
  2208.0 36.6 reduce-scatter.25
  2247.9 36.6 reduce-scatter.27
  2287.9 53.7 reduce-scatter.17
  2345.2 53.7 reduce-scatter.19
  (7 shorter events, 174.3 us)
where the time goes:
time: 2420 us; the launch traced here: 2410 us
  waiting for transfers between devices  1110 us (46%)
  blocking collectives  671 us (28%)
  matrix products  426 us (18%)
  local copies, waits for them, and re-layouts  79.8 us (3%)
  other arithmetic  78.3 us (3%)
    psum x6, blocking collectives, tensor_sum(): return lax.psum(operand, 'tensor')  513 us
    psum x6, waiting for transfers between devices, tensor_sum(): return lax.psum(operand, 'tensor')  500 us
    dot_general x117, matrix products, rounded_dot(): return jnp.dot(left_side, right_side, preferred_element_type=jnp.float32)  247 us
    dot_general x63, matrix products, matmul(): jnp.dot(left_side, right_side, precision=HIGH, preferred_element_type=jnp...  149 us
    psum x1, blocking collectives, micro_batch(): key_sum, value_mem = lax.psum((key_part, value_part), 'tensor')  88.5 us
    reduce_scatter x1, waiting for transfers between devices, per_device(): lax.psum_scatter(g_mem_out.astype(jnp.bfloat16), 'dp', scatter_dimension=...  55.1 us
  transfers between devices with their start and end apart: 35, of which 23 were waited for; matrix products, arithmetic and copies ran while one was open for 16% of the time, Pallas kernels for 0%

commit v1 on v0

v1 whole, which is shorter than its diff:
```python
import functools

import jax
import jax.numpy as jnp
from jax import lax
from jax.experimental import pallas as pl
from jax.experimental.pallas import tpu as pltpu
from jax.sharding import PartitionSpec as P

HD = 96
EPSILON = 1e-06
RATE_SCALE = 8e-05
NEG_LARGE = -1e30
BF = jnp.bfloat16
F32 = jnp.float32
MESH = pl.DeviceIdType.MESH
TILE = 128


def chain_sum_kernel(pieces, layout, x_ref, *refs):
    given = sum(len(widths) for _, parts in layout for widths in parts)
    fills, refs = refs[:given], refs[given:]
    o_ref, refs = refs[0], refs[1:]
    if layout:
        g_ref, refs = refs[0], refs[1:]
    from_outer, from_inner, part, sent_a, got_up, sent_b, got_across, got_total = refs[:8]
    me = lax.axis_index("tensor")
    step = x_ref.shape[0] // pieces
    low = me < 2
    outer = jnp.logical_or(me == 0, me == 3)
    inner = jnp.logical_not(outer)
    outer_peer = jnp.where(low, 0, 3)
    inner_peer = jnp.where(low, 2, 1)
    toward = jnp.where(low, 1, 2)
    barrier = pltpu.get_barrier_semaphore()

    def tell(peer):
        pl.semaphore_signal(barrier, inc=1, device_id={"tensor": peer}, device_id_type=MESH)

    def at(piece):
        return pl.ds(pl.multiple_of(piece * step, step), step)

    def send(src, dst, send_sem, recv_sem, peer):
        return pltpu.make_async_remote_copy(
            src_ref=src,
            dst_ref=dst,
            send_sem=send_sem,
            recv_sem=recv_sem,
            device_id={"tensor": peer},
            device_id_type=MESH,
        )

    def up(p):
        return send(x_ref.at[at(p)], from_outer.at[at(p)], sent_a.at[p], got_up.at[p], toward)

    def across(p):
        return send(part.at[at(p)], from_inner.at[at(p)], sent_b.at[p], got_across.at[p], inner_peer)

    def down(p):
        return send(o_ref.at[at(p)], o_ref.at[at(p)], sent_a.at[p], got_total.at[p], outer_peer)

    def put(tile):
        stage, put_sem = refs[8], refs[9]
        rows = pl.ds(pl.multiple_of(tile * TILE, TILE), TILE)
        slot = lax.rem(tile, 2)
        return pltpu.make_async_copy(stage.at[slot], g_ref.at[rows], put_sem.at[slot])

    def fill(tile):
        stage = refs[8]
        columns = pl.ds(pl.multiple_of(tile * TILE, TILE), TILE)
        slot = lax.rem(tile, 2)

        @pl.when(tile >= 2)
        def _():
            put(tile - 2).wait()

        first, offset = 0, 0
        for width, parts in layout:
            for start in range(0, width, 512):
                span = min(512, width - start)
                total, index = None, first
                for part_sizes in parts:
                    if len(part_sizes) == 1:
                        term = fills[index][columns, start : start + span].astype(F32)
                    else:
                        term = lax.dot_general(
                            fills[index][:, columns],
                            fills[index + 1][:, start : start + span],
                            (((0,), (0,)), ((), ())),
                            preferred_element_type=F32,
                        )
                    total = term if total is None else total + term
                    index += len(part_sizes)
                stage[slot, :, offset + start : offset + start + span] = total.astype(BF)
            first, offset = index, offset + width
        put(tile).start()

    @pl.when(outer)
    def _():
        tell(toward)
        pl.semaphore_wait(barrier, 1)

        @pl.loop(0, pieces)
        def _(p):
            up(p).start()

    @pl.when(inner)
    def _():
        tell(outer_peer)
        tell(inner_peer)
        pl.semaphore_wait(barrier, 2)

    def first_add(p):
        up(p).wait_recv()
        part[at(p), :] = (
            x_ref[at(p), :].astype(F32) + from_outer[at(p), :].astype(F32)
        ).astype(part.dtype)
        across(p).start()

    def second_add(p):
        across(p).wait_recv()
        o_ref[at(p), :] = (
            part[at(p), :].astype(F32) + from_inner[at(p), :].astype(F32)
        ).astype(o_ref.dtype)
        down(p).start()

    tiles = g_ref.shape[0] // TILE if layout else 0

    @pl.loop(0, max(pieces + 1, tiles))
    def _(p):
        @pl.when(jnp.logical_and(inner, p < pieces))
        def _():
            first_add(p)

        @pl.when(jnp.logical_and(inner, jnp.logical_and(p >= 1, p <= pieces)))
        def _():
            second_add(p - 1)

        if layout:

            @pl.when(p < tiles)
            def _():
                fill(p)

    if layout:
        put(tiles - 2).wait()
        put(tiles - 1).wait()

    @pl.when(outer)
    def _():
        @pl.loop(0, pieces)
        def _(p):
            down(p).wait_recv()
            up(p).wait_send()

    @pl.when(inner)
    def _():
        @pl.loop(0, pieces)
        def _(p):
            across(p).wait_send()
            down(p).wait_send()


def chain_sum(x, call_id=1, products=()):
    rows, cols = x.shape
    pieces = rows // 32
    dma = pltpu.SemaphoreType.DMA
    vmem = pl.BlockSpec(memory_space=pltpu.VMEM)
    layout = tuple(
        (pairs[0][1].shape[1], tuple((0,) * len(pair) for pair in pairs)) for pairs in products
    )
    fills = [array for pairs in products for pair in pairs for array in pair]
    out_shape = [jax.ShapeDtypeStruct((rows, cols), BF)]
    out_specs = [vmem]
    scratch = [pltpu.VMEM((rows, cols), BF)] * 3 + [dma((pieces,))] * 5
    if products:
        width, high = sum(w for w, _ in layout), products[0][0][0].shape[1]
        out_shape.append(jax.ShapeDtypeStruct((high, width), BF))
        out_specs.append(pl.BlockSpec(memory_space=pl.ANY))
        scratch += [pltpu.VMEM((2, TILE, width), BF), dma((2,))]
    out = pl.pallas_call(
        functools.partial(chain_sum_kernel, pieces, layout),
        out_shape=out_shape,
        in_specs=[vmem] * (1 + len(fills)),
        out_specs=out_specs,
        scratch_shapes=scratch,
        compiler_params=pltpu.CompilerParams(collective_id=call_id, has_side_effects=True),
        cost_estimate=pl.CostEstimate(flops=0, bytes_accessed=10**8, transcendentals=0),
        name="chain_sum",
    )(x.astype(BF), *fills)
    return out if products else out[0]


def dot(left, right):
    return lax.dot_general(left, right, (((1,), (0,)), ((), ())), preferred_element_type=F32)


def dot_t(left, right):
    return lax.dot_general(left, right, (((1,), (1,)), ((), ())), preferred_element_type=F32)


def t_dot(left, right):
    return lax.dot_general(left, right, (((0,), (0,)), ((), ())), preferred_element_type=F32)


def batch_dot(spec, left, right):
    return jnp.einsum(spec, left, right, preferred_element_type=F32)


def together(*values):
    return lax.optimization_barrier(values)


def rms(v):
    return lax.rsqrt(jnp.mean(v * v, axis=-1, keepdims=True) + EPSILON)


def rms_back(v, r, gain, grad):
    scaled = grad * gain
    inner = jnp.sum(scaled * v, axis=-1, keepdims=True)
    return r * scaled - v * (r * r * r) * (inner / v.shape[-1])


def silu_parts(z):
    s = jax.nn.sigmoid(z)
    return s, z * s, s * (1.0 + z * (1.0 - s))


def per_device(
    tokens,
    cotangent,
    dest,
    source,
    lengths,
    persist,
    gain_attn,
    w_query_mem,
    mem_in,
    mem_out,
    w_query,
    w_key,
    w_value,
    w_output,
    gain_mem,
    w_key_mem,
    w_value_mem,
    w_rate,
    gain_ffn,
    w_gate,
    w_up,
    w_down,
):
    count, width = tokens.shape
    shard = gain_attn.shape[0]
    ranks = width // shard
    batches, _ = lengths.shape
    rows = count // batches
    hidden = mem_in.shape[1]
    inner = w_query.shape[1]
    heads = inner // HD
    slots = persist.shape[0]
    me = lax.axis_index("tensor")

    def gather(*parts):
        packed = jnp.concatenate(parts, axis=1)
        whole = lax.all_gather(packed, "dp", axis=0, tiled=True)
        out, low = [], 0
        for part in parts:
            out.append(whole[:, low : low + part.shape[1]])
            low += part.shape[1]
        return out

    vectors = jnp.stack([gain_attn, gain_mem, gain_ffn, w_rate], axis=1)
    pad = jnp.zeros((shard, 128 - slots - 4), BF)
    small, wqm_t = gather(jnp.concatenate([persist.T, vectors, pad], axis=1), w_query_mem.T)
    w_in, w_out_t = gather(mem_in, mem_out.T)
    persistent = small[:, :slots].T
    gains = small[:, slots : slots + 4].astype(F32).T
    g_attn, g_mem, g_ffn, rate_w = (gains[i][None, :] for i in range(4))

    ends = lax.axis_size("tensor")
    columns = jnp.concatenate([w_key_mem, w_value_mem], axis=1)
    before, after = [columns], [columns]
    for _ in range(ends - 1):
        before.append(lax.ppermute(before[-1], "tensor", [(i, i + 1) for i in range(ends - 1)]))
        after.append(lax.ppermute(after[-1], "tensor", [(i + 1, i) for i in range(ends - 1)]))
    line = jnp.concatenate(before[:0:-1] + after, axis=0)
    high = columns.shape[0]
    tall = lax.dynamic_slice_in_dim(line, (ends - 1 - me) * high, ends * high, 0)

    place = jnp.arange(count, dtype=jnp.int32)
    home = dest // count
    earlier = (home[None, :] == home[:, None]) & (place[None, :] < place[:, None])
    sent_at = home * (count // ranks) + jnp.sum(earlier.astype(jnp.int32), axis=1)
    came_at = jnp.sum((source[None, :] < source[:, None]).astype(jnp.int32), axis=1)
    send_m = (sent_at[None, :] == place[:, None]).astype(BF)
    deal_m = (came_at[:, None] == place[None, :]).astype(BF)

    def exchange(v):
        return lax.all_to_all(
            dot(send_m, v).astype(BF), "dp", split_axis=0, concat_axis=0, tiled=True
        )

    def give_back(v):
        back = lax.all_to_all(
            t_dot(deal_m, v.astype(BF)).astype(BF), "dp", split_axis=0, concat_axis=0, tiled=True
        )
        return t_dot(send_m, back).astype(BF)

    dealt = dot(deal_m, exchange(tokens)).astype(BF)
    dealt, later, late_query, late_key, late_value, late_output = together(
        dealt, cotangent, w_query, w_key, w_value, w_output
    )
    wq, wk, wv, wo_t = gather(late_query, late_key, late_value, late_output.T)
    cotangent_arrived = exchange(later)
    x = dealt.astype(F32)

    position = jnp.arange(rows, dtype=jnp.int32)
    bounds = jnp.cumsum(lengths, axis=1)
    segment = jnp.sum((position[None, :, None] >= bounds[:, None, :]).astype(jnp.int32), axis=2)
    causal = (segment[:, :, None] == segment[:, None, :]) & (
        position[None, None, :] <= position[None, :, None]
    )

    def split(v):
        return v.reshape(batches, rows, v.shape[-1])

    def join(v):
        return v.reshape(count, v.shape[-1])

    def own(v):
        return lax.dynamic_slice_in_dim(v, me * inner, inner, 1)

    def in_own(v):
        return lax.dynamic_update_slice_in_dim(
            jnp.zeros((v.shape[0], width), v.dtype), v, me * inner, 1
        )

    r1 = rms(x)
    n1 = (x * r1 * g_attn).astype(BF)
    n1_own = own(n1)
    query_mem = chain_sum(dot_t(n1_own, wqm_t))
    query_mem, cotangent_arrived, tall = together(query_mem, cotangent_arrived, tall)
    wkm_t, wvm_t = gather(tall[:, :shard].T, tall[:, shard:].T)
    d_out_low = dot(deal_m, cotangent_arrived).astype(BF)
    read_s, read_act, read_slope = silu_parts(dot(query_mem, w_in))
    read_low = read_act.astype(BF)
    memory = chain_sum(dot_t(read_low, w_out_t))

    query = dot(n1, wq).astype(BF)
    key_p, value_p = dot(persistent, wk).astype(BF), dot(persistent, wv).astype(BF)
    key_m, value_m = dot(memory, wk).astype(BF), dot(memory, wv).astype(BF)
    key_x, value_x = dot(n1, wk).astype(BF), dot(n1, wv).astype(BF)

    def context(p, m, t):
        wide = jnp.broadcast_to(p[None], (batches,) + p.shape)
        all_rows = jnp.concatenate([wide, split(m), split(t)], axis=1)
        return all_rows.reshape(batches, -1, heads, HD)

    keys, values = context(key_p, key_m, key_x), context(value_p, value_m, value_x)
    allowed = jnp.concatenate(
        [jnp.ones((batches, rows, slots), dtype=bool), causal, causal], axis=2
    )[:, None]
    query4 = query.reshape(batches, rows, heads, HD)
    scores = batch_dot("bqhd,bkhd->bhqk", query4, keys) * HD ** (-0.5)
    weights = jax.nn.softmax(jnp.where(allowed, scores, NEG_LARGE), axis=-1)
    weights_low = weights.astype(BF)
    mixed = batch_dot("bhqk,bkhd->bqhd", weights_low, values).astype(BF).reshape(count, inner)
    mixed, late_gate, late_up, late_down = together(mixed, w_gate, w_up, w_down)
    wg, wu, wd_t = gather(late_gate, late_up, late_down.T)
    after_attn = x + chain_sum(dot_t(mixed, wo_t)).astype(F32)

    r2 = rms(after_attn)
    n2 = after_attn * r2 * g_mem
    rate_s = jax.nn.sigmoid(jnp.sum(n2 * rate_w, axis=1, keepdims=True))
    rate = RATE_SCALE * rate_s
    n2_low = n2.astype(BF)
    n2_own = own(n2_low)
    key_mem = dot_t(n2_low, wkm_t).astype(BF)
    value_part = dot_t(n2_own, own(wvm_t))
    key_hidden = dot(key_mem, w_in)
    key_s, key_silu, key_slope = silu_parts(key_hidden)
    key_act = key_silu.astype(BF)
    miss = chain_sum(dot_t(key_act, w_out_t) - value_part).astype(F32)
    error = (rate * miss).astype(BF)
    back_pre = dot(error, w_out_t)
    back_hidden = (back_pre * key_slope).astype(BF)
    gram = jnp.where(causal, batch_dot("bik,bjk->bij", split(key_mem), split(key_mem)), 0.0).astype(BF)
    new_hidden = key_hidden - join(batch_dot("bij,bjk->bik", gram, split(back_hidden)))
    _, new_silu, new_slope = silu_parts(new_hidden)
    new_act = new_silu.astype(BF)
    pair = jnp.where(causal, batch_dot("bik,bjk->bij", split(new_act), split(key_act)), 0.0).astype(BF)
    update = dot_t(new_act, w_out_t) - join(batch_dot("bij,bjk->bik", pair, split(error)))
    after_mem = after_attn + chain_sum(update).astype(F32)

    r3 = rms(after_mem)
    n3 = (after_mem * r3 * g_ffn).astype(BF)
    gate, up = dot(n3, wg), dot(n3, wu)
    _, gate_silu, gate_slope = silu_parts(gate)
    ffn_act = (gate_silu * up).astype(BF)
    ffn_own = lax.psum_scatter(
        dot_t(ffn_act, wd_t).astype(BF), "tensor", scatter_dimension=1, tiled=True
    )

    d_ffn = dot(d_out_low, wd_t)
    d_gate = (d_ffn * up * gate_slope).astype(BF)
    d_up = (d_ffn * gate_silu).astype(BF)
    d_n3, gw_ffn = chain_sum(
        dot_t(d_gate, wg) + dot_t(d_up, wu),
        2,
        [[(d_out_low, ffn_act)], [(n3, d_gate)], [(n3, d_up)]],
    )
    d_n3 = d_n3.astype(F32)
    gg_ffn = jnp.sum(d_n3 * after_mem * r3, axis=0)
    d_after_mem = d_out_low.astype(F32) + rms_back(after_mem, r3, g_ffn, d_n3)
    d_update = d_after_mem.astype(BF)

    d_pair = jnp.where(
        causal, -batch_dot("bik,bjk->bij", split(d_update), split(error)), 0.0
    ).astype(BF)
    d_new_act = dot(d_update, w_out_t) + join(batch_dot("bij,bjk->bik", d_pair, split(key_act)))
    d_key_act = join(batch_dot("bij,bik->bjk", d_pair, split(new_act)))
    d_new_hidden = (d_new_act * new_slope).astype(BF)
    d_gram = jnp.where(
        causal, -batch_dot("bik,bjk->bij", split(d_new_hidden), split(back_hidden)), 0.0
    ).astype(BF)
    d_back = (-join(batch_dot("bij,bik->bjk", gram, split(d_new_hidden)))).astype(BF).astype(F32)
    d_back_pre = (d_back * key_slope).astype(BF)
    slope_grad = key_s * (1.0 - key_s) * (2.0 + key_hidden * (1.0 - 2.0 * key_s))
    d_hidden_part = d_new_hidden.astype(F32) + d_back * back_pre * slope_grad
    d_error_part = dot_t(d_back_pre, w_out_t) - join(
        batch_dot("bij,bik->bjk", pair, split(d_update))
    )
    share_ffn = lax.psum_scatter(gw_ffn, "dp", scatter_dimension=0, tiled=True)
    d_error = chain_sum(d_error_part).astype(F32)
    d_rate = jnp.sum(d_error * miss, axis=1, keepdims=True)
    d_miss = (rate * d_error).astype(BF)
    d_key_act = d_key_act + dot(d_miss, w_out_t)
    d_key_hidden = (d_hidden_part + d_key_act * key_slope).astype(BF)
    d_key_part = dot_t(d_key_hidden, w_in) + join(
        batch_dot("bij,bjk->bik", d_gram, split(key_mem))
        + batch_dot("bij,bik->bjk", d_gram, split(key_mem))
    )
    d_key_part, ffn_own = together(d_key_part.astype(BF), ffn_own)
    result_own = give_back(own(after_mem) + ffn_own.astype(F32))
    d_key, gw_out_early = chain_sum(
        d_key_part, 6, [[(d_update, new_act), (error, d_back_pre)]]
    )
    d_n2 = dot(d_key, wkm_t) - dot(d_miss, wvm_t)
    d_logit = d_rate * rate * (1.0 - rate_s)
    gg_rate = jnp.sum(n2 * d_logit, axis=0)
    d_n2 = d_n2 + d_logit * rate_w
    gg_mem = jnp.sum(d_n2 * after_attn * r2, axis=0)
    d_after_attn = d_after_mem + rms_back(after_attn, r2, g_mem, d_n2)
    d_attn = d_after_attn.astype(BF)

    d_mixed = dot(d_attn, wo_t).astype(BF)
    d_mixed4 = d_mixed.reshape(batches, rows, heads, HD)
    d_weights = batch_dot("bqhd,bkhd->bhqk", d_mixed4, values)
    d_values = batch_dot("bhqk,bqhd->bkhd", weights_low, d_mixed4)
    d_scores = (
        weights * (d_weights - jnp.sum(weights * d_weights, axis=-1, keepdims=True))
    ).astype(BF)
    d_query = batch_dot("bhqk,bkhd->bqhd", d_scores, keys) * HD ** (-0.5)
    d_keys = batch_dot("bhqk,bqhd->bkhd", d_scores, query4) * HD ** (-0.5)
    d_query = d_query.astype(BF).reshape(count, inner)

    def apart(v):
        v = v.reshape(batches, -1, inner)
        return (
            jnp.sum(v[:, :slots], axis=0).astype(BF),
            join(v[:, slots : slots + rows]).astype(BF),
            join(v[:, slots + rows :]).astype(BF),
        )

    dk_p, dk_m, dk_x = apart(d_keys)
    dv_p, dv_m, dv_x = apart(d_values)
    d_memory_part, share_ffn, result_own = together(
        (dot_t(dk_m, wk) + dot_t(dv_m, wv)).astype(BF), share_ffn, result_own
    )
    output = lax.all_gather(result_own, "tensor", axis=1, tiled=True)
    d_memory, gw_attn = chain_sum(
        d_memory_part,
        3,
        [
            [(d_key, n2_own)],
            [(d_miss, n2_own)],
            [(d_attn, mixed)],
            [(n1, d_query)],
            [(persistent, dk_p), (memory, dk_m), (n1, dk_x)],
            [(persistent, dv_p), (memory, dv_m), (n1, dv_x)],
        ],
    )
    d_n1_part = dot_t(d_query, wq) + dot_t(dk_x, wk) + dot_t(dv_x, wv)
    d_persist_part = dot_t(dk_p, wk) + dot_t(dv_p, wv)

    share_attn = lax.psum_scatter(gw_attn, "dp", scatter_dimension=0, tiled=True)
    d_read = (dot(d_memory, w_out_t) * read_slope).astype(BF)
    d_query_mem, gw_mem = chain_sum(
        dot_t(d_read, w_in),
        4,
        [
            [(key_mem, d_key_hidden), (query_mem, d_read)],
            [(d_miss, key_act), (d_memory, read_low), (gw_out_early,)],
        ],
    )
    share_mem = lax.psum_scatter(gw_mem, "dp", scatter_dimension=0, tiled=True)
    d_n1_part = d_n1_part + in_own(dot(d_query_mem, wqm_t))
    d_n1_part, share_attn, output = together(d_n1_part.astype(BF), share_attn, output)
    last, gw_query_mem = chain_sum(
        jnp.concatenate([d_n1_part, d_persist_part.astype(BF)], axis=0), 5, [[(d_query_mem, n1_own)]]
    )
    d_n1 = last[:count].astype(F32)
    g_persist = last[count:]
    gg_attn = jnp.sum(d_n1 * x * r1, axis=0)
    d_x = d_after_attn + rms_back(x, r1, g_attn, d_n1)

    def cut(share, *widths):
        out, low = [], 0
        for part in widths:
            out.append(share[:, low : low + part].astype(F32))
            low += part
        return out

    s_down, s_gate, s_up = cut(share_ffn, *[w_gate.shape[1]] * 3)
    s_key_mem, s_value_mem, s_output, s_query, s_key, s_value = cut(share_attn, *[inner] * 6)
    s_in, s_out = cut(share_mem, hidden, hidden)
    grad_vectors = jnp.stack([gg_attn, gg_mem, gg_ffn, gg_rate], axis=1)
    rest = jnp.concatenate(
        [
            gw_query_mem,
            g_persist.T,
            grad_vectors.astype(BF),
            jnp.zeros((width, 128 - slots - 4), BF),
        ],
        axis=1,
    ).reshape(ranks, -1, width)
    turned = t_dot(deal_m, d_x.astype(BF)).astype(BF).reshape(ranks, -1, width)
    came = lax.all_to_all(
        jnp.concatenate([turned, rest], axis=1), "dp", split_axis=0, concat_axis=0, tiled=True
    )
    seats = count // ranks
    grad_tokens = t_dot(send_m, came[:, :seats].reshape(count, width)).astype(BF)
    share_rest = jnp.sum(came[:, seats:].astype(F32), axis=0).reshape(shard, -1)
    s_query_mem, s_small = cut(share_rest, inner, 128)
    s_vectors = s_small[:, slots : slots + 4].T

    return (
        output,
        grad_tokens,
        s_small[:, :slots].T,
        s_vectors[0],
        s_query_mem.T,
        s_in,
        s_out.T,
        s_query,
        s_key,
        s_value,
        s_output.T,
        s_vectors[1],
        s_key_mem.T,
        -s_value_mem.T,
        s_vectors[3],
        s_vectors[2],
        s_gate,
        s_up,
        s_down.T,
    )


def solution(mesh):
    rows = P("dp", None)
    vector = P("dp")
    across = P("tensor", "dp")
    along = P("dp", "tensor")
    return jax.shard_map(
        per_device,
        mesh=mesh,
        in_specs=(
            rows,
            rows,
            vector,
            vector,
            rows,
            P(None, "dp"),
            vector,
            across,
            along,
            across,
            along,
            along,
            along,
            across,
            vector,
            across,
            across,
            vector,
            vector,
            along,
            along,
            across,
        ),
        out_specs=(
            rows,
            rows,
            P(None, "dp"),
            vector,
            across,
            along,
            across,
            along,
            along,
            along,
            across,
            vector,
            across,
            across,
            vector,
            vector,
            along,
            along,
            across,
        ),
        check_vma=False,
    )
```

time: 2420 us -> 889 us (0.37)
  waiting for transfers between devices: 1110 us -> 64.1 us
  blocking collectives: 671 us -> 0 us
  Pallas kernels: 0 us -> 461 us
  matrix products: 426 us -> 169 us
  other arithmetic: 78.3 us -> 47.9 us
    psum x7 -> x0, blocking collectives: 602 us -> none  [the longest x6 513 us: tensor_sum(): return lax.psum(operand, 'tensor')]
    psum x6 -> x0, waiting for transfers between devices: 500 us -> none  [tensor_sum(): return lax.psum(operand, 'tensor')]
    pallas_call x0 -> x11, Pallas kernels: none -> 461 us  [chain_sum(): pl.pallas_call(functools.partial(chain_sum_kernel, pieces, layout), out_s...]
    reduce_scatter x12 -> x3, waiting for transfers between devices: 459 us -> 0.02 us  [the longest x1 0.02 us: per_device(): lax.psum_scatter(gw_attn, 'dp', scatter_dimension=0, tiled=True)]
    dot_general x201 -> x65, matrix products: 422 us -> 166 us  [the longest x24 83.3 us: dot(): lax.dot_general(left, right, (((1,), (0,)), ((), ())), preferred_element_...]
    all_gather x12 -> x6, waiting for transfers between devices: 80.6 us -> 1.62 us  [the longest x5 1.6 us: gather(): whole = lax.all_gather(packed, 'dp', axis=0, tiled=True)]
    unnamed x2 -> x0, blocking collectives: 47.4 us -> none
    unnamed x32 -> x11, waiting for transfers between devices: 42.4 us -> 0.17 us
  transfers between devices with their start and end apart: 35 -> 20, of which waited for: 23 -> 8; matrix products, arithmetic and copies ran while one was open for 16% -> 28% of each run, Pallas kernels for 0% -> 52%
where the time goes in v1:
time: 889 us; the launch traced here: 881 us
  Pallas kernels  461 us (52%)
  matrix products  169 us (19%)
  local copies, waits for them, and re-layouts  85.1 us (10%)
  waiting for transfers between devices  64.1 us (7%)
  other arithmetic  47.9 us (5%)
  starting transfers between devices  37 us (4%)
  between operations  16.5 us (2%)
    pallas_call x11, Pallas kernels, chain_sum(): pl.pallas_call(functools.partial(chain_sum_kernel, pieces, layout), out_s...  461 us
    dot_general x24, matrix products, dot(): lax.dot_general(left, right, (((1,), (0,)), ((), ())), preferred_element_...  83.3 us
    dot_general x20, matrix products, dot_t(): lax.dot_general(left, right, (((1,), (1,)), ((), ())), preferred_element_...  56.5 us
    unnamed x264, local copies, waits for them, and re-layouts  33.2 us
    all_to_all x1, waiting for transfers between devices, per_device(): lax.all_to_all(jnp.concatenate([turned, rest], axis=1), 'dp', split_axis=...  30.2 us
    all_to_all x2, waiting for transfers between devices, exchange(): lax.all_to_all(dot(send_m, v).astype(BF), 'dp', split_axis=0, concat_axis...  18.6 us
  transfers between devices with their start and end apart: 20, of which 8 were waited for; matrix products, arithmetic and copies ran while one was open for 28% of the time, Pallas kernels for 52%

profile of v1, /device:TPU:0, one launch (start us, length us, event | category | flops | bytes accessed | tf_op | source)
XLA Modules:
  0.0 881.0 jit_solution(12163124492887324684)
XLA Ops:
  16.5 5.2 all-to-all-start
  22.0 18.6 %all-to-all-done = bf16[8,48,1536]{2,1,0:T(8,128)(2,1)S(1)} async-done(((bf16[8,48,1536]{2,1,0:T(8,128)(2,1)}), bf16[8,48,1536]{2,1,0:T(8,128)(2,1)S(1)}, u32[]{:S(2)}, u32[]{:S(2)}) %all-to-all-start) | async-done | bytes 1179680 | tf_op jit(solution)/shard_map/all_to_all | solution.py:300
  76.7 5.2 all-to-all-start.1
  89.4 41.4 %chain_sum.11.refs_2_ = bf16[384,1536]{1,0:T(8,128)(2,1)} custom-call(bf16[384,1536]{1,0:T(8,128)(2,1)} %convolution_convert_fusion.7.x_ref), custom_call_target="tpu_custom_call" | custom-call | bytes 100000000 | tf_op jit(solution)/shard_map/chain_sum/pallas_call | solution.py:181
  153.4 6.0 multiply_convert_fusion.4
  163.5 40.9 %chain_sum.12.refs_10_.refs_16_ = bf16[384,1536]{1,0:T(8,128)(2,1)} custom-call(bf16[384,1536]{1,0:T(8,128)(2,1)} %convolution_convert_fusion.x_ref), custom_call_target="tpu_custom_call" | custom-call | bytes 100000000 | tf_op jit(solution)/shard_map/chain_sum/pallas_call | solution.py:181
  228.8 37.6 %chain_sum.13 = bf16[384,1536]{1,0:T(8,128)(2,1)} custom-call(bf16[384,1536]{1,0:T(8,128)(2,1)} %convolution_convert_fusion.4.x_ref), custom_call_target="tpu_custom_call" | custom-call | bytes 100000000 | tf_op jit(solution)/shard_map/chain_sum/pallas_call | solution.py:181
  287.0 37.6 %chain_sum.14 = bf16[384,1536]{1,0:T(8,128)(2,1)} custom-call(bf16[384,1536]{1,0:T(8,128)(2,1)} %fusion.32.x_ref), custom_call_target="tpu_custom_call" | custom-call | bytes 100000000 | tf_op jit(solution)/shard_map/chain_sum/pallas_call | solution.py:181
  326.6 6.0 multiply_convert_fusion.2
  339.5 36.9 %chain_sum.15 = bf16[384,1536]{1,0:T(8,128)(2,1)} custom-call(bf16[384,1536]{1,0:T(8,128)(2,1)} %fusion.38.x_ref), custom_call_target="tpu_custom_call" | custom-call | bytes 100000000 | tf_op jit(solution)/shard_map/chain_sum/pallas_call | solution.py:181
  406.2 52.2 %chain_sum.16 = (bf16[384,1536]{1,0:T(8,128)(2,1)}, bf16[1536,3072]{1,0:T(8,128)(2,1)}) custom-call(bf16[384,1536]{1,0:T(8,128)(2,1)} %fusion.28.x_ref, bf16[384,1536]{1,0:T(8,128)(2,1)} %convolution_convert_fusion.5.refs_0_, bf16[384,1024]{1,0:T(8,128)(2,1)} %copy-done.58, bf16[384,1536]{1,0:T(8,128)(2,1)} %multiply_convert_fusion.refs_2_.refs_4_, ...), custom_call_target="tpu_custom_call" | custom-call | bytes 100000000 | tf_op jit(solution)/shard_map/chain_sum/pallas_call | solution.py:181
  467.6 6.3 fusion.37
  482.5 33.2 %chain_sum.17 = bf16[384,1536]{1,0:T(8,128)(2,1)} custom-call(bf16[384,1536]{1,0:T(8,128)(2,1)} %fusion.39.x_ref), custom_call_target="tpu_custom_call" | custom-call | bytes 100000000 | tf_op jit(solution)/shard_map/chain_sum/pallas_call | solution.py:181
  522.2 5.9 fusion.163
  528.2 5.6 fusion.40.refs_1_
  539.7 38.0 %chain_sum.18 = (bf16[384,1536]{1,0:T(8,128)(2,1)}, bf16[1536,1536]{1,0:T(8,128)(2,1)}) custom-call(bf16[384,1536]{1,0:T(8,128)(2,1)} %fusion.41.x_ref, bf16[384,1536]{1,0:T(8,128)(2,1)} %copy-done.14, bf16[384,1536]{1,0:T(8,128)(2,1)} %copy-done.10, bf16[384,1536]{1,0:T(8,128)(2,1)} %copy-done.8, bf16[384,1536]{1,0:T(8,128)(2,1)} %copy-done.26), custom_call_target="tpu_custom_call" | custom-call | bytes 100000000 | tf_op jit(solution)/shard_map/chain_sum/pallas_call | solution.py:181
  584.3 7.2 multiply_reduce_fusion.1
  634.0 52.3 %chain_sum.19 = (bf16[384,1536]{1,0:T(8,128)(2,1)}, bf16[1536,2304]{1,0:T(8,128)(2,1)}) custom-call(bf16[384,1536]{1,0:T(8,128)(2,1)} %fusion.33.x_ref, bf16[384,1536]{1,0:T(8,128)(2,1)} %get-tuple-element.65.refs_0_, bf16[384,384]{1,0:T(8,128)(2,1)} %constant_dynamic-slice_fusion.refs_1_.refs_3_, bf16[384,1536]{1,0:T(8,128)(2,1)} %copy-done.15, ...), custom_call_target="tpu_custom_call" | custom-call | bytes 100000000 | tf_op jit(solution)/shard_map/chain_sum/pallas_call | solution.py:181
  687.6 5.8 fusion.45.refs_3_
  693.4 6.6 fusion.29.x_ref
  700.0 47.3 %chain_sum.20 = (bf16[384,1536]{1,0:T(8,128)(2,1)}, bf16[1536,3072]{1,0:T(8,128)(2,1)}) custom-call(bf16[384,1536]{1,0:T(8,128)(2,1)} %fusion.29.x_ref, bf16[384,1536]{1,0:T(8,128)(2,1)} %copy-done.16, bf16[384,1536]{1,0:T(8,128)(2,1)} %copy-done.54, bf16[384,1536]{1,0:T(8,128)(2,1)} %chain_sum.11.refs_2_, bf16[384,1536]{1,0:T(8,128)(2,1)} %copy-done.56, ...), custom_call_target="tpu_custom_call" | custom-call | bytes 100000000 | tf_op jit(solution)/shard_map/chain_sum/pallas_call | solution.py:181
  762.4 43.9 %chain_sum.21 = (bf16[448,1536]{1,0:T(8,128)(2,1)}, bf16[1536,384]{1,0:T(8,128)(2,1)}) custom-call(bf16[448,1536]{1,0:T(8,128)(2,1)} %pad_maximum_fusion.1.x_ref, bf16[384,1536]{1,0:T(8,128)(2,1)} %get-tuple-element.71.refs_0_, bf16[384,384]{1,0:T(8,128)(2,1)} %copy-done.51), custom_call_target="tpu_custom_call" | custom-call | bytes 100000000 | tf_op jit(solution)/shard_map/chain_sum/pallas_call | solution.py:181
  811.1 5.4 concatenate.65
  832.0 30.2 %all-to-all-done.3 = bf16[8,112,1536]{2,1,0:T(8,128)(2,1)} async-done(((bf16[8,112,1536]{2,1,0:T(8,128)(2,1)}), bf16[8,112,1536]{2,1,0:T(8,128)(2,1)}, u32[]{:S(2)}, u32[]{:S(2)}) %all-to-all-start.3) | async-done | bytes 2752544 | tf_op jit(solution)/shard_map/all_to_all | solution.py:539
  (481 shorter events, 289.1 us)
Async XLA Ops:
  7.2 75.7 %all-gather.7.cloned.1.call-start = ((), (), s32[]{:S(2)}) async-start(), calls=%async_computation.8 | async-start | bytes 1769472 | tf_op jit(solution)/shard_map/all_gather | solution.py:266
  14.7 60.3 %copy-start.89 = (s32[384]{0:T(512)}, s32[384]{0:T(512)S(1)}, u32[]{:S(2)}) copy-start(s32[384]{0:T(512)S(1)} %multiply_add_fusion) | copy-start | bytes 4612
  16.5 24.1 %all-to-all-start = ((bf16[8,48,1536]{2,1,0:T(8,128)(2,1)}), bf16[8,48,1536]{2,1,0:T(8,128)(2,1)S(1)}, u32[]{:S(2)}, u32[]{:S(2)}) async-start(bf16[8,48,1536]{2,1,0:T(8,128)(2,1)} %bitcast.2), calls=%async_computation | async-start | bytes 2359296 | tf_op jit(solution)/shard_map/all_to_all | solution.py:300
  21.7 113.7 %all-gather.9.cloned.1.call-start = ((), (), s32[]{:S(2)}) async-start(), calls=%async_computation.9 | async-start | bytes 5308416 | tf_op jit(solution)/shard_map/all_gather | solution.py:266
  43.5 109.9 %all-gather.11.cloned.1.call-start = ((), (), s32[]{:S(2)}) async-start(), calls=%async_computation.10 | async-start | bytes 10616832 | tf_op jit(solution)/shard_map/all_gather | solution.py:266
  44.8 7.7 collective-permute-start
  48.3 8.6 collective-permute-start.3
  52.5 9.1 %collective-permute-start.1 = (bf16[384,384]{0,1:T(8,128)(2,1)S(1)}, bf16[384,384]{0,1:T(8,128)(2,1)S(1)}, u32[]{:S(2)}, u32[]{:S(2)}) collective-permute-start(bf16[384,384]{0,1:T(8,128)(2,1)S(1)} %collective-permute-done), channel_id=1, source_target_pairs={{0,1},{1,2},{2,3},{4,5},{5,6},{6,7},{8,9},{9,10},{10,11},{12,13},{... | collective-permute-start | bytes 884744 | tf_op jit(solution)/shard_map/ppermute | solution.py:285
  57.0 9.2 %collective-permute-start.4 = (bf16[384,384]{0,1:T(8,128)(2,1)S(1)}, bf16[384,384]{0,1:T(8,128)(2,1)S(1)}, u32[]{:S(2)}, u32[]{:S(2)}) collective-permute-start(bf16[384,384]{0,1:T(8,128)(2,1)S(1)} %collective-permute-done.3), channel_id=1, source_target_pairs={{1,0},{2,1},{3,2},{5,4},{6,5},{7,6},{9,8},{10,9},{11,10},{13,12},{... | collective-permute-start | bytes 884744 | tf_op jit(solution)/shard_map/ppermute | solution.py:286
  61.7 8.6 collective-permute-start.2
  66.2 8.6 collective-permute-start.5
  76.7 54.1 %all-to-all-start.1 = ((bf16[8,48,1536]{2,1,0:T(8,128)(2,1)}), bf16[8,48,1536]{2,1,0:T(8,128)(2,1)}, u32[]{:S(2)}, u32[]{:S(2)}) async-start(bf16[8,48,1536]{2,1,0:T(8,128)(2,1)} %bitcast.7), calls=%async_computation.1 | async-start | bytes 2359296 | tf_op jit(solution)/shard_map/all_to_all | solution.py:300
  81.9 188.3 %all-gather.13.cloned.1.call-start = ((), (), s32[]{:S(2)}) async-start(), calls=%async_computation.11 | async-start | bytes 10616832 | tf_op jit(solution)/shard_map/all_gather | solution.py:266
  86.7 60.1 %copy-start.4 = (bf16[384,1536]{1,0:T(8,128)(2,1)}, bf16[384,1536]{1,0:T(8,128)(2,1)S(1)}, u32[]{:S(2)}) copy-start(bf16[384,1536]{1,0:T(8,128)(2,1)S(1)} %fusion.75.refs_6_.refs_12_.refs_18_) | copy-start | bytes 3538948
  132.1 249.1 %all-gather.15.cloned.1.call-start = ((), (), s32[]{:S(2)}) async-start(), calls=%async_computation.12 | async-start | bytes 10616832 | tf_op jit(solution)/shard_map/all_gather | solution.py:266
  222.3 315.5 %reduce-scatter.13.cloned.1.call-start = ((), (), s32[]{:S(2)}) async-start(), calls=%async_computation.17 | async-start | bytes 1474560
  277.8 46.8 %copy-start.16 = (bf16[384,1536]{1,0:T(8,128)(2,1)}, bf16[384,1536]{1,0:T(8,128)(2,1)S(1)}, u32[]{:S(2)}) copy-start(bf16[384,1536]{1,0:T(8,128)(2,1)S(1)} %fusion.34.refs_0_) | copy-start | bytes 3538948
  281.4 53.9 %copy-start.27 = (bf16[384,1536]{1,0:T(8,128)(2,1)}, bf16[384,1536]{1,0:T(8,128)(2,1)S(1)}, u32[]{:S(2)}) copy-start(bf16[384,1536]{1,0:T(8,128)(2,1)S(1)} %get-tuple-element.230.refs_5_) | copy-start | bytes 3538948
  397.6 221.5 %reduce-scatter.7.cloned.1.call-start = ((), (), s32[]{:S(2)}) async-start(), calls=%async_computation.13 | async-start | bytes 10616832 | tf_op jit(solution)/shard_map/reduce_scatter | solution.py:434
  579.9 37.1 %all-to-all-start.2 = ((bf16[8,48,384]{2,1,0:T(8,128)(2,1)}), bf16[8,48,384]{2,1,0:T(8,128)(2,1)}, u32[]{:S(2)}, u32[]{:S(2)}) async-start(bf16[8,48,384]{2,1,0:T(8,128)(2,1)} %bitcast.185), calls=%async_computation.3 | async-start | bytes 589824 | tf_op jit(solution)/shard_map/all_to_all | solution.py:305
  584.0 177.2 %all-gather.17.cloned.1.call-start = ((), (), s32[]{:S(2)}) async-start(), calls=%async_computation.15 | async-start | bytes 1474560 | tf_op jit(solution)/shard_map/all_gather | solution.py:481
  619.1 142.1 %reduce-scatter.9.cloned.1.call-start = ((), (), s32[]{:S(2)}) async-start(), calls=%async_computation.14 | async-start | bytes 7962624 | tf_op jit(solution)/shard_map/reduce_scatter | solution.py:497
  686.4 183.2 %reduce-scatter.11.cloned.1.call-start = ((), (), s32[]{:S(2)}) async-start(), calls=%async_computation.16 | async-start | bytes 10616832 | tf_op jit(solution)/shard_map/reduce_scatter | solution.py:507
  824.0 38.2 %all-to-all-start.3 = ((bf16[8,112,1536]{2,1,0:T(8,128)(2,1)}), bf16[8,112,1536]{2,1,0:T(8,128)(2,1)}, u32[]{:S(2)}, u32[]{:S(2)}) async-start(bf16[8,112,1536]{2,1,0:T(8,128)(2,1)} %pad_maximum_fusion), calls=%async_computation.5 | async-start | bytes 5505024 | tf_op jit(solution)/shard_map/all_to_all | solution.py:539
  (122 other events, 519.6 us)
Sparse Core Ops, SparseCore 0:
  13.1 33.1 all-gather.6
  48.8 38.6 all-gather.8
  90.0 63.3 all-gather.10
  155.7 58.7 all-gather.12
  222.5 57.1 all-gather.14
  397.7 39.1 reduce-scatter.12
  461.7 75.5 reduce-scatter.6
  619.2 32.1 all-gather.16
  686.5 63.7 reduce-scatter.8
  753.6 76.8 reduce-scatter.10

commit v2 on v1

--- a/solution.py
+++ b/solution.py
@@ -63,7 +63,8 @@
         stage, put_sem = refs[8], refs[9]
         rows = pl.ds(pl.multiple_of(tile * TILE, TILE), TILE)
         slot = lax.rem(tile, 2)
-        return pltpu.make_async_copy(stage.at[slot], g_ref.at[rows], put_sem.at[slot])
+        target = g_ref.at[rows, pl.ds(0, stage.shape[2])]
+        return pltpu.make_async_copy(stage.at[slot], target, put_sem.at[slot])
 
     def fill(tile):
         stage = refs[8]
@@ -126,15 +127,20 @@
 
     tiles = g_ref.shape[0] // TILE if layout else 0
 
-    @pl.loop(0, max(pieces + 1, tiles))
+    per = 2 if layout else 1
+    turns = pieces // per
+
+    @pl.loop(0, max(turns + 1, tiles))
     def _(p):
-        @pl.when(jnp.logical_and(inner, p < pieces))
+        @pl.when(jnp.logical_and(inner, p < turns))
         def _():
-            first_add(p)
-
-        @pl.when(jnp.logical_and(inner, jnp.logical_and(p >= 1, p <= pieces)))
+            for k in range(per):
+                first_add(p * per + k)
+
+        @pl.when(jnp.logical_and(inner, jnp.logical_and(p >= 1, p <= turns)))
         def _():
-            second_add(p - 1)
+            for k in range(per):
+                second_add((p - 1) * per + k)
 
         if layout:
 
@@ -161,9 +167,9 @@
             down(p).wait_send()
 
 
-def chain_sum(x, call_id=1, products=()):
+def chain_sum(x, call_id=1, products=(), room=0):
     rows, cols = x.shape
-    pieces = rows // 32
+    pieces = rows // 16
     dma = pltpu.SemaphoreType.DMA
     vmem = pl.BlockSpec(memory_space=pltpu.VMEM)
     layout = tuple(
@@ -175,7 +181,7 @@
     scratch = [pltpu.VMEM((rows, cols), BF)] * 3 + [dma((pieces,))] * 5
     if products:
         width, high = sum(w for w, _ in layout), products[0][0][0].shape[1]
-        out_shape.append(jax.ShapeDtypeStruct((high, width), BF))
+        out_shape.append(jax.ShapeDtypeStruct((high, width + room), BF))
         out_specs.append(pl.BlockSpec(memory_space=pl.ANY))
         scratch += [pltpu.VMEM((2, TILE, width), BF), dma((2,))]
     out = pl.pallas_call(
@@ -272,21 +278,17 @@
 
     vectors = jnp.stack([gain_attn, gain_mem, gain_ffn, w_rate], axis=1)
     pad = jnp.zeros((shard, 128 - slots - 4), BF)
-    small, wqm_t = gather(jnp.concatenate([persist.T, vectors, pad], axis=1), w_query_mem.T)
-    w_in, w_out_t = gather(mem_in, mem_out.T)
+    small, wqm_t, wq, wk, wv, wo_t = gather(
+        jnp.concatenate([persist.T, vectors, pad], axis=1),
+        w_query_mem.T,
+        w_query,
+        w_key,
+        w_value,
+        w_output.T,
+    )
     persistent = small[:, :slots].T
     gains = small[:, slots : slots + 4].astype(F32).T
     g_attn, g_mem, g_ffn, rate_w = (gains[i][None, :] for i in range(4))
-
-    ends = lax.axis_size("tensor")
-    columns = jnp.concatenate([w_key_mem, w_value_mem], axis=1)
-    before, after = [columns], [columns]
-    for _ in range(ends - 1):
-        before.append(lax.ppermute(before[-1], "tensor", [(i, i + 1) for i in range(ends - 1)]))
-        after.append(lax.ppermute(after[-1], "tensor", [(i + 1, i) for i in range(ends - 1)]))
-    line = jnp.concatenate(before[:0:-1] + after, axis=0)
-    high = columns.shape[0]
-    tall = lax.dynamic_slice_in_dim(line, (ends - 1 - me) * high, ends * high, 0)
 
     place = jnp.arange(count, dtype=jnp.int32)
     home = dest // count
@@ -308,10 +310,8 @@
         return t_dot(send_m, back).astype(BF)
 
     dealt = dot(deal_m, exchange(tokens)).astype(BF)
-    dealt, later, late_query, late_key, late_value, late_output = together(
-        dealt, cotangent, w_query, w_key, w_value, w_output
-    )
-    wq, wk, wv, wo_t = gather(late_query, late_key, late_value, late_output.T)
+    dealt, later, late_in, late_mem_out = together(dealt, cotangent, mem_in, mem_out)
+    w_in, w_out_t = gather(late_in, late_mem_out.T)
     cotangent_arrived = exchange(later)
     x = dealt.astype(F32)
 
@@ -340,17 +340,21 @@
     n1 = (x * r1 * g_attn).astype(BF)
     n1_own = own(n1)
     query_mem = chain_sum(dot_t(n1_own, wqm_t))
-    query_mem, cotangent_arrived, tall = together(query_mem, cotangent_arrived, tall)
-    wkm_t, wvm_t = gather(tall[:, :shard].T, tall[:, shard:].T)
+    columns = jnp.concatenate([w_key_mem, w_value_mem], axis=1)
+    query_mem, cotangent_arrived, columns = together(query_mem, cotangent_arrived, columns)
+    tall = lax.all_gather(columns, "tensor", axis=0, tiled=True)
     d_out_low = dot(deal_m, cotangent_arrived).astype(BF)
+    query = dot(n1, wq).astype(BF)
+    key_p, value_p = dot(persistent, wk).astype(BF), dot(persistent, wv).astype(BF)
+    key_x, value_x = dot(n1, wk).astype(BF), dot(n1, wv).astype(BF)
+    w_in, query, key_p, value_p, key_x, value_x = together(w_in, query, key_p, value_p, key_x, value_x)
     read_s, read_act, read_slope = silu_parts(dot(query_mem, w_in))
     read_low = read_act.astype(BF)
     memory = chain_sum(dot_t(read_low, w_out_t))
-
-    query = dot(n1, wq).astype(BF)
-    key_p, value_p = dot(persistent, wk).astype(BF), dot(persistent, wv).astype(BF)
+    memory, tall = together(memory, tall)
+    wkm_t, wvm_t = gather(tall[:, :shard].T, tall[:, shard:].T)
+
     key_m, value_m = dot(memory, wk).astype(BF), dot(memory, wv).astype(BF)
-    key_x, value_x = dot(n1, wk).astype(BF), dot(n1, wv).astype(BF)
 
     def context(p, m, t):
         wide = jnp.broadcast_to(p[None], (batches,) + p.shape)
@@ -503,13 +507,14 @@
             [(key_mem, d_key_hidden), (query_mem, d_read)],
             [(d_miss, key_act), (d_memory, read_low), (gw_out_early,)],
         ],
-    )
+        inner,
+    )
+    gw_query_mem = t_dot(d_query_mem, n1_own).astype(BF)
+    gw_mem = lax.dynamic_update_slice(gw_mem, gw_query_mem, (0, 2 * hidden))
     share_mem = lax.psum_scatter(gw_mem, "dp", scatter_dimension=0, tiled=True)
     d_n1_part = d_n1_part + in_own(dot(d_query_mem, wqm_t))
     d_n1_part, share_attn, output = together(d_n1_part.astype(BF), share_attn, output)
-    last, gw_query_mem = chain_sum(
-        jnp.concatenate([d_n1_part, d_persist_part.astype(BF)], axis=0), 5, [[(d_query_mem, n1_own)]]
-    )
+    last = chain_sum(jnp.concatenate([d_n1_part, d_persist_part.astype(BF)], axis=0), 5)
     d_n1 = last[:count].astype(F32)
     g_persist = last[count:]
     gg_attn = jnp.sum(d_n1 * x * r1, axis=0)
@@ -524,11 +529,10 @@
 
     s_down, s_gate, s_up = cut(share_ffn, *[w_gate.shape[1]] * 3)
     s_key_mem, s_value_mem, s_output, s_query, s_key, s_value = cut(share_attn, *[inner] * 6)
-    s_in, s_out = cut(share_mem, hidden, hidden)
+    s_in, s_out, s_query_mem = cut(share_mem, hidden, hidden, inner)
     grad_vectors = jnp.stack([gg_attn, gg_mem, gg_ffn, gg_rate], axis=1)
     rest = jnp.concatenate(
         [
-            gw_query_mem,
             g_persist.T,
             grad_vectors.astype(BF),
             jnp.zeros((width, 128 - slots - 4), BF),
@@ -542,7 +546,7 @@
     seats = count // ranks
     grad_tokens = t_dot(send_m, came[:, :seats].reshape(count, width)).astype(BF)
     share_rest = jnp.sum(came[:, seats:].astype(F32), axis=0).reshape(shard, -1)
-    s_query_mem, s_small = cut(share_rest, inner, 128)
+    s_small = share_rest
     s_vectors = s_small[:, slots : slots + 4].T
 
     return (

time: 889 us -> 978 us (1.10)
  Pallas kernels: 461 us -> 559 us
  starting transfers between devices: 37 us -> 18.1 us
    pallas_call x11, Pallas kernels: 461 us -> 559 us  [chain_sum(): pl.pallas_call(functools.partial(chain_sum_kernel, pieces, layout), out_s...]
    all_gather x5 -> x4, waiting for transfers between devices: 1.6 us -> 26.9 us  [gather(): whole = lax.all_gather(packed, 'dp', axis=0, tiled=True)]
    ppermute x6 -> x0, starting transfers between devices: 16.2 us -> none  [the longest x3 12.3 us: per_device(): lax.ppermute(before[-1], 'tensor', [(i, i + 1) for i in range(ends - 1)])]
    ppermute x6 -> x0, waiting for transfers between devices: 13.4 us -> none  [the longest x3 9.18 us: per_device(): lax.ppermute(before[-1], 'tensor', [(i, i + 1) for i in range(ends - 1)])]
    unnamed x264 -> x265, local copies, waits for them, and re-layouts: 33.2 us -> 28.3 us
  transfers between devices with their start and end apart: 20 -> 14, of which waited for: 8 -> 3; matrix products, arithmetic and copies ran while one was open for 28% -> 26% of each run, Pallas kernels for 52% -> 58%
where the time goes in v2:
time: 978 us; the launch traced here: 967 us
  Pallas kernels  559 us (57%)
  matrix products  167 us (17%)
  local copies, waits for them, and re-layouts  83.9 us (9%)
  waiting for transfers between devices  73.5 us (8%)
  other arithmetic  49.2 us (5%)
  starting transfers between devices  18.1 us (2%)
  between operations  16.4 us (2%)
    pallas_call x11, Pallas kernels, chain_sum(): pl.pallas_call(functools.partial(chain_sum_kernel, pieces, layout), out_s...  559 us
    dot_general x24, matrix products, dot(): lax.dot_general(left, right, (((1,), (0,)), ((), ())), preferred_element_...  81.9 us
    dot_general x20, matrix products, dot_t(): lax.dot_general(left, right, (((1,), (1,)), ((), ())), preferred_element_...  51.6 us
    unnamed x265, local copies, waits for them, and re-layouts  28.3 us
    all_gather x4, waiting for transfers between devices, gather(): whole = lax.all_gather(packed, 'dp', axis=0, tiled=True)  26.9 us
    all_to_all x2, waiting for transfers between devices, exchange(): lax.all_to_all(dot(send_m, v).astype(BF), 'dp', split_axis=0, concat_axis...  24.9 us
    all_to_all x1, waiting for transfers between devices, per_device(): lax.all_to_all(jnp.concatenate([turned, rest], axis=1), 'dp', split_axis=...  21.5 us
  transfers between devices with their start and end apart: 14, of which 3 were waited for; matrix products, arithmetic and copies ran while one was open for 26% of the time, Pallas kernels for 58%

profile of v2, /device:TPU:0, one launch (start us, length us, event | category | flops | bytes accessed | tf_op | source)
XLA Modules:
  0.0 967.1 jit_solution(5083979346365198209)
XLA Ops:
  15.5 5.3 all-to-all-start
  21.1 24.9 %all-to-all-done = bf16[8,48,1536]{2,1,0:T(8,128)(2,1)S(1)} async-done(((bf16[8,48,1536]{2,1,0:T(8,128)(2,1)}), bf16[8,48,1536]{2,1,0:T(8,128)(2,1)S(1)}, u32[]{:S(2)}, u32[]{:S(2)}) %all-to-all-start) | async-done | bytes 1179680 | tf_op jit(solution)/shard_map/all_to_all | solution.py:302
  56.1 26.9 %all-gather.9.cloned.1.call-done = bf16[1536,2048]{1,0:T(8,128)(2,1)} async-done(((bf16[192,2048]{1,0:T(8,128)(2,1)}), bf16[1536,2048]{1,0:T(8,128)(2,1)}) %all-gather.9.cloned.1.call-update) | async-done | bytes 6291472 | tf_op jit(solution)/shard_map/all_gather | solution.py:272
  89.4 51.8 %chain_sum.11.refs_2_ = bf16[384,1536]{1,0:T(8,128)(2,1)} custom-call(bf16[384,1536]{1,0:T(8,128)(2,1)} %convolution_convert_fusion.9.x_ref), custom_call_target="tpu_custom_call" | custom-call | bytes 100000000 | tf_op jit(solution)/shard_map/chain_sum/pallas_call | solution.py:187
  166.2 55.5 %chain_sum.12.refs_10_.refs_16_ = bf16[384,1536]{1,0:T(8,128)(2,1)} custom-call(bf16[384,1536]{1,0:T(8,128)(2,1)} %convolution_convert_fusion.1.x_ref), custom_call_target="tpu_custom_call" | custom-call | bytes 100000000 | tf_op jit(solution)/shard_map/chain_sum/pallas_call | solution.py:187
  269.6 50.1 %chain_sum.13 = bf16[384,1536]{1,0:T(8,128)(2,1)} custom-call(bf16[384,1536]{1,0:T(8,128)(2,1)} %convolution_convert_fusion.6.x_ref), custom_call_target="tpu_custom_call" | custom-call | bytes 100000000 | tf_op jit(solution)/shard_map/chain_sum/pallas_call | solution.py:187
  338.7 56.3 %chain_sum.14 = bf16[384,1536]{1,0:T(8,128)(2,1)} custom-call(bf16[384,1536]{1,0:T(8,128)(2,1)} %fusion.18.x_ref), custom_call_target="tpu_custom_call" | custom-call | bytes 100000000 | tf_op jit(solution)/shard_map/chain_sum/pallas_call | solution.py:187
  397.1 6.0 multiply_convert_fusion.2
  409.9 47.4 %chain_sum.15 = bf16[384,1536]{1,0:T(8,128)(2,1)} custom-call(bf16[384,1536]{1,0:T(8,128)(2,1)} %fusion.24.x_ref), custom_call_target="tpu_custom_call" | custom-call | bytes 100000000 | tf_op jit(solution)/shard_map/chain_sum/pallas_call | solution.py:187
  482.4 4.3 fusion.17.x_ref
  486.7 52.0 %chain_sum.16 = (bf16[384,1536]{1,0:T(8,128)(2,1)}, bf16[1536,3072]{1,0:T(8,128)(2,1)}) custom-call(bf16[384,1536]{1,0:T(8,128)(2,1)} %fusion.17.x_ref, bf16[384,1536]{1,0:T(8,128)(2,1)} %convolution_convert_fusion.7.refs_0_, bf16[384,1024]{1,0:T(8,128)(2,1)} %copy-done.56, bf16[384,1536]{1,0:T(8,128)(2,1)} %multiply_convert_fusion.refs_2_.refs_4_, ...), custom_call_target="tpu_custom_call" | custom-call | bytes 100000000 | tf_op jit(solution)/shard_map/chain_sum/pallas_call | solution.py:187
  546.8 5.5 fusion.23
  561.1 51.2 %chain_sum.17 = bf16[384,1536]{1,0:T(8,128)(2,1)} custom-call(bf16[384,1536]{1,0:T(8,128)(2,1)} %fusion.25.x_ref), custom_call_target="tpu_custom_call" | custom-call | bytes 100000000 | tf_op jit(solution)/shard_map/chain_sum/pallas_call | solution.py:187
  619.5 5.9 fusion.152
  625.4 5.6 fusion.26.refs_1_
  636.9 37.1 %chain_sum.18 = (bf16[384,1536]{1,0:T(8,128)(2,1)}, bf16[1536,1536]{1,0:T(8,128)(2,1)}) custom-call(bf16[384,1536]{1,0:T(8,128)(2,1)} %fusion.27.x_ref, bf16[384,1536]{1,0:T(8,128)(2,1)} %copy-done.15, bf16[384,1536]{1,0:T(8,128)(2,1)} %copy-done.11, bf16[384,1536]{1,0:T(8,128)(2,1)} %copy-done.9, bf16[384,1536]{1,0:T(8,128)(2,1)} %copy-done.28), custom_call_target="tpu_custom_call" | custom-call | bytes 100000000 | tf_op jit(solution)/shard_map/chain_sum/pallas_call | solution.py:187
  676.2 4.1 all-to-all-start.2
  680.6 7.2 multiply_reduce_fusion.1
  730.9 52.1 %chain_sum.19 = (bf16[384,1536]{1,0:T(8,128)(2,1)}, bf16[1536,2304]{1,0:T(8,128)(2,1)}) custom-call(bf16[384,1536]{1,0:T(8,128)(2,1)} %fusion.19.x_ref, bf16[384,1536]{1,0:T(8,128)(2,1)} %get-tuple-element.75.refs_0_, bf16[384,384]{1,0:T(8,128)(2,1)} %constant_dynamic-slice_fusion.refs_1_.refs_3_, bf16[384,1536]{1,0:T(8,128)(2,1)} %copy-done.16, ...), custom_call_target="tpu_custom_call" | custom-call | bytes 100000000 | tf_op jit(solution)/shard_map/chain_sum/pallas_call | solution.py:187
  784.3 5.4 fusion.29.refs_3_
  792.9 48.0 %chain_sum.20 = (bf16[384,1536]{1,0:T(8,128)(2,1)}, bf16[1536,3456]{1,0:T(8,128)(2,1)}) custom-call(bf16[384,1536]{1,0:T(8,128)(2,1)} %convolution_convert_fusion.x_ref, bf16[384,1536]{1,0:T(8,128)(2,1)} %copy-done.17, bf16[384,1536]{1,0:T(8,128)(2,1)} %copy-done.52, bf16[384,1536]{1,0:T(8,128)(2,1)} %chain_sum.11.refs_2_, bf16[384,1536]{1,0:T(8,128)(2,1)} %copy-done.54, ...), custom_call_target="tpu_custom_call" | custom-call | bytes 100000000 | tf_op jit(solution)/shard_map/chain_sum/pallas_call | solution.py:187
  856.5 57.2 %chain_sum.21 = bf16[448,1536]{1,0:T(8,128)(2,1)} custom-call(bf16[448,1536]{1,0:T(8,128)(2,1)} %pad_maximum_fusion.1.x_ref), custom_call_target="tpu_custom_call" | custom-call | bytes 100000000 | tf_op jit(solution)/shard_map/chain_sum/pallas_call | solution.py:187
  921.4 4.1 all-to-all-start.3
  928.9 21.5 %all-to-all-done.3 = bf16[8,64,1536]{2,1,0:T(8,128)(2,1)S(1)} async-done(((bf16[8,64,1536]{2,1,0:T(8,128)(2,1)}), bf16[8,64,1536]{2,1,0:T(8,128)(2,1)S(1)}, u32[]{:S(2)}, u32[]{:S(2)}) %all-to-all-start.3) | async-done | bytes 1572896 | tf_op jit(solution)/shard_map/all_to_all | solution.py:543
  (473 shorter events, 265.2 us)
Async XLA Ops:
  7.2 75.7 %all-gather.9.cloned.1.call-start = ((), (), s32[]{:S(2)}) async-start(), calls=%async_computation.9 | async-start | bytes 7077888 | tf_op jit(solution)/shard_map/all_gather | solution.py:272
  13.6 36.1 %copy-start.84 = (s32[384]{0:T(512)}, s32[384]{0:T(512)S(1)}, u32[]{:S(2)}) copy-start(s32[384]{0:T(512)S(1)} %multiply_add_fusion) | copy-start | bytes 4612
  15.5 31.3 %copy-start.58 = (bf16[1536,192]{0,1:T(8,128)(2,1)S(1)}, bf16[1536,192]{0,1:T(8,128)(2,1)}, u32[]{:S(2)}) copy-start(bf16[1536,192]{0,1:T(8,128)(2,1)} %param.31) | copy-start | bytes 1769476
  15.5 31.3 %copy-start.59 = (bf16[192,1536]{1,0:T(8,128)(2,1)S(1)}, bf16[192,1536]{1,0:T(8,128)(2,1)}, u32[]{:S(2)}) copy-start(bf16[192,1536]{1,0:T(8,128)(2,1)} %param.30) | copy-start | bytes 1769476
  15.5 30.5 %all-to-all-start = ((bf16[8,48,1536]{2,1,0:T(8,128)(2,1)}), bf16[8,48,1536]{2,1,0:T(8,128)(2,1)S(1)}, u32[]{:S(2)}, u32[]{:S(2)}) async-start(bf16[8,48,1536]{2,1,0:T(8,128)(2,1)} %bitcast), calls=%async_computation | async-start | bytes 2359296 | tf_op jit(solution)/shard_map/all_to_all | solution.py:302
  20.8 133.6 %all-gather.7.cloned.1.call-start = ((), (), s32[]{:S(2)}) async-start(), calls=%async_computation.8 | async-start | bytes 10616832 | tf_op jit(solution)/shard_map/all_gather | solution.py:272
  21.1 26.9 %copy-start.81 = (s32[384]{0:T(512)}, s32[384]{0:T(512)S(1)}, u32[]{:S(2)}) copy-start(s32[384]{0:T(512)S(1)} %convert_reduce_fusion.2) | copy-start | bytes 4612
  51.5 89.7 %all-to-all-start.1 = ((bf16[8,48,1536]{2,1,0:T(8,128)(2,1)}), bf16[8,48,1536]{2,1,0:T(8,128)(2,1)S(1)}, u32[]{:S(2)}, u32[]{:S(2)}) async-start(bf16[8,48,1536]{2,1,0:T(8,128)(2,1)} %bitcast.8), calls=%async_computation.1 | async-start | bytes 2359296 | tf_op jit(solution)/shard_map/all_to_all | solution.py:302
  55.1 166.6 %all-gather.11.cloned.1.call-start = ((), (), s32[]{:S(2)}) async-start(), calls=%async_computation.10 | async-start | bytes 1474560 | tf_op jit(solution)/shard_map/all_gather | solution.py:345
  87.6 64.0 %copy-start.4 = (bf16[384,1536]{1,0:T(8,128)(2,1)}, bf16[384,1536]{1,0:T(8,128)(2,1)S(1)}, u32[]{:S(2)}) copy-start(bf16[384,1536]{1,0:T(8,128)(2,1)S(1)} %fusion.60.refs_6_.refs_12_.refs_18_) | copy-start | bytes 3538948
  141.3 182.2 %all-gather.13.cloned.1.call-start = ((), (), s32[]{:S(2)}) async-start(), calls=%async_computation.11 | async-start | bytes 10616832 | tf_op jit(solution)/shard_map/all_gather | solution.py:272
  224.2 237.9 %all-gather.15.cloned.1.call-start = ((), (), s32[]{:S(2)}) async-start(), calls=%async_computation.12 | async-start | bytes 10616832 | tf_op jit(solution)/shard_map/all_gather | solution.py:272
  264.6 370.5 %reduce-scatter.13.cloned.1.call-start = ((), (), s32[]{:S(2)}) async-start(), calls=%async_computation.17 | async-start | bytes 1474560
  269.6 52.5 %copy-start.80 = (f32[1536]{0:T(1024)S(1)}, f32[1536]{0:T(1024)}, u32[]{:S(2)}) copy-start(f32[1536]{0:T(1024)} %get-tuple-element.192) | copy-start | bytes 18436
  329.5 65.5 %copy-start.17 = (bf16[384,1536]{1,0:T(8,128)(2,1)}, bf16[384,1536]{1,0:T(8,128)(2,1)S(1)}, u32[]{:S(2)}) copy-start(bf16[384,1536]{1,0:T(8,128)(2,1)S(1)} %fusion.20.refs_0_) | copy-start | bytes 3538948
  333.1 72.6 %copy-start.29 = (bf16[384,1536]{1,0:T(8,128)(2,1)}, bf16[384,1536]{1,0:T(8,128)(2,1)S(1)}, u32[]{:S(2)}) copy-start(bf16[384,1536]{1,0:T(8,128)(2,1)S(1)} %get-tuple-element.238.refs_5_) | copy-start | bytes 3538948
  478.5 238.5 %reduce-scatter.7.cloned.1.call-start = ((), (), s32[]{:S(2)}) async-start(), calls=%async_computation.13 | async-start | bytes 10616832 | tf_op jit(solution)/shard_map/reduce_scatter | solution.py:438
  676.2 38.8 %all-to-all-start.2 = ((bf16[8,48,384]{2,1,0:T(8,128)(2,1)}), bf16[8,48,384]{2,1,0:T(8,128)(2,1)}, u32[]{:S(2)}, u32[]{:S(2)}) async-start(bf16[8,48,384]{2,1,0:T(8,128)(2,1)} %bitcast.207), calls=%async_computation.3 | async-start | bytes 589824 | tf_op jit(solution)/shard_map/all_to_all | solution.py:307
  680.2 175.1 %all-gather.17.cloned.1.call-start = ((), (), s32[]{:S(2)}) async-start(), calls=%async_computation.15 | async-start | bytes 1474560 | tf_op jit(solution)/shard_map/all_gather | solution.py:485
  717.0 138.3 %reduce-scatter.9.cloned.1.call-start = ((), (), s32[]{:S(2)}) async-start(), calls=%async_computation.14 | async-start | bytes 7962624 | tf_op jit(solution)/shard_map/reduce_scatter | solution.py:501
  783.0 171.1 %reduce-scatter.11.cloned.1.call-start = ((), (), s32[]{:S(2)}) async-start(), calls=%async_computation.16 | async-start | bytes 11943936 | tf_op jit(solution)/shard_map/reduce_scatter | solution.py:514
  855.3 58.5 %copy-start.74 = (f32[1536]{0:T(1024)S(1)}, f32[1536]{0:T(1024)}, u32[]{:S(2)}) copy-start(f32[1536]{0:T(1024)} %copy-done.73) | copy-start | bytes 18436
  855.3 58.5 %copy-start.90 = (f32[384]{0:T(512)S(1)}, f32[384]{0:T(512)}, u32[]{:S(2)}) copy-start(f32[384]{0:T(512)} %get-tuple-element.229) | copy-start | bytes 4612
  921.4 29.0 %all-to-all-start.3 = ((bf16[8,64,1536]{2,1,0:T(8,128)(2,1)}), bf16[8,64,1536]{2,1,0:T(8,128)(2,1)S(1)}, u32[]{:S(2)}, u32[]{:S(2)}) async-start(bf16[8,64,1536]{2,1,0:T(8,128)(2,1)} %pad_maximum_fusion), calls=%async_computation.5 | async-start | bytes 3145728 | tf_op jit(solution)/shard_map/all_to_all | solution.py:543
  (121 other events, 505.4 us)
Sparse Core Ops, SparseCore 0:
  13.5 69.4 all-gather.8
  85.4 60.3 all-gather.6
  148.0 39.1 all-gather.10
  224.3 59.4 all-gather.12
  286.1 58.6 all-gather.14
  478.6 38.2 reduce-scatter.12
  542.0 75.8 reduce-scatter.6
  717.2 34.1 all-gather.16
  783.2 65.0 reduce-scatter.8
  851.6 86.5 reduce-scatter.10

commit v3 on v2

--- a/solution.py
+++ b/solution.py
@@ -127,20 +127,20 @@
 
     tiles = g_ref.shape[0] // TILE if layout else 0
 
-    per = 2 if layout else 1
+    per, lag = (2, 2) if layout else (1, 3)
     turns = pieces // per
 
-    @pl.loop(0, max(turns + 1, tiles))
+    @pl.loop(0, max(turns + lag, tiles))
     def _(p):
         @pl.when(jnp.logical_and(inner, p < turns))
         def _():
             for k in range(per):
                 first_add(p * per + k)
 
-        @pl.when(jnp.logical_and(inner, jnp.logical_and(p >= 1, p <= turns)))
+        @pl.when(jnp.logical_and(inner, jnp.logical_and(p >= lag, p < turns + lag)))
         def _():
             for k in range(per):
-                second_add((p - 1) * per + k)
+                second_add((p - lag) * per + k)
 
         if layout:
 
@@ -197,6 +197,101 @@
     return out if products else out[0]
 
 
+def line_gather_kernel(pieces, x_ref, o_ref, sent, got, keep):
+    me = lax.axis_index("tensor")
+    high = x_ref.shape[0]
+    step = high // pieces
+    last = 3
+    barrier = pltpu.get_barrier_semaphore()
+    ways = ((0, me < last, 1), (1, me > 0, -1))
+
+    for _, open_, move in ways:
+
+        @pl.when(open_)
+        def _():
+            pl.semaphore_signal(
+                barrier, inc=1, device_id={"tensor": me + move}, device_id_type=MESH
+            )
+
+    at_end = jnp.logical_or(me == 0, me == last)
+
+    @pl.when(at_end)
+    def _():
+        pl.semaphore_wait(barrier, 1)
+
+    @pl.when(jnp.logical_not(at_end))
+    def _():
+        pl.semaphore_wait(barrier, 2)
+
+    def copy(way, hop, piece, move, block, first=False):
+        rows = pl.ds(pl.multiple_of(block * high + piece * step, step), step)
+        return pltpu.make_async_remote_copy(
+            src_ref=x_ref.at[pl.ds(piece * step, step)] if first else o_ref.at[rows],
+            dst_ref=o_ref.at[rows],
+            send_sem=sent.at[way, hop, piece],
+            recv_sem=got.at[way, hop, piece],
+            device_id={"tensor": jnp.clip(me + move, 0, last)},
+            device_id_type=MESH,
+        )
+
+    def forward(way, move, hop):
+        block = me - move * hop
+        return jnp.logical_and(
+            jnp.logical_and(me + move >= 0, me + move <= last),
+            jnp.logical_and(block >= 0, block <= last),
+        )
+
+    def comes(way, move, hop):
+        block = me - move * (hop + 1)
+        return jnp.logical_and(block >= 0, block <= last)
+
+    def own():
+        rows = pl.ds(pl.multiple_of(me * high, high), high)
+        return pltpu.make_async_copy(x_ref, o_ref.at[rows], keep.at[0])
+
+    for hop in range(last):
+        for piece in range(pieces):
+            for way, _, move in ways:
+
+                @pl.when(forward(way, move, hop))
+                def _():
+                    copy(way, hop, piece, move, me - move * hop, hop == 0).start()
+
+        if hop == 0:
+            own().start()
+        for piece in range(pieces):
+            for way, _, move in ways:
+
+                @pl.when(comes(way, move, hop))
+                def _():
+                    copy(way, hop, piece, move, me - move * (hop + 1)).wait_recv()
+
+    own().wait()
+    for hop in range(last):
+        for piece in range(pieces):
+            for way, _, move in ways:
+
+                @pl.when(forward(way, move, hop))
+                def _():
+                    copy(way, hop, piece, move, me - move * hop, hop == 0).wait_send()
+
+
+def line_gather(x, call_id, pieces=2):
+    rows, cols = x.shape
+    dma = pltpu.SemaphoreType.DMA
+    vmem = pl.BlockSpec(memory_space=pltpu.VMEM)
+    return pl.pallas_call(
+        functools.partial(line_gather_kernel, pieces),
+        out_shape=jax.ShapeDtypeStruct((4 * rows, cols), BF),
+        in_specs=[vmem],
+        out_specs=vmem,
+        scratch_shapes=[dma((2, 3, pieces)), dma((2, 3, pieces)), dma((1,))],
+        compiler_params=pltpu.CompilerParams(collective_id=call_id, has_side_effects=True),
+        cost_estimate=pl.CostEstimate(flops=0, bytes_accessed=5 * 10**7, transcendentals=0),
+        name="line_gather",
+    )(x)
+
+
 def dot(left, right):
     return lax.dot_general(left, right, (((1,), (0,)), ((), ())), preferred_element_type=F32)
 
@@ -211,6 +306,14 @@
 
 def batch_dot(spec, left, right):
     return jnp.einsum(spec, left, right, preferred_element_type=F32)
+
+
+def cut_apart(whole, *widths):
+    out, low = [], 0
+    for width in widths:
+        out.append(whole[:, low : low + width])
+        low += width
+    return out
 
 
 def together(*values):
@@ -267,25 +370,16 @@
     slots = persist.shape[0]
     me = lax.axis_index("tensor")
 
+    def gather_whole(*parts):
+        return lax.all_gather(jnp.concatenate(parts, axis=1), "dp", axis=0, tiled=True)
+
     def gather(*parts):
-        packed = jnp.concatenate(parts, axis=1)
-        whole = lax.all_gather(packed, "dp", axis=0, tiled=True)
-        out, low = [], 0
-        for part in parts:
-            out.append(whole[:, low : low + part.shape[1]])
-            low += part.shape[1]
-        return out
+        return cut_apart(gather_whole(*parts), *[part.shape[1] for part in parts])
 
     vectors = jnp.stack([gain_attn, gain_mem, gain_ffn, w_rate], axis=1)
     pad = jnp.zeros((shard, 128 - slots - 4), BF)
-    small, wqm_t, wq, wk, wv, wo_t = gather(
-        jnp.concatenate([persist.T, vectors, pad], axis=1),
-        w_query_mem.T,
-        w_query,
-        w_key,
-        w_value,
-        w_output.T,
-    )
+    small, wqm_t = gather(jnp.concatenate([persist.T, vectors, pad], axis=1), w_query_mem.T)
+    tall = line_gather(jnp.concatenate([w_key_mem, w_value_mem], axis=1), 7)
     persistent = small[:, :slots].T
     gains = small[:, slots : slots + 4].astype(F32).T
     g_attn, g_mem, g_ffn, rate_w = (gains[i][None, :] for i in range(4))
@@ -309,8 +403,10 @@
         )
         return t_dot(send_m, back).astype(BF)
 
-    dealt = dot(deal_m, exchange(tokens)).astype(BF)
-    dealt, later, late_in, late_mem_out = together(dealt, cotangent, mem_in, mem_out)
+    arrived, tall = together(exchange(tokens), tall)
+    dealt, later, late_in, late_mem_out = together(
+        dot(deal_m, arrived).astype(BF), cotangent, mem_in, mem_out
+    )
     w_in, w_out_t = gather(late_in, late_mem_out.T)
     cotangent_arrived = exchange(later)
     x = dealt.astype(F32)
@@ -340,19 +436,20 @@
     n1 = (x * r1 * g_attn).astype(BF)
     n1_own = own(n1)
     query_mem = chain_sum(dot_t(n1_own, wqm_t))
-    columns = jnp.concatenate([w_key_mem, w_value_mem], axis=1)
-    query_mem, cotangent_arrived, columns = together(query_mem, cotangent_arrived, columns)
-    tall = lax.all_gather(columns, "tensor", axis=0, tiled=True)
+    query_mem, cotangent_arrived, late_query, late_key, late_value, late_output = together(
+        query_mem, cotangent_arrived, w_query, w_key, w_value, w_output
+    )
+    w_attn = gather_whole(late_query, late_key, late_value, late_output.T)
     d_out_low = dot(deal_m, cotangent_arrived).astype(BF)
+    read_s, read_act, read_slope = silu_parts(dot(query_mem, w_in))
+    read_low, tall = together(read_act.astype(BF), tall)
+    wkm_t, wvm_t = gather(tall[:, :shard].T, tall[:, shard:].T)
+    memory = chain_sum(dot_t(read_low, w_out_t))
+    memory, w_attn = together(memory, w_attn)
+    wq, wk, wv, wo_t = cut_apart(w_attn, inner, inner, inner, inner)
     query = dot(n1, wq).astype(BF)
     key_p, value_p = dot(persistent, wk).astype(BF), dot(persistent, wv).astype(BF)
     key_x, value_x = dot(n1, wk).astype(BF), dot(n1, wv).astype(BF)
-    w_in, query, key_p, value_p, key_x, value_x = together(w_in, query, key_p, value_p, key_x, value_x)
-    read_s, read_act, read_slope = silu_parts(dot(query_mem, w_in))
-    read_low = read_act.astype(BF)
-    memory = chain_sum(dot_t(read_low, w_out_t))
-    memory, tall = together(memory, tall)
-    wkm_t, wvm_t = gather(tall[:, :shard].T, tall[:, shard:].T)
 
     key_m, value_m = dot(memory, wk).astype(BF), dot(memory, wv).astype(BF)
 
@@ -521,11 +618,7 @@
     d_x = d_after_attn + rms_back(x, r1, g_attn, d_n1)
 
     def cut(share, *widths):
-        out, low = [], 0
-        for part in widths:
-            out.append(share[:, low : low + part].astype(F32))
-            low += part
-        return out
+        return [part.astype(F32) for part in cut_apart(share, *widths)]
 
     s_down, s_gate, s_up = cut(share_ffn, *[w_gate.shape[1]] * 3)
     s_key_mem, s_value_mem, s_output, s_query, s_key, s_value = cut(share_attn, *[inner] * 6)

time: 978 us -> 879 us (0.90)
  Pallas kernels: 559 us -> 482 us
  waiting for transfers between devices: 73.5 us -> 44.4 us
  matrix products: 167 us -> 179 us
    pallas_call x11, Pallas kernels: 559 us -> 454 us  [chain_sum(): pl.pallas_call(functools.partial(chain_sum_kernel, pieces, layout), out_s...]
    pallas_call x0 -> x1, Pallas kernels: none -> 27.7 us  [line_gather(): pl.pallas_call(functools.partial(line_gather_kernel, pieces), out_shape=j...]
    all_to_all x2, waiting for transfers between devices: 24.9 us -> 0.01 us  [exchange(): lax.all_to_all(dot(send_m, v).astype(BF), 'dp', split_axis=0, concat_axis...]
    all_gather x5, waiting for transfers between devices: 26.9 us -> 15.4 us  [gather_whole(): lax.all_gather(jnp.concatenate(parts, axis=1), 'dp', axis=0, tiled=True)]
    unnamed x265 -> x250, local copies, waits for them, and re-layouts: 28.3 us -> 29.3 us
  transfers between devices with their start and end apart: 14 -> 14, of which waited for: 3 -> 3; matrix products, arithmetic and copies ran while one was open for 26% -> 30% of each run, Pallas kernels for 58% -> 56%
where the time goes in v3:
time: 879 us; the launch traced here: 868 us
  Pallas kernels  482 us (55%)
  matrix products  179 us (20%)
  local copies, waits for them, and re-layouts  74.3 us (8%)
  other arithmetic  54.3 us (6%)
  waiting for transfers between devices  44.4 us (5%)
  starting transfers between devices  17.7 us (2%)
  between operations  16.4 us (2%)
    pallas_call x11, Pallas kernels, chain_sum(): pl.pallas_call(functools.partial(chain_sum_kernel, pieces, layout), out_s...  454 us
    dot_general x24, matrix products, dot(): lax.dot_general(left, right, (((1,), (0,)), ((), ())), preferred_element_...  84.9 us
    dot_general x20, matrix products, dot_t(): lax.dot_general(left, right, (((1,), (1,)), ((), ())), preferred_element_...  61 us
    unnamed x250, local copies, waits for them, and re-layouts  29.3 us
    all_to_all x1, waiting for transfers between devices, per_device(): lax.all_to_all(jnp.concatenate([turned, rest], axis=1), 'dp', split_axis=...  27.8 us
    pallas_call x1, Pallas kernels, line_gather(): pl.pallas_call(functools.partial(line_gather_kernel, pieces), out_shape=j...  27.7 us
  transfers between devices with their start and end apart: 14, of which 3 were waited for; matrix products, arithmetic and copies ran while one was open for 30% of the time, Pallas kernels for 56%

profile of v3, /device:TPU:0, one launch (start us, length us, event | category | flops | bytes accessed | tf_op | source)
XLA Modules:
  0.0 867.8 jit_solution(2023123763733959200)
XLA Ops:
  16.5 5.3 all-to-all-start
  23.0 27.7 %line_gather.1 = bf16[1536,384]{1,0:T(8,128)(2,1)} custom-call(bf16[384,384]{1,0:T(8,128)(2,1)} %pad_maximum_fusion.12.x_ref), custom_call_target="tpu_custom_call" | custom-call | bytes 50000000 | tf_op jit(solution)/shard_map/line_gather/pallas_call | solution.py:283
  65.6 38.0 %chain_sum.11.refs_2_ = bf16[384,1536]{1,0:T(8,128)(2,1)} custom-call(bf16[384,1536]{1,0:T(8,128)(2,1)} %convolution_convert_fusion.8.x_ref), custom_call_target="tpu_custom_call" | custom-call | bytes 100000000 | tf_op jit(solution)/shard_map/chain_sum/pallas_call | solution.py:187
  106.2 15.4 %all-gather.9.cloned.1.call-done = bf16[1536,3072]{1,0:T(8,128)(2,1)} async-done(((bf16[192,3072]{1,0:T(8,128)(2,1)}), bf16[1536,3072]{1,0:T(8,128)(2,1)}) %all-gather.9.cloned.1.call-update) | async-done | bytes 9437200 | tf_op jit(solution)/shard_map/all_gather | solution.py:374
  121.6 6.6 multiply_convert_fusion.4
  138.2 5.5 convolution_convert_fusion.x_ref
  143.7 39.1 %chain_sum.12.refs_10_.refs_16_ = bf16[384,1536]{1,0:T(8,128)(2,1)} custom-call(bf16[384,1536]{1,0:T(8,128)(2,1)} %convolution_convert_fusion.x_ref), custom_call_target="tpu_custom_call" | custom-call | bytes 100000000 | tf_op jit(solution)/shard_map/chain_sum/pallas_call | solution.py:187
  228.1 36.8 %chain_sum.13 = bf16[384,1536]{1,0:T(8,128)(2,1)} custom-call(bf16[384,1536]{1,0:T(8,128)(2,1)} %convolution_convert_fusion.5.x_ref), custom_call_target="tpu_custom_call" | custom-call | bytes 100000000 | tf_op jit(solution)/shard_map/chain_sum/pallas_call | solution.py:187
  274.7 6.3 multiply_convert_fusion.3
  286.5 44.3 %chain_sum.14 = bf16[384,1536]{1,0:T(8,128)(2,1)} custom-call(bf16[384,1536]{1,0:T(8,128)(2,1)} %fusion.32.x_ref), custom_call_target="tpu_custom_call" | custom-call | bytes 100000000 | tf_op jit(solution)/shard_map/chain_sum/pallas_call | solution.py:187
  332.9 6.0 multiply_convert_fusion.2
  345.8 35.8 %chain_sum.15 = bf16[384,1536]{1,0:T(8,128)(2,1)} custom-call(bf16[384,1536]{1,0:T(8,128)(2,1)} %fusion.38.x_ref), custom_call_target="tpu_custom_call" | custom-call | bytes 100000000 | tf_op jit(solution)/shard_map/chain_sum/pallas_call | solution.py:187
  411.1 51.9 %chain_sum.16 = (bf16[384,1536]{1,0:T(8,128)(2,1)}, bf16[1536,3072]{1,0:T(8,128)(2,1)}) custom-call(bf16[384,1536]{1,0:T(8,128)(2,1)} %fusion.28.x_ref, bf16[384,1536]{1,0:T(8,128)(2,1)} %convolution_convert_fusion.6.refs_0_, bf16[384,1024]{1,0:T(8,128)(2,1)} %copy-done.58, bf16[384,1536]{1,0:T(8,128)(2,1)} %multiply_convert_fusion.refs_2_.refs_4_, ...), custom_call_target="tpu_custom_call" | custom-call | bytes 100000000 | tf_op jit(solution)/shard_map/chain_sum/pallas_call | solution.py:187
  482.7 5.7 fusion.39.x_ref
  488.4 37.4 %chain_sum.17 = bf16[384,1536]{1,0:T(8,128)(2,1)} custom-call(bf16[384,1536]{1,0:T(8,128)(2,1)} %fusion.39.x_ref), custom_call_target="tpu_custom_call" | custom-call | bytes 100000000 | tf_op jit(solution)/shard_map/chain_sum/pallas_call | solution.py:187
  533.6 5.9 fusion.168
  539.6 5.7 fusion.40.refs_1_
  551.2 35.2 %chain_sum.18 = (bf16[384,1536]{1,0:T(8,128)(2,1)}, bf16[1536,1536]{1,0:T(8,128)(2,1)}) custom-call(bf16[384,1536]{1,0:T(8,128)(2,1)} %fusion.41.x_ref, bf16[384,1536]{1,0:T(8,128)(2,1)} %copy-done.14, bf16[384,1536]{1,0:T(8,128)(2,1)} %copy-done.10, bf16[384,1536]{1,0:T(8,128)(2,1)} %copy-done.8, bf16[384,1536]{1,0:T(8,128)(2,1)} %copy-done.29), custom_call_target="tpu_custom_call" | custom-call | bytes 100000000 | tf_op jit(solution)/shard_map/chain_sum/pallas_call | solution.py:187
  593.0 7.2 multiply_reduce_fusion.1
  642.6 49.8 %chain_sum.19 = (bf16[384,1536]{1,0:T(8,128)(2,1)}, bf16[1536,2304]{1,0:T(8,128)(2,1)}) custom-call(bf16[384,1536]{1,0:T(8,128)(2,1)} %fusion.33.x_ref, bf16[384,1536]{1,0:T(8,128)(2,1)} %get-tuple-element.77.refs_0_, bf16[384,384]{1,0:T(8,128)(2,1)} %constant_dynamic-slice_fusion.refs_1_.refs_3_, bf16[384,1536]{1,0:T(8,128)(2,1)} %copy-done.15, ...), custom_call_target="tpu_custom_call" | custom-call | bytes 100000000 | tf_op jit(solution)/shard_map/chain_sum/pallas_call | solution.py:187
  699.0 6.2 fusion.29.x_ref
  705.2 44.0 %chain_sum.20 = (bf16[384,1536]{1,0:T(8,128)(2,1)}, bf16[1536,3456]{1,0:T(8,128)(2,1)}) custom-call(bf16[384,1536]{1,0:T(8,128)(2,1)} %fusion.29.x_ref, bf16[384,1536]{1,0:T(8,128)(2,1)} %copy-done.16, bf16[384,1536]{1,0:T(8,128)(2,1)} %copy-done.54, bf16[384,1536]{1,0:T(8,128)(2,1)} %chain_sum.11.refs_2_, bf16[384,1536]{1,0:T(8,128)(2,1)} %copy-done.56, ...), custom_call_target="tpu_custom_call" | custom-call | bytes 100000000 | tf_op jit(solution)/shard_map/chain_sum/pallas_call | solution.py:187
  765.6 41.8 %chain_sum.21 = bf16[448,1536]{1,0:T(8,128)(2,1)} custom-call(bf16[448,1536]{1,0:T(8,128)(2,1)} %pad_maximum_fusion.2.x_ref), custom_call_target="tpu_custom_call" | custom-call | bytes 100000000 | tf_op jit(solution)/shard_map/chain_sum/pallas_call | solution.py:187
  822.4 27.8 %all-to-all-done.3 = bf16[8,64,1536]{2,1,0:T(8,128)(2,1)S(1)} async-done(((bf16[8,64,1536]{2,1,0:T(8,128)(2,1)}), bf16[8,64,1536]{2,1,0:T(8,128)(2,1)S(1)}, u32[]{:S(2)}, u32[]{:S(2)}) %all-to-all-start.3) | async-done | bytes 1572896 | tf_op jit(solution)/shard_map/all_to_all | solution.py:636
  (455 shorter events, 265.9 us)
Async XLA Ops:
  7.2 52.7 %all-gather.7.cloned.1.call-start = ((), (), s32[]{:S(2)}) async-start(), calls=%async_computation.8 | async-start | bytes 1769472 | tf_op jit(solution)/shard_map/all_gather | solution.py:374
  14.7 38.4 %copy-start.89 = (s32[384]{0:T(512)}, s32[384]{0:T(512)S(1)}, u32[]{:S(2)}) copy-start(s32[384]{0:T(512)S(1)} %multiply_add_fusion) | copy-start | bytes 4612
  16.5 34.3 %copy-start.103 = (s32[384]{0:T(512)S(1)}, s32[384]{0:T(512)}, u32[]{:S(2)}) copy-start(s32[384]{0:T(512)} %param.25) | copy-start | bytes 4612
  16.5 34.5 %all-to-all-start = ((bf16[8,48,1536]{2,1,0:T(8,128)(2,1)}), bf16[8,48,1536]{2,1,0:T(8,128)(2,1)S(1)}, u32[]{:S(2)}, u32[]{:S(2)}) async-start(bf16[8,48,1536]{2,1,0:T(8,128)(2,1)} %bitcast.2), calls=%async_computation | async-start | bytes 2359296 | tf_op jit(solution)/shard_map/all_to_all | solution.py:396
  21.8 99.7 %all-gather.9.cloned.1.call-start = ((), (), s32[]{:S(2)}) async-start(), calls=%async_computation.9 | async-start | bytes 10616832 | tf_op jit(solution)/shard_map/all_gather | solution.py:374
  22.0 29.8 %copy-start.60 = (bf16[1536,192]{0,1:T(8,128)(2,1)S(1)}, bf16[1536,192]{0,1:T(8,128)(2,1)}, u32[]{:S(2)}) copy-start(bf16[1536,192]{0,1:T(8,128)(2,1)} %param.31) | copy-start | bytes 1769476
  22.0 29.8 %copy-start.61 = (bf16[192,1536]{1,0:T(8,128)(2,1)S(1)}, bf16[192,1536]{1,0:T(8,128)(2,1)}, u32[]{:S(2)}) copy-start(bf16[192,1536]{1,0:T(8,128)(2,1)} %param.30) | copy-start | bytes 1769476
  55.3 48.3 %all-to-all-start.1 = ((bf16[8,48,1536]{2,1,0:T(8,128)(2,1)}), bf16[8,48,1536]{2,1,0:T(8,128)(2,1)S(1)}, u32[]{:S(2)}, u32[]{:S(2)}) async-start(bf16[8,48,1536]{2,1,0:T(8,128)(2,1)} %bitcast.5), calls=%async_computation.1 | async-start | bytes 2359296 | tf_op jit(solution)/shard_map/all_to_all | solution.py:396
  58.9 123.9 %all-gather.11.cloned.1.call-start = ((), (), s32[]{:S(2)}) async-start(), calls=%async_computation.10 | async-start | bytes 5308416 | tf_op jit(solution)/shard_map/all_gather | solution.py:374
  63.8 145.0 %copy-start.4 = (bf16[384,1536]{1,0:T(8,128)(2,1)}, bf16[384,1536]{1,0:T(8,128)(2,1)S(1)}, u32[]{:S(2)}) copy-start(bf16[384,1536]{1,0:T(8,128)(2,1)S(1)} %fusion.76.refs_6_.refs_12_.refs_18_) | copy-start | bytes 3538948
  106.1 162.6 %all-gather.13.cloned.1.call-start = ((), (), s32[]{:S(2)}) async-start(), calls=%async_computation.11 | async-start | bytes 10616832 | tf_op jit(solution)/shard_map/all_gather | solution.py:374
  132.6 253.7 %all-gather.15.cloned.1.call-start = ((), (), s32[]{:S(2)}) async-start(), calls=%async_computation.12 | async-start | bytes 10616832 | tf_op jit(solution)/shard_map/all_gather | solution.py:374
  223.0 326.3 %reduce-scatter.13.cloned.1.call-start = ((), (), s32[]{:S(2)}) async-start(), calls=%async_computation.17 | async-start | bytes 1474560
  228.1 39.3 %copy-start.85 = (f32[1536]{0:T(1024)S(1)}, f32[1536]{0:T(1024)}, u32[]{:S(2)}) copy-start(f32[1536]{0:T(1024)} %get-tuple-element.194) | copy-start | bytes 18436
  274.6 56.3 %copy-start.16 = (bf16[384,1536]{1,0:T(8,128)(2,1)}, bf16[384,1536]{1,0:T(8,128)(2,1)S(1)}, u32[]{:S(2)}) copy-start(bf16[384,1536]{1,0:T(8,128)(2,1)S(1)} %fusion.34.refs_0_) | copy-start | bytes 3538948
  281.0 60.7 %copy-start.30 = (bf16[384,1536]{1,0:T(8,128)(2,1)}, bf16[384,1536]{1,0:T(8,128)(2,1)S(1)}, u32[]{:S(2)}) copy-start(bf16[384,1536]{1,0:T(8,128)(2,1)S(1)} %get-tuple-element.240.refs_5_) | copy-start | bytes 3538948
  402.8 224.9 %reduce-scatter.7.cloned.1.call-start = ((), (), s32[]{:S(2)}) async-start(), calls=%async_computation.13 | async-start | bytes 10616832 | tf_op jit(solution)/shard_map/reduce_scatter | solution.py:535
  588.6 37.1 %all-to-all-start.2 = ((bf16[8,48,384]{2,1,0:T(8,128)(2,1)}), bf16[8,48,384]{2,1,0:T(8,128)(2,1)}, u32[]{:S(2)}, u32[]{:S(2)}) async-start(bf16[8,48,384]{2,1,0:T(8,128)(2,1)} %bitcast.187), calls=%async_computation.3 | async-start | bytes 589824 | tf_op jit(solution)/shard_map/all_to_all | solution.py:401
  592.7 171.7 %all-gather.17.cloned.1.call-start = ((), (), s32[]{:S(2)}) async-start(), calls=%async_computation.15 | async-start | bytes 1474560 | tf_op jit(solution)/shard_map/all_gather | solution.py:582
  627.8 136.7 %reduce-scatter.9.cloned.1.call-start = ((), (), s32[]{:S(2)}) async-start(), calls=%async_computation.14 | async-start | bytes 7962624 | tf_op jit(solution)/shard_map/reduce_scatter | solution.py:598
  692.4 162.4 %reduce-scatter.11.cloned.1.call-start = ((), (), s32[]{:S(2)}) async-start(), calls=%async_computation.16 | async-start | bytes 11943936 | tf_op jit(solution)/shard_map/reduce_scatter | solution.py:611
  764.4 43.1 %copy-start.79 = (f32[1536]{0:T(1024)S(1)}, f32[1536]{0:T(1024)}, u32[]{:S(2)}) copy-start(f32[1536]{0:T(1024)} %copy-done.78) | copy-start | bytes 18436
  764.4 43.1 %copy-start.96 = (f32[384]{0:T(512)S(1)}, f32[384]{0:T(512)}, u32[]{:S(2)}) copy-start(f32[384]{0:T(512)} %get-tuple-element.231) | copy-start | bytes 4612
  815.2 34.9 %all-to-all-start.3 = ((bf16[8,64,1536]{2,1,0:T(8,128)(2,1)}), bf16[8,64,1536]{2,1,0:T(8,128)(2,1)S(1)}, u32[]{:S(2)}, u32[]{:S(2)}) async-start(bf16[8,64,1536]{2,1,0:T(8,128)(2,1)} %pad_maximum_fusion.1), calls=%async_computation.5 | async-start | bytes 3145728 | tf_op jit(solution)/shard_map/all_to_all | solution.py:636
  (112 other events, 456.8 us)
Sparse Core Ops, SparseCore 0:
  13.1 33.2 all-gather.6
  53.2 68.3 all-gather.8
  124.0 38.7 all-gather.10
  165.1 58.8 all-gather.12
  226.3 58.6 all-gather.14
  402.9 43.4 reduce-scatter.12
  466.2 76.9 reduce-scatter.6
  627.9 34.2 all-gather.16
  692.6 66.5 reduce-scatter.8
  762.5 92.3 reduce-scatter.10

commit v4 on v3

--- a/solution.py
+++ b/solution.py
@@ -15,6 +15,7 @@
 F32 = jnp.float32
 MESH = pl.DeviceIdType.MESH
 TILE = 128
+GRANT = 1 << 20
 
 
 def chain_sum_kernel(pieces, layout, x_ref, *refs):
@@ -127,7 +128,7 @@
 
     tiles = g_ref.shape[0] // TILE if layout else 0
 
-    per, lag = (2, 2) if layout else (1, 3)
+    per, lag = 2, 2
     turns = pieces // per
 
     @pl.loop(0, max(turns + lag, tiles))
@@ -179,18 +180,22 @@
     out_shape = [jax.ShapeDtypeStruct((rows, cols), BF)]
     out_specs = [vmem]
     scratch = [pltpu.VMEM((rows, cols), BF)] * 3 + [dma((pieces,))] * 5
+    grant = 3 * rows * cols * 2 + GRANT
     if products:
         width, high = sum(w for w, _ in layout), products[0][0][0].shape[1]
         out_shape.append(jax.ShapeDtypeStruct((high, width + room), BF))
         out_specs.append(pl.BlockSpec(memory_space=pl.ANY))
         scratch += [pltpu.VMEM((2, TILE, width), BF), dma((2,))]
+        grant += 2 * TILE * width * 2 + 4 * GRANT
     out = pl.pallas_call(
         functools.partial(chain_sum_kernel, pieces, layout),
         out_shape=out_shape,
         in_specs=[vmem] * (1 + len(fills)),
         out_specs=out_specs,
         scratch_shapes=scratch,
-        compiler_params=pltpu.CompilerParams(collective_id=call_id, has_side_effects=True),
+        compiler_params=pltpu.CompilerParams(
+            collective_id=call_id, has_side_effects=True, vmem_limit_bytes=grant
+        ),
         cost_estimate=pl.CostEstimate(flops=0, bytes_accessed=10**8, transcendentals=0),
         name="chain_sum",
     )(x.astype(BF), *fills)
@@ -286,7 +291,9 @@
         in_specs=[vmem],
         out_specs=vmem,
         scratch_shapes=[dma((2, 3, pieces)), dma((2, 3, pieces)), dma((1,))],
-        compiler_params=pltpu.CompilerParams(collective_id=call_id, has_side_effects=True),
+        compiler_params=pltpu.CompilerParams(
+            collective_id=call_id, has_side_effects=True, vmem_limit_bytes=GRANT
+        ),
         cost_estimate=pl.CostEstimate(flops=0, bytes_accessed=5 * 10**7, transcendentals=0),
         name="line_gather",
     )(x)
@@ -393,9 +400,7 @@
     deal_m = (came_at[:, None] == place[None, :]).astype(BF)
 
     def exchange(v):
-        return lax.all_to_all(
-            dot(send_m, v).astype(BF), "dp", split_axis=0, concat_axis=0, tiled=True
-        )
+        return lax.all_to_all(v, "dp", split_axis=0, concat_axis=0, tiled=True)
 
     def give_back(v):
         back = lax.all_to_all(
@@ -403,16 +408,17 @@
         )
         return t_dot(send_m, back).astype(BF)
 
-    arrived, tall = together(exchange(tokens), tall)
-    dealt, later, late_in, late_mem_out = together(
-        dot(deal_m, arrived).astype(BF), cotangent, mem_in, mem_out
-    )
+    leaving, late_in, late_mem_out = together(dot(send_m, tokens).astype(BF), mem_in, mem_out)
     w_in, w_out_t = gather(late_in, late_mem_out.T)
-    cotangent_arrived = exchange(later)
+    arrived, tall = together(exchange(leaving), tall)
+    dealt = dot(deal_m, arrived).astype(BF)
     x = dealt.astype(F32)
 
     position = jnp.arange(rows, dtype=jnp.int32)
-    bounds = jnp.cumsum(lengths, axis=1)
+    turn = jnp.arange(lengths.shape[1])
+    bounds = jnp.sum(
+        jnp.where(turn[:, None] <= turn[None, :], lengths[:, :, None], 0), axis=1, dtype=jnp.int32
+    )
     segment = jnp.sum((position[None, :, None] >= bounds[:, None, :]).astype(jnp.int32), axis=2)
     causal = (segment[:, :, None] == segment[:, None, :]) & (
         position[None, None, :] <= position[None, :, None]
@@ -436,11 +442,10 @@
     n1 = (x * r1 * g_attn).astype(BF)
     n1_own = own(n1)
     query_mem = chain_sum(dot_t(n1_own, wqm_t))
-    query_mem, cotangent_arrived, late_query, late_key, late_value, late_output = together(
-        query_mem, cotangent_arrived, w_query, w_key, w_value, w_output
+    query_mem, late_query, late_key, late_value, late_output = together(
+        query_mem, w_query, w_key, w_value, w_output
     )
     w_attn = gather_whole(late_query, late_key, late_value, late_output.T)
-    d_out_low = dot(deal_m, cotangent_arrived).astype(BF)
     read_s, read_act, read_slope = silu_parts(dot(query_mem, w_in))
     read_low, tall = together(read_act.astype(BF), tall)
     wkm_t, wvm_t = gather(tall[:, :shard].T, tall[:, shard:].T)
@@ -467,9 +472,12 @@
     weights = jax.nn.softmax(jnp.where(allowed, scores, NEG_LARGE), axis=-1)
     weights_low = weights.astype(BF)
     mixed = batch_dot("bhqk,bkhd->bqhd", weights_low, values).astype(BF).reshape(count, inner)
-    mixed, late_gate, late_up, late_down = together(mixed, w_gate, w_up, w_down)
+    mixed, late_gate, late_up, late_down, later = together(mixed, w_gate, w_up, w_down, cotangent)
+    cotangent_arrived = exchange(dot(send_m, later).astype(BF))
     wg, wu, wd_t = gather(late_gate, late_up, late_down.T)
-    after_attn = x + chain_sum(dot_t(mixed, wo_t)).astype(F32)
+    attended, cotangent_arrived = together(chain_sum(dot_t(mixed, wo_t)), cotangent_arrived)
+    after_attn = x + attended.astype(F32)
+    d_out_low = dot(deal_m, cotangent_arrived).astype(BF)
 
     r2 = rms(after_attn)
     n2 = after_attn * r2 * g_mem
@@ -535,14 +543,14 @@
     share_ffn = lax.psum_scatter(gw_ffn, "dp", scatter_dimension=0, tiled=True)
     d_error = chain_sum(d_error_part).astype(F32)
     d_rate = jnp.sum(d_error * miss, axis=1, keepdims=True)
-    d_miss = (rate * d_error).astype(BF)
+    late_rate, ffn_own = together(rate, ffn_own)
+    d_miss = (late_rate * d_error).astype(BF)
     d_key_act = d_key_act + dot(d_miss, w_out_t)
     d_key_hidden = (d_hidden_part + d_key_act * key_slope).astype(BF)
     d_key_part = dot_t(d_key_hidden, w_in) + join(
         batch_dot("bij,bjk->bik", d_gram, split(key_mem))
         + batch_dot("bij,bik->bjk", d_gram, split(key_mem))
     )
-    d_key_part, ffn_own = together(d_key_part.astype(BF), ffn_own)
     result_own = give_back(own(after_mem) + ffn_own.astype(F32))
     d_key, gw_out_early = chain_sum(
         d_key_part, 6, [[(d_update, new_act), (error, d_back_pre)]]
@@ -552,7 +560,9 @@
     gg_rate = jnp.sum(n2 * d_logit, axis=0)
     d_n2 = d_n2 + d_logit * rate_w
     gg_mem = jnp.sum(d_n2 * after_attn * r2, axis=0)
-    d_after_attn = d_after_mem + rms_back(after_attn, r2, g_mem, d_n2)
+    late_r2, share_ffn, result_own = together(r2, share_ffn, result_own)
+    output = lax.all_gather(result_own, "tensor", axis=1, tiled=True)
+    d_after_attn = d_after_mem + rms_back(after_attn, late_r2, g_mem, d_n2)
     d_attn = d_after_attn.astype(BF)
 
     d_mixed = dot(d_attn, wo_t).astype(BF)
@@ -576,12 +586,8 @@
 
     dk_p, dk_m, dk_x = apart(d_keys)
     dv_p, dv_m, dv_x = apart(d_values)
-    d_memory_part, share_ffn, result_own = together(
-        (dot_t(dk_m, wk) + dot_t(dv_m, wv)).astype(BF), share_ffn, result_own
-    )
-    output = lax.all_gather(result_own, "tensor", axis=1, tiled=True)
     d_memory, gw_attn = chain_sum(
-        d_memory_part,
+        dot_t(dk_m, wk) + dot_t(dv_m, wv),
         3,
         [
             [(d_key, n2_own)],
@@ -610,8 +616,8 @@
     gw_mem = lax.dynamic_update_slice(gw_mem, gw_query_mem, (0, 2 * hidden))
     share_mem = lax.psum_scatter(gw_mem, "dp", scatter_dimension=0, tiled=True)
     d_n1_part = d_n1_part + in_own(dot(d_query_mem, wqm_t))
-    d_n1_part, share_attn, output = together(d_n1_part.astype(BF), share_attn, output)
-    last = chain_sum(jnp.concatenate([d_n1_part, d_persist_part.astype(BF)], axis=0), 5)
+    d_persist_part, share_attn, output = together(d_persist_part.astype(BF), share_attn, output)
+    last = chain_sum(jnp.concatenate([d_n1_part.astype(BF), d_persist_part], axis=0), 5)
     d_n1 = last[:count].astype(F32)
     g_persist = last[count:]
     gg_attn = jnp.sum(d_n1 * x * r1, axis=0)

time: 879 us -> 859 us (0.977)
  Pallas kernels: 482 us -> 463 us
  matrix products: 179 us -> 163 us
  waiting for transfers between devices: 44.4 us -> 58.4 us
    reduce_scatter x1, waiting for transfers between devices: 0.97 us -> 19.3 us  [per_device(): share_mem = lax.psum_scatter(gw_mem, 'dp', scatter_dimension=0, tiled=True)]
    pallas_call x11, Pallas kernels: 454 us -> 437 us  [chain_sum(): pl.pallas_call(functools.partial(chain_sum_kernel, pieces, layout), out_s...]
    unnamed x250 -> x306, local copies, waits for them, and re-layouts: 29.3 us -> 45.6 us
  transfers between devices with their start and end apart: 14 -> 14, of which waited for: 3 -> 4; matrix products, arithmetic and copies ran while one was open for 30% -> 25% of each run, Pallas kernels for 56% -> 54%
where the time goes in v4:
time: 859 us; the launch traced here: 850 us
  Pallas kernels  463 us (54%)
  matrix products  163 us (19%)
  local copies, waits for them, and re-layouts  80.9 us (9%)
  waiting for transfers between devices  58.4 us (7%)
  other arithmetic  47.2 us (5%)
  starting transfers between devices  21 us (2%)
  between operations  16.9 us (2%)
    pallas_call x11, Pallas kernels, chain_sum(): pl.pallas_call(functools.partial(chain_sum_kernel, pieces, layout), out_s...  437 us
    dot_general x24, matrix products, dot(): lax.dot_general(left, right, (((1,), (0,)), ((), ())), preferred_element_...  79.2 us
    dot_general x20, matrix products, dot_t(): lax.dot_general(left, right, (((1,), (1,)), ((), ())), preferred_element_...  52.7 us
    unnamed x306, local copies, waits for them, and re-layouts  45.6 us
    pallas_call x1, Pallas kernels, line_gather(): pl.pallas_call(functools.partial(line_gather_kernel, pieces), out_shape=j...  25.8 us
    all_to_all x1, waiting for transfers between devices, per_device(): lax.all_to_all(jnp.concatenate([turned, rest], axis=1), 'dp', split_axis=...  23.6 us
    reduce_scatter x1, waiting for transfers between devices, per_device(): share_mem = lax.psum_scatter(gw_mem, 'dp', scatter_dimension=0, tiled=True)  19.3 us
  transfers between devices with their start and end apart: 14, of which 4 were waited for; matrix products, arithmetic and copies ran while one was open for 25% of the time, Pallas kernels for 54%

profile of v4, /device:TPU:0, one launch (start us, length us, event | category | flops | bytes accessed | tf_op | source)
XLA Modules:
  0.0 850.3 jit_solution(16339400553166080277)
XLA Ops:
  18.4 5.3 all-to-all-start
  24.2 25.8 %line_gather.1 = bf16[1536,384]{1,0:T(8,128)(2,1)S(1)} custom-call(bf16[384,384]{1,0:T(8,128)(2,1)S(1)} %pad_maximum_fusion.12.x_ref), custom_call_target="tpu_custom_call" | custom-call | bytes 50000000 | tf_op jit(solution)/shard_map/line_gather/pallas_call | solution.py:288
  58.3 35.2 %chain_sum.11.refs_2_ = bf16[384,1536]{1,0:T(8,128)(2,1)S(1)} custom-call(bf16[384,1536]{1,0:T(8,128)(2,1)S(1)} %convolution_convert_fusion.8.x_ref), custom_call_target="tpu_custom_call" | custom-call | bytes 100000000 | tf_op jit(solution)/shard_map/chain_sum/pallas_call | solution.py:190
  94.7 13.2 %all-gather.9.cloned.1.call-done = bf16[1536,3072]{1,0:T(8,128)(2,1)} async-done(((bf16[192,3072]{1,0:T(8,128)(2,1)}), bf16[1536,3072]{1,0:T(8,128)(2,1)}) %all-gather.9.cloned.1.call-update) | async-done | bytes 9437200 | tf_op jit(solution)/shard_map/all_gather | solution.py:381
  107.9 6.3 multiply_convert_fusion.4
  125.5 38.7 %chain_sum.12.refs_10_.refs_16_ = bf16[384,1536]{1,0:T(8,128)(2,1)S(1)} custom-call(bf16[384,1536]{1,0:T(8,128)(2,1)S(1)} %convolution_convert_fusion.x_ref), custom_call_target="tpu_custom_call" | custom-call | bytes 100000000 | tf_op jit(solution)/shard_map/chain_sum/pallas_call | solution.py:190
  203.7 37.1 %chain_sum.13 = bf16[384,1536]{1,0:T(8,128)(2,1)S(1)} custom-call(bf16[384,1536]{1,0:T(8,128)(2,1)S(1)} %convolution_convert_fusion.7.x_ref), custom_call_target="tpu_custom_call" | custom-call | bytes 100000000 | tf_op jit(solution)/shard_map/chain_sum/pallas_call | solution.py:190
  253.6 5.0 multiply_convert_fusion.3
  264.1 36.7 %chain_sum.14 = bf16[384,1536]{1,0:T(8,128)(2,1)S(1)} custom-call(bf16[384,1536]{1,0:T(8,128)(2,1)S(1)} %fusion.32.x_ref), custom_call_target="tpu_custom_call" | custom-call | bytes 100000000 | tf_op jit(solution)/shard_map/chain_sum/pallas_call | solution.py:190
  311.3 35.3 %chain_sum.15 = bf16[384,1536]{1,0:T(8,128)(2,1)S(1)} custom-call(bf16[384,1536]{1,0:T(8,128)(2,1)S(1)} %fusion.38.x_ref), custom_call_target="tpu_custom_call" | custom-call | bytes 100000000 | tf_op jit(solution)/shard_map/chain_sum/pallas_call | solution.py:190
  373.4 53.8 %chain_sum.16 = (bf16[384,1536]{1,0:T(8,128)(2,1)S(1)}, bf16[1536,3072]{1,0:T(8,128)(2,1)S(1)}) custom-call(bf16[384,1536]{1,0:T(8,128)(2,1)S(1)} %fusion.28.x_ref, bf16[384,1536]{1,0:T(8,128)(2,1)S(1)} %convolution_convert_fusion.5.refs_0_, bf16[384,1024]{1,0:T(8,128)(2,1)S(1)} %copy-done.51, bf16[384,1536]{1,0:T(8,128)(2,1)S(1)} %copy-done.5, ...), custom_call_target="tpu_custom_call" | custom-call | bytes 100000000 | tf_op jit(solution)/shard_map/chain_sum/pallas_call | solution.py:190
  448.4 5.6 fusion.37
  463.1 33.9 %chain_sum.17 = bf16[384,1536]{1,0:T(8,128)(2,1)S(1)} custom-call(bf16[384,1536]{1,0:T(8,128)(2,1)S(1)} %fusion.39.x_ref), custom_call_target="tpu_custom_call" | custom-call | bytes 100000000 | tf_op jit(solution)/shard_map/chain_sum/pallas_call | solution.py:190
  507.1 6.9 all-to-all-start.2
  518.2 7.0 fusion.40.refs_1_
  530.2 36.9 %chain_sum.18 = (bf16[384,1536]{1,0:T(8,128)(2,1)S(1)}, bf16[1536,1536]{1,0:T(8,128)(2,1)S(1)}) custom-call(bf16[384,1536]{1,0:T(8,128)(2,1)S(1)} %fusion.41.x_ref, bf16[384,1536]{1,0:T(8,128)(2,1)S(1)} %copy-done.16, bf16[384,1536]{1,0:T(8,128)(2,1)S(1)} %copy-done.11, bf16[384,1536]{1,0:T(8,128)(2,1)S(1)} %copy-done.8, bf16[384,1536]{1,0:T(8,128)(2,1)S(1)} %copy-done.30), custom_call_target="tpu_custom_call" | custom-call | bytes 100000000 | tf_op jit(solution)/shard_map/chain_sum/pallas_call | solution.py:190
  582.3 5.0 fusion.172
  613.4 51.6 %chain_sum.19 = (bf16[384,1536]{1,0:T(8,128)(2,1)S(1)}, bf16[1536,2304]{1,0:T(8,128)(2,1)S(1)}) custom-call(bf16[384,1536]{1,0:T(8,128)(2,1)S(1)} %fusion.33.x_ref, bf16[384,1536]{1,0:T(8,128)(2,1)S(1)} %copy-done.41, bf16[384,384]{1,0:T(8,128)(2,1)S(1)} %copy-done.36, bf16[384,1536]{1,0:T(8,128)(2,1)S(1)} %copy-done.18, bf16[384,384]{1,0:T(8,128)(2,1)S(1)} %copy-done.36, ...), custom_call_target="tpu_custom_call" | custom-call | bytes 100000000 | tf_op jit(solution)/shard_map/chain_sum/pallas_call | solution.py:190
  668.9 5.7 fusion.45.refs_3_
  674.7 4.9 fusion.29.x_ref
  683.7 36.4 %chain_sum.20 = (bf16[384,1536]{1,0:T(8,128)(2,1)S(1)}, bf16[1536,3456]{1,0:T(8,128)(2,1)}) custom-call(bf16[384,1536]{1,0:T(8,128)(2,1)S(1)} %fusion.29.x_ref, bf16[384,1536]{1,0:T(8,128)(2,1)S(1)} %copy-done.21, bf16[384,1536]{1,0:T(8,128)(2,1)S(1)} %copy-done.47, bf16[384,1536]{1,0:T(8,128)(2,1)S(1)} %copy-done.35, bf16[384,1536]{1,0:T(8,128)(2,1)S(1)} %fusion.45.refs_3_, ...), custom_call_target="tpu_custom_call" | custom-call | bytes 100000000 | tf_op jit(solution)/shard_map/chain_sum/pallas_call | solution.py:190
  735.6 41.6 %chain_sum.21 = bf16[448,1536]{1,0:T(8,128)(2,1)S(1)} custom-call(bf16[448,1536]{1,0:T(8,128)(2,1)S(1)} %pad_maximum_fusion.2.x_ref), custom_call_target="tpu_custom_call" | custom-call | bytes 100000000 | tf_op jit(solution)/shard_map/chain_sum/pallas_call | solution.py:190
  790.7 23.6 %all-to-all-done.3 = bf16[8,64,1536]{2,1,0:T(8,128)(2,1)S(1)} async-done(((bf16[8,64,1536]{2,1,0:T(8,128)(2,1)}), bf16[8,64,1536]{2,1,0:T(8,128)(2,1)S(1)}, u32[]{:S(2)}, u32[]{:S(2)}) %all-to-all-start.3) | async-done | bytes 1572896 | tf_op jit(solution)/shard_map/all_to_all | solution.py:642
  818.1 19.3 %reduce-scatter.11.cloned.1.call-done = bf16[192,3456]{1,0:T(8,128)(2,1)} async-done(((bf16[1536,3456]{1,0:T(8,128)(2,1)}), bf16[192,3456]{1,0:T(8,128)(2,1)}) %reduce-scatter.11.cloned.1.call-update) | async-done | bytes 1327120 | tf_op jit(solution)/shard_map/reduce_scatter | solution.py:617
  (515 shorter events, 262.6 us)
Async XLA Ops:
  7.2 47.0 %all-gather.7.cloned.1.call-start = ((), (), s32[]{:S(2)}) async-start(), calls=%async_computation.8 | async-start | bytes 1769472 | tf_op jit(solution)/shard_map/all_gather | solution.py:381
  13.1 94.7 %all-gather.9.cloned.1.call-start = ((), (), s32[]{:S(2)}) async-start(), calls=%async_computation.9 | async-start | bytes 10616832 | tf_op jit(solution)/shard_map/all_gather | solution.py:381
  18.4 31.9 %all-to-all-start = ((bf16[8,48,1536]{2,1,0:T(8,128)(2,1)}), bf16[8,48,1536]{2,1,0:T(8,128)(2,1)S(1)}, u32[]{:S(2)}, u32[]{:S(2)}) async-start(bf16[8,48,1536]{2,1,0:T(8,128)(2,1)} %bitcast), calls=%async_computation | async-start | bytes 2359296 | tf_op jit(solution)/shard_map/all_to_all | solution.py:403
  23.7 140.5 %all-gather.11.cloned.1.call-start = ((), (), s32[]{:S(2)}) async-start(), calls=%async_computation.10 | async-start | bytes 5308416 | tf_op jit(solution)/shard_map/all_gather | solution.py:381
  94.6 151.8 %all-gather.13.cloned.1.call-start = ((), (), s32[]{:S(2)}) async-start(), calls=%async_computation.11 | async-start | bytes 10616832 | tf_op jit(solution)/shard_map/all_gather | solution.py:381
  118.6 231.5 %all-gather.15.cloned.1.call-start = ((), (), s32[]{:S(2)}) async-start(), calls=%async_computation.12 | async-start | bytes 10616832 | tf_op jit(solution)/shard_map/all_gather | solution.py:381
  197.2 43.6 %all-to-all-start.1 = ((bf16[8,48,1536]{2,1,0:T(8,128)(2,1)}), bf16[8,48,1536]{2,1,0:T(8,128)(2,1)}, u32[]{:S(2)}, u32[]{:S(2)}) async-start(bf16[8,48,1536]{2,1,0:T(8,128)(2,1)} %bitcast.10), calls=%async_computation.1 | async-start | bytes 2359296 | tf_op jit(solution)/shard_map/all_to_all | solution.py:403
  201.4 301.4 %reduce-scatter.13.cloned.1.call-start = ((), (), s32[]{:S(2)}) async-start(), calls=%async_computation.17 | async-start | bytes 1474560
  253.6 47.2 %copy-start.19 = (bf16[384,1536]{1,0:T(8,128)(2,1)}, bf16[384,1536]{1,0:T(8,128)(2,1)S(1)}, u32[]{:S(2)}) copy-start(bf16[384,1536]{1,0:T(8,128)(2,1)S(1)} %fusion.34.refs_0_) | copy-start | bytes 3538948
  258.6 47.3 %copy-start.67 = (f32[384,1536]{1,0:T(8,128)}, f32[384,1536]{1,0:T(8,128)S(1)}, u32[]{:S(2)}) copy-start(f32[384,1536]{1,0:T(8,128)S(1)} %get-tuple-element.245) | copy-start | bytes 7077892
  258.7 49.5 %copy-start.31 = (bf16[384,1536]{1,0:T(8,128)(2,1)}, bf16[384,1536]{1,0:T(8,128)(2,1)S(1)}, u32[]{:S(2)}) copy-start(bf16[384,1536]{1,0:T(8,128)(2,1)S(1)} %get-tuple-element.244.refs_5_) | copy-start | bytes 3538948
  366.2 215.5 %reduce-scatter.7.cloned.1.call-start = ((), (), s32[]{:S(2)}) async-start(), calls=%async_computation.13 | async-start | bytes 10616832 | tf_op jit(solution)/shard_map/reduce_scatter | solution.py:543
  454.1 42.9 %copy-start.83 = (bf16[384,1536]{1,0:T(8,128)(2,1)}, bf16[384,1536]{1,0:T(8,128)(2,1)S(1)}, u32[]{:S(2)}) copy-start(bf16[384,1536]{1,0:T(8,128)(2,1)S(1)} %fusion.37) | copy-start | bytes 3538948
  507.1 72.5 %all-to-all-start.2 = ((bf16[8,48,384]{2,1,0:T(8,128)(2,1)}), bf16[8,48,384]{2,1,0:T(8,128)(2,1)}, u32[]{:S(2)}, u32[]{:S(2)}) async-start(bf16[8,48,384]{2,1,0:T(8,128)(2,1)} %bitcast.190), calls=%async_computation.3 | async-start | bytes 589824 | tf_op jit(solution)/shard_map/all_to_all | solution.py:406
  514.0 219.4 %all-gather.17.cloned.1.call-start = ((), (), s32[]{:S(2)}) async-start(), calls=%async_computation.15 | async-start | bytes 1474560 | tf_op jit(solution)/shard_map/all_gather | solution.py:564
  517.8 51.4 %copy-start.17 = (bf16[384,1536]{1,0:T(8,128)(2,1)}, bf16[384,1536]{1,0:T(8,128)(2,1)S(1)}, u32[]{:S(2)}) copy-start(bf16[384,1536]{1,0:T(8,128)(2,1)S(1)} %get-tuple-element.222.refs_2_.refs_4_) | copy-start | bytes 3538948
  525.3 48.7 %slice-start.2 = ((s8[9437184]{0:T(1024)(128)(4,1)}), s8[1048576]{0:T(1024)(128)(4,1)S(1)}, s32[]{:S(2)}) async-start(s8[9437184]{0:T(1024)(128)(4,1)} %bitcast.173), calls=%async_computation.20 | async-start | bytes 2097152
  525.3 48.7 %slice-start.3 = ((s8[9437184]{0:T(1024)(128)(4,1)}), s8[4194304]{0:T(1024)(128)(4,1)S(1)}, s32[]{:S(2)}) async-start(s8[9437184]{0:T(1024)(128)(4,1)} %bitcast.173), calls=%async_computation.21 | async-start | bytes 8388608
  600.4 135.0 %reduce-scatter.9.cloned.1.call-start = ((), (), s32[]{:S(2)}) async-start(), calls=%async_computation.14 | async-start | bytes 7962624 | tf_op jit(solution)/shard_map/reduce_scatter | solution.py:604
  668.9 168.5 %reduce-scatter.11.cloned.1.call-start = ((), (), s32[]{:S(2)}) async-start(), calls=%async_computation.16 | async-start | bytes 11943936 | tf_op jit(solution)/shard_map/reduce_scatter | solution.py:617
  733.4 43.8 %copy-start.66 = (bf16[384,1536]{1,0:T(8,128)(2,1)S(1)}, bf16[384,1536]{1,0:T(8,128)(2,1)}, u32[]{:S(2)}) copy-start(bf16[384,1536]{1,0:T(8,128)(2,1)} %copy-done.62) | copy-start | bytes 3538948
  733.4 43.8 %copy-start.107 = (f32[1536]{0:T(1024)S(1)}, f32[1536]{0:T(1024)}, u32[]{:S(2)}) copy-start(f32[1536]{0:T(1024)} %copy-done.106) | copy-start | bytes 18436
  733.4 43.8 %copy-start.129 = (f32[384]{0:T(512)S(1)}, f32[384]{0:T(512)}, u32[]{:S(2)}) copy-start(f32[384]{0:T(512)} %get-tuple-element.235) | copy-start | bytes 4612
  783.5 30.8 %all-to-all-start.3 = ((bf16[8,64,1536]{2,1,0:T(8,128)(2,1)}), bf16[8,64,1536]{2,1,0:T(8,128)(2,1)S(1)}, u32[]{:S(2)}, u32[]{:S(2)}) async-start(bf16[8,64,1536]{2,1,0:T(8,128)(2,1)} %pad_maximum_fusion.1), calls=%async_computation.5 | async-start | bytes 3145728 | tf_op jit(solution)/shard_map/all_to_all | solution.py:642
  (140 other events, 978.9 us)
Sparse Core Ops, SparseCore 0:
  13.2 34.1 all-gather.6
  49.9 57.8 all-gather.8
  110.3 38.7 all-gather.10
  151.5 62.3 all-gather.12
  215.6 66.4 all-gather.14
  366.3 49.6 reduce-scatter.12
  432.0 79.5 reduce-scatter.6
  600.5 43.4 all-gather.16
  669.0 66.4 reduce-scatter.8
  738.8 98.4 reduce-scatter.10

commit v5 on v4

--- a/solution.py
+++ b/solution.py
@@ -202,11 +202,17 @@
     return out if products else out[0]
 
 
-def line_gather_kernel(pieces, x_ref, o_ref, sent, got, keep):
+def line_gather_kernel(pieces, side, x_ref, o_ref, sent, got, keep):
     me = lax.axis_index("tensor")
-    high = x_ref.shape[0]
+    high, wide = x_ref.shape
     step = high // pieces
     last = 3
+
+    def place(block, low, size):
+        if side:
+            return o_ref.at[pl.ds(low, size), pl.ds(pl.multiple_of(block * wide, wide), wide)]
+        return o_ref.at[pl.ds(pl.multiple_of(block * high + low, size), size)]
+
     barrier = pltpu.get_barrier_semaphore()
     ways = ((0, me < last, 1), (1, me > 0, -1))
 
@@ -229,10 +235,10 @@
         pl.semaphore_wait(barrier, 2)
 
     def copy(way, hop, piece, move, block, first=False):
-        rows = pl.ds(pl.multiple_of(block * high + piece * step, step), step)
+        there = place(block, piece * step, step)
         return pltpu.make_async_remote_copy(
-            src_ref=x_ref.at[pl.ds(piece * step, step)] if first else o_ref.at[rows],
-            dst_ref=o_ref.at[rows],
+            src_ref=x_ref.at[pl.ds(piece * step, step)] if first else there,
+            dst_ref=there,
             send_sem=sent.at[way, hop, piece],
             recv_sem=got.at[way, hop, piece],
             device_id={"tensor": jnp.clip(me + move, 0, last)},
@@ -251,8 +257,7 @@
         return jnp.logical_and(block >= 0, block <= last)
 
     def own():
-        rows = pl.ds(pl.multiple_of(me * high, high), high)
-        return pltpu.make_async_copy(x_ref, o_ref.at[rows], keep.at[0])
+        return pltpu.make_async_copy(x_ref, place(me, 0, high), keep.at[0])
 
     for hop in range(last):
         for piece in range(pieces):
@@ -281,13 +286,14 @@
                     copy(way, hop, piece, move, me - move * hop, hop == 0).wait_send()
 
 
-def line_gather(x, call_id, pieces=2):
+def line_gather(x, call_id, side=False, pieces=2):
     rows, cols = x.shape
+    shape = (rows, 4 * cols) if side else (4 * rows, cols)
     dma = pltpu.SemaphoreType.DMA
     vmem = pl.BlockSpec(memory_space=pltpu.VMEM)
     return pl.pallas_call(
-        functools.partial(line_gather_kernel, pieces),
-        out_shape=jax.ShapeDtypeStruct((4 * rows, cols), BF),
+        functools.partial(line_gather_kernel, pieces, side),
+        out_shape=jax.ShapeDtypeStruct(shape, BF),
         in_specs=[vmem],
         out_specs=vmem,
         scratch_shapes=[dma((2, 3, pieces)), dma((2, 3, pieces)), dma((1,))],
@@ -321,6 +327,99 @@
         out.append(whole[:, low : low + width])
         low += width
     return out
+
+
+def by_head(v, heads):
+    column = lax.broadcasted_iota(jnp.int32, v.shape, 1)
+    zero = jnp.zeros_like(v)
+    return jnp.concatenate(
+        [
+            jnp.where(jnp.logical_and(column >= h * HD, column < (h + 1) * HD), v, zero)
+            for h in range(heads)
+        ],
+        axis=0,
+    )
+
+
+def from_heads(v, heads):
+    rows = v.shape[0] // heads
+    column = lax.broadcasted_iota(jnp.int32, (rows, v.shape[1]), 1)
+    out = jnp.zeros((rows, v.shape[1]), v.dtype)
+    for h in range(heads):
+        here = jnp.logical_and(column >= h * HD, column < (h + 1) * HD)
+        out = jnp.where(here, v[h * rows : (h + 1) * rows], out)
+    return out
+
+
+def batch_parts(qkv_ref, mask_ref, batch, slots):
+    batches, rows, _ = mask_ref.shape
+    inner = qkv_ref.shape[1] // 3
+    heads = inner // HD
+    mem = slots + batch * rows
+    tok = slots + (batches + batch) * rows
+
+    def context(low):
+        cols = slice(low, low + inner)
+        return jnp.concatenate(
+            [qkv_ref[:slots, cols], qkv_ref[mem : mem + rows, cols], qkv_ref[tok : tok + rows, cols]],
+            axis=0,
+        )
+
+    query = by_head(qkv_ref[tok : tok + rows, :inner], heads)
+    keys, values = context(inner), context(2 * inner)
+    scores = dot_t(query, keys) * HD ** (-0.5)
+    allowed = jnp.concatenate([mask_ref[batch]] * heads, axis=0)
+    scores = jnp.where(allowed > 0.5, scores, NEG_LARGE)
+    high = jnp.max(scores, axis=1, keepdims=True)
+    raised = jnp.exp(scores - high)
+    weights = raised / jnp.sum(raised, axis=1, keepdims=True)
+    return query, keys, values, weights, heads
+
+
+def attend_kernel(slots, qkv_ref, mask_ref, o_ref):
+    batches, rows, _ = mask_ref.shape
+    for batch in range(batches):
+        _, _, values, weights, heads = batch_parts(qkv_ref, mask_ref, batch, slots)
+        mixed = from_heads(dot(weights.astype(BF), values), heads)
+        o_ref[batch * rows : (batch + 1) * rows, :] = mixed.astype(BF)
+
+
+def attend_back_kernel(slots, qkv_ref, mask_ref, d_ref, o_ref):
+    batches, rows, _ = mask_ref.shape
+    inner = d_ref.shape[1]
+    o_ref[: slots + batches * rows, :inner] = jnp.zeros((slots + batches * rows, inner), BF)
+    d_keys_p, d_values_p = jnp.zeros((slots, inner), F32), jnp.zeros((slots, inner), F32)
+    for batch in range(batches):
+        query, keys, values, weights, heads = batch_parts(qkv_ref, mask_ref, batch, slots)
+        mem = slots + batch * rows
+        tok = slots + (batches + batch) * rows
+        d_mixed = by_head(d_ref[batch * rows : (batch + 1) * rows, :], heads)
+        d_weights = dot_t(d_mixed, values)
+        d_values = t_dot(weights.astype(BF), d_mixed)
+        even = jnp.sum(weights * d_weights, axis=1, keepdims=True)
+        d_scores = (weights * (d_weights - even)).astype(BF)
+        d_query = from_heads(dot(d_scores, keys), heads) * HD ** (-0.5)
+        d_keys = t_dot(d_scores, query) * HD ** (-0.5)
+        o_ref[tok : tok + rows, :inner] = d_query.astype(BF)
+        d_keys_p, d_values_p = d_keys_p + d_keys[:slots], d_values_p + d_values[:slots]
+        for low, grad in ((inner, d_keys), (2 * inner, d_values)):
+            o_ref[mem : mem + rows, low : low + inner] = grad[slots : slots + rows].astype(BF)
+            o_ref[tok : tok + rows, low : low + inner] = grad[slots + rows :].astype(BF)
+    o_ref[:slots, inner : 2 * inner] = d_keys_p.astype(BF)
+    o_ref[:slots, 2 * inner :] = d_values_p.astype(BF)
+
+
+def local_call(body, shape, *operands):
+    vmem = pl.BlockSpec(memory_space=pltpu.VMEM)
+    return pl.pallas_call(
+        body,
+        out_shape=jax.ShapeDtypeStruct(shape, BF),
+        in_specs=[vmem] * len(operands),
+        out_specs=vmem,
+        compiler_params=pltpu.CompilerParams(vmem_limit_bytes=16 * GRANT),
+        cost_estimate=pl.CostEstimate(flops=0, bytes_accessed=2 * 10**7, transcendentals=0),
+        name="attend",
+    )(*operands)
 
 
 def together(*values):
@@ -402,12 +501,6 @@
     def exchange(v):
         return lax.all_to_all(v, "dp", split_axis=0, concat_axis=0, tiled=True)
 
-    def give_back(v):
-        back = lax.all_to_all(
-            t_dot(deal_m, v.astype(BF)).astype(BF), "dp", split_axis=0, concat_axis=0, tiled=True
-        )
-        return t_dot(send_m, back).astype(BF)
-
     leaving, late_in, late_mem_out = together(dot(send_m, tokens).astype(BF), mem_in, mem_out)
     w_in, w_out_t = gather(late_in, late_mem_out.T)
     arrived, tall = together(exchange(leaving), tall)
@@ -451,27 +544,14 @@
     wkm_t, wvm_t = gather(tall[:, :shard].T, tall[:, shard:].T)
     memory = chain_sum(dot_t(read_low, w_out_t))
     memory, w_attn = together(memory, w_attn)
-    wq, wk, wv, wo_t = cut_apart(w_attn, inner, inner, inner, inner)
-    query = dot(n1, wq).astype(BF)
-    key_p, value_p = dot(persistent, wk).astype(BF), dot(persistent, wv).astype(BF)
-    key_x, value_x = dot(n1, wk).astype(BF), dot(n1, wv).astype(BF)
-
-    key_m, value_m = dot(memory, wk).astype(BF), dot(memory, wv).astype(BF)
-
-    def context(p, m, t):
-        wide = jnp.broadcast_to(p[None], (batches,) + p.shape)
-        all_rows = jnp.concatenate([wide, split(m), split(t)], axis=1)
-        return all_rows.reshape(batches, -1, heads, HD)
-
-    keys, values = context(key_p, key_m, key_x), context(value_p, value_m, value_x)
+    w_qkv, wo_t = cut_apart(w_attn, 3 * inner, inner)
+    w_kv = w_attn[:, inner : 3 * inner]
+    all_rows = jnp.concatenate([persistent, memory, n1], axis=0)
+    qkv = dot(all_rows, w_qkv).astype(BF)
     allowed = jnp.concatenate(
-        [jnp.ones((batches, rows, slots), dtype=bool), causal, causal], axis=2
-    )[:, None]
-    query4 = query.reshape(batches, rows, heads, HD)
-    scores = batch_dot("bqhd,bkhd->bhqk", query4, keys) * HD ** (-0.5)
-    weights = jax.nn.softmax(jnp.where(allowed, scores, NEG_LARGE), axis=-1)
-    weights_low = weights.astype(BF)
-    mixed = batch_dot("bhqk,bkhd->bqhd", weights_low, values).astype(BF).reshape(count, inner)
+        [jnp.ones((batches, rows, slots), F32), causal.astype(F32), causal.astype(F32)], axis=2
+    )
+    mixed = local_call(functools.partial(attend_kernel, slots), (count, inner), qkv, allowed)
     mixed, late_gate, late_up, late_down, later = together(mixed, w_gate, w_up, w_down, cotangent)
     cotangent_arrived = exchange(dot(send_m, later).astype(BF))
     wg, wu, wd_t = gather(late_gate, late_up, late_down.T)
@@ -507,9 +587,7 @@
     gate, up = dot(n3, wg), dot(n3, wu)
     _, gate_silu, gate_slope = silu_parts(gate)
     ffn_act = (gate_silu * up).astype(BF)
-    ffn_own = lax.psum_scatter(
-        dot_t(ffn_act, wd_t).astype(BF), "tensor", scatter_dimension=1, tiled=True
-    )
+    ffn_part = dot_t(ffn_act, wd_t).astype(BF)
 
     d_ffn = dot(d_out_low, wd_t)
     d_gate = (d_ffn * up * gate_slope).astype(BF)
@@ -543,65 +621,53 @@
     share_ffn = lax.psum_scatter(gw_ffn, "dp", scatter_dimension=0, tiled=True)
     d_error = chain_sum(d_error_part).astype(F32)
     d_rate = jnp.sum(d_error * miss, axis=1, keepdims=True)
-    late_rate, ffn_own = together(rate, ffn_own)
-    d_miss = (late_rate * d_error).astype(BF)
+    d_miss = (rate * d_error).astype(BF)
     d_key_act = d_key_act + dot(d_miss, w_out_t)
     d_key_hidden = (d_hidden_part + d_key_act * key_slope).astype(BF)
     d_key_part = dot_t(d_key_hidden, w_in) + join(
         batch_dot("bij,bjk->bik", d_gram, split(key_mem))
         + batch_dot("bij,bik->bjk", d_gram, split(key_mem))
     )
-    result_own = give_back(own(after_mem) + ffn_own.astype(F32))
     d_key, gw_out_early = chain_sum(
         d_key_part, 6, [[(d_update, new_act), (error, d_back_pre)]]
     )
+    d_key, ffn_part = together(d_key, ffn_part)
+    ffn_own = lax.psum_scatter(ffn_part, "tensor", scatter_dimension=1, tiled=True)
     d_n2 = dot(d_key, wkm_t) - dot(d_miss, wvm_t)
     d_logit = d_rate * rate * (1.0 - rate_s)
     gg_rate = jnp.sum(n2 * d_logit, axis=0)
     d_n2 = d_n2 + d_logit * rate_w
     gg_mem = jnp.sum(d_n2 * after_attn * r2, axis=0)
-    late_r2, share_ffn, result_own = together(r2, share_ffn, result_own)
-    output = lax.all_gather(result_own, "tensor", axis=1, tiled=True)
+    late_r2, share_ffn = together(r2, share_ffn)
     d_after_attn = d_after_mem + rms_back(after_attn, late_r2, g_mem, d_n2)
     d_attn = d_after_attn.astype(BF)
 
     d_mixed = dot(d_attn, wo_t).astype(BF)
-    d_mixed4 = d_mixed.reshape(batches, rows, heads, HD)
-    d_weights = batch_dot("bqhd,bkhd->bhqk", d_mixed4, values)
-    d_values = batch_dot("bhqk,bqhd->bkhd", weights_low, d_mixed4)
-    d_scores = (
-        weights * (d_weights - jnp.sum(weights * d_weights, axis=-1, keepdims=True))
-    ).astype(BF)
-    d_query = batch_dot("bhqk,bkhd->bqhd", d_scores, keys) * HD ** (-0.5)
-    d_keys = batch_dot("bhqk,bqhd->bkhd", d_scores, query4) * HD ** (-0.5)
-    d_query = d_query.astype(BF).reshape(count, inner)
-
-    def apart(v):
-        v = v.reshape(batches, -1, inner)
-        return (
-            jnp.sum(v[:, :slots], axis=0).astype(BF),
-            join(v[:, slots : slots + rows]).astype(BF),
-            join(v[:, slots + rows :]).astype(BF),
-        )
-
-    dk_p, dk_m, dk_x = apart(d_keys)
-    dv_p, dv_m, dv_x = apart(d_values)
+    d_qkv = local_call(
+        functools.partial(attend_back_kernel, slots), qkv.shape, qkv, allowed, d_mixed
+    )
+    d_persist_rows, d_memory_rows, d_rows = (
+        d_qkv[:slots],
+        d_qkv[slots : slots + count],
+        d_qkv[slots + count :],
+    )
     d_memory, gw_attn = chain_sum(
-        dot_t(dk_m, wk) + dot_t(dv_m, wv),
+        dot_t(d_memory_rows[:, inner:], w_kv),
         3,
         [
             [(d_key, n2_own)],
             [(d_miss, n2_own)],
             [(d_attn, mixed)],
-            [(n1, d_query)],
-            [(persistent, dk_p), (memory, dk_m), (n1, dk_x)],
-            [(persistent, dv_p), (memory, dv_m), (n1, dv_x)],
+            [(all_rows, d_qkv)],
         ],
     )
-    d_n1_part = dot_t(d_query, wq) + dot_t(dk_x, wk) + dot_t(dv_x, wv)
-    d_persist_part = dot_t(dk_p, wk) + dot_t(dv_p, wv)
+    d_n1_part = dot_t(d_rows, w_qkv)
+    d_persist_part = dot_t(d_persist_rows[:, inner:], w_kv)
 
     share_attn = lax.psum_scatter(gw_attn, "dp", scatter_dimension=0, tiled=True)
+    d_memory, ffn_own = together(d_memory, ffn_own)
+    result_own = (own(after_mem) + ffn_own.astype(F32)).astype(BF)
+    result_back = exchange(t_dot(deal_m, result_own).astype(BF))
     d_read = (dot(d_memory, w_out_t) * read_slope).astype(BF)
     d_query_mem, gw_mem = chain_sum(
         dot_t(d_read, w_in),
@@ -616,8 +682,9 @@
     gw_mem = lax.dynamic_update_slice(gw_mem, gw_query_mem, (0, 2 * hidden))
     share_mem = lax.psum_scatter(gw_mem, "dp", scatter_dimension=0, tiled=True)
     d_n1_part = d_n1_part + in_own(dot(d_query_mem, wqm_t))
-    d_persist_part, share_attn, output = together(d_persist_part.astype(BF), share_attn, output)
+    d_persist_part, share_attn = together(d_persist_part.astype(BF), share_attn)
     last = chain_sum(jnp.concatenate([d_n1_part.astype(BF), d_persist_part], axis=0), 5)
+    last, result_back = together(last, result_back)
     d_n1 = last[:count].astype(F32)
     g_persist = last[count:]
     gg_attn = jnp.sum(d_n1 * x * r1, axis=0)
@@ -642,6 +709,8 @@
     came = lax.all_to_all(
         jnp.concatenate([turned, rest], axis=1), "dp", split_axis=0, concat_axis=0, tiled=True
     )
+    output = line_gather(t_dot(send_m, result_back).astype(BF), 8, True)
+    came, output = together(came, output)
     seats = count // ranks
     grad_tokens = t_dot(send_m, came[:, :seats].reshape(count, width)).astype(BF)
     share_rest = jnp.sum(came[:, seats:].astype(F32), axis=0).reshape(shard, -1)

time: 859 us -> 736 us (0.86)
  waiting for transfers between devices: 58.4 us -> 17.9 us
  matrix products: 163 us -> 127 us
  local copies, waits for them, and re-layouts: 80.9 us -> 56.2 us
  Pallas kernels: 463 us -> 447 us
    pallas_call x11, Pallas kernels: 437 us -> 389 us  [chain_sum(): pl.pallas_call(functools.partial(chain_sum_kernel, pieces, layout), out_s...]
    pallas_call x1 -> x4, Pallas kernels: 25.8 us -> 58 us  [the longest x2 51 us: line_gather(): pl.pallas_call(functools.partial(line_gather_kernel, pieces, side), out_s...]
    all_to_all x1, waiting for transfers between devices: 23.6 us -> 0.01 us  [per_device(): lax.all_to_all(jnp.concatenate([turned, rest], axis=1), 'dp', split_axis=...]
    reduce_scatter x1, waiting for transfers between devices: 19.3 us -> 2.71 us  [per_device(): share_mem = lax.psum_scatter(gw_mem, 'dp', scatter_dimension=0, tiled=True)]
    dot_general x24 -> x18, matrix products: 79.2 us -> 64.2 us  [dot(): lax.dot_general(left, right, (((1,), (0,)), ((), ())), preferred_element_...]
    dot_general x17 -> x12, matrix products: 16.8 us -> 5.76 us  [batch_dot(): return jnp.einsum(spec, left, right, preferred_element_type=F32)]
    unnamed x306 -> x255, local copies, waits for them, and re-layouts: 45.6 us -> 38 us
    dot_general x20 -> x16, matrix products: 52.7 us -> 46.1 us  [dot_t(): lax.dot_general(left, right, (((1,), (1,)), ((), ())), preferred_element_...]
  transfers between devices with their start and end apart: 14 -> 13, of which waited for: 4 -> 2; matrix products, arithmetic and copies ran while one was open for 25% -> 23% of each run, Pallas kernels for 54% -> 57%
where the time goes in v5:
time: 736 us; the launch traced here: 726 us
  Pallas kernels  447 us (61%)
  matrix products  127 us (17%)
  local copies, waits for them, and re-layouts  56.2 us (8%)
  other arithmetic  44.5 us (6%)
  starting transfers between devices  18.2 us (2%)
  waiting for transfers between devices  17.9 us (2%)
  between operations  16.1 us (2%)
    pallas_call x11, Pallas kernels, chain_sum(): pl.pallas_call(functools.partial(chain_sum_kernel, pieces, layout), out_s...  389 us
    dot_general x18, matrix products, dot(): lax.dot_general(left, right, (((1,), (0,)), ((), ())), preferred_element_...  64.2 us
    pallas_call x2, Pallas kernels, line_gather(): pl.pallas_call(functools.partial(line_gather_kernel, pieces, side), out_s...  51 us
    dot_general x16, matrix products, dot_t(): lax.dot_general(left, right, (((1,), (1,)), ((), ())), preferred_element_...  46.1 us
    unnamed x255, local copies, waits for them, and re-layouts  38 us
    all_gather x5, waiting for transfers between devices, gather_whole(): lax.all_gather(jnp.concatenate(parts, axis=1), 'dp', axis=0, tiled=True)  15 us
  transfers between devices with their start and end apart: 13, of which 2 were waited for; matrix products, arithmetic and copies ran while one was open for 23% of the time, Pallas kernels for 57%

profile of v5, /device:TPU:0, one launch (start us, length us, event | category | flops | bytes accessed | tf_op | source)
XLA Modules:
  0.0 726.1 jit_solution(4454851940285969275)
XLA Ops:
  18.4 5.3 all-to-all-start
  24.2 25.8 %line_gather.2 = bf16[1536,384]{1,0:T(8,128)(2,1)S(1)} custom-call(bf16[384,384]{1,0:T(8,128)(2,1)S(1)} %pad_maximum_fusion.8.x_ref), custom_call_target="tpu_custom_call" | custom-call | bytes 50000000 | tf_op jit(solution)/shard_map/line_gather/pallas_call | solution.py:294
  56.6 35.2 %chain_sum.11.refs_2_ = bf16[384,1536]{1,0:T(8,128)(2,1)S(1)} custom-call(bf16[384,1536]{1,0:T(8,128)(2,1)S(1)} %convolution_convert_fusion.10.x_ref), custom_call_target="tpu_custom_call" | custom-call | bytes 100000000 | tf_op jit(solution)/shard_map/chain_sum/pallas_call | solution.py:190
  92.9 14.9 %all-gather.8.cloned.1.call-done = bf16[1536,3072]{1,0:T(8,128)(2,1)} async-done(((bf16[192,3072]{1,0:T(8,128)(2,1)}), bf16[1536,3072]{1,0:T(8,128)(2,1)}) %all-gather.8.cloned.1.call-update) | async-done | bytes 9437200 | tf_op jit(solution)/shard_map/all_gather | solution.py:480
  107.8 5.9 multiply_convert_fusion.4
  124.5 38.4 %chain_sum.12 = bf16[384,1536]{1,0:T(8,128)(2,1)S(1)} custom-call(bf16[384,1536]{1,0:T(8,128)(2,1)S(1)} %convolution_convert_fusion.1.x_ref), custom_call_target="tpu_custom_call" | custom-call | bytes 100000000 | tf_op jit(solution)/shard_map/chain_sum/pallas_call | solution.py:190
  162.9 5.8 convolution_convert_fusion.qkv_ref
  182.7 37.0 %chain_sum.13 = bf16[384,1536]{1,0:T(8,128)(2,1)S(1)} custom-call(bf16[384,1536]{1,0:T(8,128)(2,1)S(1)} %convolution_convert_fusion.9.x_ref), custom_call_target="tpu_custom_call" | custom-call | bytes 100000000 | tf_op jit(solution)/shard_map/chain_sum/pallas_call | solution.py:190
  241.9 36.2 %chain_sum.14 = bf16[384,1536]{1,0:T(8,128)(2,1)S(1)} custom-call(bf16[384,1536]{1,0:T(8,128)(2,1)S(1)} %fusion.34.x_ref), custom_call_target="tpu_custom_call" | custom-call | bytes 100000000 | tf_op jit(solution)/shard_map/chain_sum/pallas_call | solution.py:190
  288.5 35.1 %chain_sum.15 = bf16[384,1536]{1,0:T(8,128)(2,1)S(1)} custom-call(bf16[384,1536]{1,0:T(8,128)(2,1)S(1)} %fusion.39.x_ref), custom_call_target="tpu_custom_call" | custom-call | bytes 100000000 | tf_op jit(solution)/shard_map/chain_sum/pallas_call | solution.py:190
  337.8 33.7 %chain_sum.16 = (bf16[384,1536]{1,0:T(8,128)(2,1)S(1)}, bf16[1536,3072]{1,0:T(8,128)(2,1)S(1)}) custom-call(bf16[384,1536]{1,0:T(8,128)(2,1)S(1)} %fusion.30.x_ref, bf16[384,1536]{1,0:T(8,128)(2,1)S(1)} %convolution_convert_fusion.7.refs_0_, bf16[384,1024]{1,0:T(8,128)(2,1)S(1)} %get-tuple-element.219.refs_1_, ...), custom_call_target="tpu_custom_call" | custom-call | bytes 100000000 | tf_op jit(solution)/shard_map/chain_sum/pallas_call | solution.py:190
  388.3 5.8 fusion.38
  399.8 32.8 %chain_sum.17 = bf16[384,1536]{1,0:T(8,128)(2,1)S(1)} custom-call(bf16[384,1536]{1,0:T(8,128)(2,1)S(1)} %fusion.40.x_ref), custom_call_target="tpu_custom_call" | custom-call | bytes 100000000 | tf_op jit(solution)/shard_map/chain_sum/pallas_call | solution.py:190
  437.1 4.7 fusion.41.refs_1_
  444.9 31.8 %chain_sum.18 = (bf16[384,1536]{1,0:T(8,128)(2,1)S(1)}, bf16[1536,1536]{1,0:T(8,128)(2,1)S(1)}) custom-call(bf16[384,1536]{1,0:T(8,128)(2,1)S(1)} %fusion.42.x_ref, bf16[384,1536]{1,0:T(8,128)(2,1)S(1)} %fusion.135.refs_0_, bf16[384,1536]{1,0:T(8,128)(2,1)S(1)} %copy-done.7, bf16[384,1536]{1,0:T(8,128)(2,1)S(1)} %copy-done.5, ...), custom_call_target="tpu_custom_call" | custom-call | bytes 100000000 | tf_op jit(solution)/shard_map/chain_sum/pallas_call | solution.py:190
  476.7 6.4 convolution_convert_fusion.6
  487.4 4.8 fusion.136
  492.3 7.2 multiply_reduce_fusion.1
  515.2 33.6 %chain_sum.19 = (bf16[384,1536]{1,0:T(8,128)(2,1)S(1)}, bf16[1536,2304]{1,0:T(8,128)(2,1)S(1)}) custom-call(bf16[384,1536]{1,0:T(8,128)(2,1)S(1)} %convolution_convert_fusion.5.x_ref, bf16[384,1536]{1,0:T(8,128)(2,1)S(1)} %copy-done.33, bf16[384,384]{1,0:T(8,128)(2,1)S(1)} %copy-done.30, bf16[384,1536]{1,0:T(8,128)(2,1)S(1)} %copy-done.11, ...), custom_call_target="tpu_custom_call" | custom-call | bytes 100000000 | tf_op jit(solution)/shard_map/chain_sum/pallas_call | solution.py:190
  554.2 5.7 fusion.46.refs_3_
  559.9 5.5 fusion.31.x_ref
  569.0 33.4 %chain_sum.20 = (bf16[384,1536]{1,0:T(8,128)(2,1)S(1)}, bf16[1536,3456]{1,0:T(8,128)(2,1)}) custom-call(bf16[384,1536]{1,0:T(8,128)(2,1)S(1)} %fusion.31.x_ref, bf16[384,1536]{1,0:T(8,128)(2,1)S(1)} %copy-done.14, bf16[384,1536]{1,0:T(8,128)(2,1)S(1)} %copy-done.39, bf16[384,1536]{1,0:T(8,128)(2,1)S(1)} %copy-done.29, bf16[384,1536]{1,0:T(8,128)(2,1)S(1)} %fusion.46.refs_3_, ...), custom_call_target="tpu_custom_call" | custom-call | bytes 100000000 | tf_op jit(solution)/shard_map/chain_sum/pallas_call | solution.py:190
  623.5 41.3 %chain_sum.21 = bf16[448,1536]{1,0:T(8,128)(2,1)S(1)} custom-call(bf16[448,1536]{1,0:T(8,128)(2,1)S(1)} %pad_maximum_fusion.3.x_ref), custom_call_target="tpu_custom_call" | custom-call | bytes 100000000 | tf_op jit(solution)/shard_map/chain_sum/pallas_call | solution.py:190
  677.8 25.2 %line_gather.3 = bf16[384,1536]{1,0:T(8,128)(2,1)S(1)} custom-call(bf16[384,384]{1,0:T(8,128)(2,1)S(1)} %convolution_convert_fusion.14.x_ref), custom_call_target="tpu_custom_call" | custom-call | bytes 50000000 | tf_op jit(solution)/shard_map/line_gather/pallas_call | solution.py:294
  (413 shorter events, 198.3 us)
Async XLA Ops:
  7.2 44.6 %all-gather.6.cloned.1.call-start = ((), (), s32[]{:S(2)}) async-start(), calls=%async_computation.8 | async-start | bytes 1769472 | tf_op jit(solution)/shard_map/all_gather | solution.py:480
  13.1 94.7 %all-gather.8.cloned.1.call-start = ((), (), s32[]{:S(2)}) async-start(), calls=%async_computation.9 | async-start | bytes 10616832 | tf_op jit(solution)/shard_map/all_gather | solution.py:480
  18.4 31.9 %all-to-all-start = ((bf16[8,48,1536]{2,1,0:T(8,128)(2,1)}), bf16[8,48,1536]{2,1,0:T(8,128)(2,1)S(1)}, u32[]{:S(2)}, u32[]{:S(2)}) async-start(bf16[8,48,1536]{2,1,0:T(8,128)(2,1)} %bitcast.3), calls=%async_computation | async-start | bytes 2359296 | tf_op jit(solution)/shard_map/all_to_all | solution.py:502
  23.7 139.2 %all-gather.10.cloned.1.call-start = ((), (), s32[]{:S(2)}) async-start(), calls=%async_computation.10 | async-start | bytes 5308416 | tf_op jit(solution)/shard_map/all_gather | solution.py:480
  92.9 132.5 %all-gather.12.cloned.1.call-start = ((), (), s32[]{:S(2)}) async-start(), calls=%async_computation.11 | async-start | bytes 10616832 | tf_op jit(solution)/shard_map/all_gather | solution.py:480
  118.1 208.1 %all-gather.14.cloned.1.call-start = ((), (), s32[]{:S(2)}) async-start(), calls=%async_computation.12 | async-start | bytes 10616832 | tf_op jit(solution)/shard_map/all_gather | solution.py:480
  119.8 49.0 %copy-start.20 = (f32[3,128,320]{2,1,0:T(8,128)}, f32[3,128,320]{2,1,0:T(8,128)S(1)}, u32[]{:S(2)}) copy-start(f32[3,128,320]{2,1,0:T(8,128)S(1)} %pad_maximum_fusion.7.mask_ref) | copy-start | bytes 1474564
  120.0 42.9 %copy-start.66 = (bf16[1536,64]{0,1:T(8,128)(2,1)}, bf16[1536,64]{0,1:T(8,128)(2,1)S(1)}, u32[]{:S(2)}) copy-start(bf16[1536,64]{0,1:T(8,128)(2,1)S(1)} %copy.113) | copy-start | bytes 589828
  124.4 38.5 %copy-start.56 = (bf16[384,1536]{1,0:T(8,128)(2,1)S(1)}, bf16[384,1536]{1,0:T(8,128)(2,1)}, u32[]{:S(2)}) copy-start(bf16[384,1536]{1,0:T(8,128)(2,1)} %copy-done.55) | copy-start | bytes 3538948
  176.4 43.3 %all-to-all-start.1 = ((bf16[8,48,1536]{2,1,0:T(8,128)(2,1)}), bf16[8,48,1536]{2,1,0:T(8,128)(2,1)S(1)}, u32[]{:S(2)}, u32[]{:S(2)}) async-start(bf16[8,48,1536]{2,1,0:T(8,128)(2,1)} %bitcast.8), calls=%async_computation.1 | async-start | bytes 2359296 | tf_op jit(solution)/shard_map/all_to_all | solution.py:502
  180.0 39.7 %copy-start.49 = (bf16[384,1536]{1,0:T(8,128)(2,1)S(1)}, bf16[384,1536]{1,0:T(8,128)(2,1)}, u32[]{:S(2)}) copy-start(bf16[384,1536]{1,0:T(8,128)(2,1)} %copy-done.48) | copy-start | bytes 3538948
  180.0 320.1 %reduce-scatter.7.cloned.1.call-start = ((), (), s32[]{:S(2)}) async-start(), calls=%async_computation.13 | async-start | bytes 10616832 | tf_op jit(solution)/shard_map/reduce_scatter | solution.py:621
  234.2 43.9 %copy-start.12 = (bf16[384,1536]{1,0:T(8,128)(2,1)}, bf16[384,1536]{1,0:T(8,128)(2,1)S(1)}, u32[]{:S(2)}) copy-start(bf16[384,1536]{1,0:T(8,128)(2,1)S(1)} %fusion.35.refs_0_) | copy-start | bytes 3538948
  236.4 46.8 %copy-start.52 = (f32[384,1536]{1,0:T(8,128)}, f32[384,1536]{1,0:T(8,128)S(1)}, u32[]{:S(2)}) copy-start(f32[384,1536]{1,0:T(8,128)S(1)} %get-tuple-element.247) | copy-start | bytes 7077892
  236.5 48.9 %copy-start.25 = (bf16[384,1536]{1,0:T(8,128)(2,1)}, bf16[384,1536]{1,0:T(8,128)(2,1)S(1)}, u32[]{:S(2)}) copy-start(bf16[384,1536]{1,0:T(8,128)(2,1)S(1)} %get-tuple-element.246.refs_5_) | copy-start | bytes 3538948
  241.9 36.7 %copy-start.108 = (f32[384]{0:T(512)S(1)}, f32[384]{0:T(512)}, u32[]{:S(2)}) copy-start(f32[384]{0:T(512)} %broadcast_multiply_fusion) | copy-start | bytes 4612
  376.2 176.7 %reduce-scatter.13.cloned.1.call-start = ((), (), s32[]{:S(2)}) async-start(), calls=%async_computation.16 | async-start | bytes 1474560
  486.8 135.1 %reduce-scatter.9.cloned.1.call-start = ((), (), s32[]{:S(2)}) async-start(), calls=%async_computation.14 | async-start | bytes 7962624 | tf_op jit(solution)/shard_map/reduce_scatter | solution.py:667
  552.7 160.9 %reduce-scatter.11.cloned.1.call-start = ((), (), s32[]{:S(2)}) async-start(), calls=%async_computation.15 | async-start | bytes 11943936 | tf_op jit(solution)/shard_map/reduce_scatter | solution.py:683
  615.3 49.5 %all-to-all-start.2 = ((bf16[8,48,384]{2,1,0:T(8,128)(2,1)}), bf16[8,48,384]{2,1,0:T(8,128)(2,1)S(1)}, u32[]{:S(2)}, u32[]{:S(2)}) async-start(bf16[8,48,384]{2,1,0:T(8,128)(2,1)} %bitcast.28), calls=%async_computation.4 | async-start | bytes 589824 | tf_op jit(solution)/shard_map/all_to_all | solution.py:502
  621.9 42.9 %copy-start.51 = (bf16[384,1536]{1,0:T(8,128)(2,1)S(1)}, bf16[384,1536]{1,0:T(8,128)(2,1)}, u32[]{:S(2)}) copy-start(bf16[384,1536]{1,0:T(8,128)(2,1)} %copy-done.48) | copy-start | bytes 3538948
  621.9 42.9 %copy-start.85 = (f32[1536]{0:T(1024)S(1)}, f32[1536]{0:T(1024)}, u32[]{:S(2)}) copy-start(f32[1536]{0:T(1024)} %copy-done.84) | copy-start | bytes 18436
  621.9 42.9 %copy-start.107 = (f32[384]{0:T(512)S(1)}, f32[384]{0:T(512)}, u32[]{:S(2)}) copy-start(f32[384]{0:T(512)} %copy-done.106) | copy-start | bytes 4612
  671.2 33.6 %all-to-all-start.3 = ((bf16[8,64,1536]{2,1,0:T(8,128)(2,1)}), bf16[8,64,1536]{2,1,0:T(8,128)(2,1)}, u32[]{:S(2)}, u32[]{:S(2)}) async-start(bf16[8,64,1536]{2,1,0:T(8,128)(2,1)} %pad_maximum_fusion.2), calls=%async_computation.5 | async-start | bytes 3145728 | tf_op jit(solution)/shard_map/all_to_all | solution.py:709
  (115 other events, 830.7 us)
Sparse Core Ops, SparseCore 0:
  13.2 34.1 all-gather.5
  49.9 57.8 all-gather.7
  110.3 38.7 all-gather.9
  151.4 71.3 all-gather.11
  224.5 58.0 all-gather.13
  376.4 76.4 reduce-scatter.6
  487.0 31.8 reduce-scatter.12
  552.9 65.7 reduce-scatter.8
  622.1 91.4 reduce-scatter.10

commit v6 on v5

--- a/solution.py
+++ b/solution.py
@@ -286,7 +286,7 @@
                     copy(way, hop, piece, move, me - move * hop, hop == 0).wait_send()
 
 
-def line_gather(x, call_id, side=False, pieces=2):
+def line_gather(x, call_id, side=False, pieces=4):
     rows, cols = x.shape
     shape = (rows, 4 * cols) if side else (4 * rows, cols)
     dma = pltpu.SemaphoreType.DMA
@@ -484,12 +484,8 @@
 
     vectors = jnp.stack([gain_attn, gain_mem, gain_ffn, w_rate], axis=1)
     pad = jnp.zeros((shard, 128 - slots - 4), BF)
-    small, wqm_t = gather(jnp.concatenate([persist.T, vectors, pad], axis=1), w_query_mem.T)
+    small = jnp.concatenate([persist.T, vectors, pad], axis=1)
     tall = line_gather(jnp.concatenate([w_key_mem, w_value_mem], axis=1), 7)
-    persistent = small[:, :slots].T
-    gains = small[:, slots : slots + 4].astype(F32).T
-    g_attn, g_mem, g_ffn, rate_w = (gains[i][None, :] for i in range(4))
-
     place = jnp.arange(count, dtype=jnp.int32)
     home = dest // count
     earlier = (home[None, :] == home[:, None]) & (place[None, :] < place[:, None])
@@ -501,10 +497,28 @@
     def exchange(v):
         return lax.all_to_all(v, "dp", split_axis=0, concat_axis=0, tiled=True)
 
-    leaving, late_in, late_mem_out = together(dot(send_m, tokens).astype(BF), mem_in, mem_out)
-    w_in, w_out_t = gather(late_in, late_mem_out.T)
-    arrived, tall = together(exchange(leaving), tall)
-    dealt = dot(deal_m, arrived).astype(BF)
+    def fold(v):
+        return v.reshape(width // v.shape[-1], -1, v.shape[-1]).swapaxes(0, 1).reshape(-1, width)
+
+    def unfold(v, columns):
+        return v.reshape(-1, width // columns, columns).swapaxes(0, 1).reshape(-1, columns)
+
+    w_in, w_out_t = gather(mem_in, mem_out.T)
+    seats = count // ranks
+    leaving = dot(send_m, tokens).astype(BF).reshape(ranks, seats, width)
+    same = jnp.concatenate([fold(w_query_mem.T), fold(small)], axis=0)
+    high = seats + shard * w_query_mem.shape[0] // width
+    arrived, tall = together(
+        exchange(jnp.concatenate([leaving, jnp.broadcast_to(same, (ranks,) + same.shape)], axis=1)),
+        tall,
+    )
+    dealt = dot(deal_m, arrived[:, :seats].reshape(count, width)).astype(BF)
+    wqm_t = jax.vmap(lambda v: unfold(v, inner))(arrived[:, seats:high]).reshape(width, inner)
+    small = jax.vmap(lambda v: unfold(v, 128))(arrived[:, high:]).reshape(width, 128)
+    persistent = small[:, :slots].T
+    gains = small[:, slots : slots + 4].astype(F32).T
+    g_attn, g_mem, g_ffn, rate_w = (gains[i][None, :] for i in range(4))
+
     x = dealt.astype(F32)
 
     position = jnp.arange(rows, dtype=jnp.int32)
@@ -532,21 +546,21 @@
         )
 
     r1 = rms(x)
-    n1 = (x * r1 * g_attn).astype(BF)
+    n1, late_query, late_key, late_value, late_output = together(
+        (x * r1 * g_attn).astype(BF), w_query, w_key, w_value, w_output
+    )
+    w_attn = gather_whole(late_query, late_key, late_value, late_output.T)
     n1_own = own(n1)
     query_mem = chain_sum(dot_t(n1_own, wqm_t))
-    query_mem, late_query, late_key, late_value, late_output = together(
-        query_mem, w_query, w_key, w_value, w_output
-    )
-    w_attn = gather_whole(late_query, late_key, late_value, late_output.T)
+    query_mem, tall = together(query_mem, tall)
+    wkm_t, wvm_t = gather(tall[:, :shard].T, tall[:, shard:].T)
     read_s, read_act, read_slope = silu_parts(dot(query_mem, w_in))
-    read_low, tall = together(read_act.astype(BF), tall)
-    wkm_t, wvm_t = gather(tall[:, :shard].T, tall[:, shard:].T)
+    read_low = read_act.astype(BF)
     memory = chain_sum(dot_t(read_low, w_out_t))
     memory, w_attn = together(memory, w_attn)
     w_qkv, wo_t = cut_apart(w_attn, 3 * inner, inner)
     w_kv = w_attn[:, inner : 3 * inner]
-    all_rows = jnp.concatenate([persistent, memory, n1], axis=0)
+    (all_rows,) = together(jnp.concatenate([persistent, memory, n1], axis=0))
     qkv = dot(all_rows, w_qkv).astype(BF)
     allowed = jnp.concatenate(
         [jnp.ones((batches, rows, slots), F32), causal.astype(F32), causal.astype(F32)], axis=2
@@ -591,7 +605,7 @@
 
     d_ffn = dot(d_out_low, wd_t)
     d_gate = (d_ffn * up * gate_slope).astype(BF)
-    d_up = (d_ffn * gate_silu).astype(BF)
+    d_up, ffn_part = together((d_ffn * gate_silu).astype(BF), ffn_part)
     d_n3, gw_ffn = chain_sum(
         dot_t(d_gate, wg) + dot_t(d_up, wu),
         2,
@@ -704,16 +718,16 @@
             jnp.zeros((width, 128 - slots - 4), BF),
         ],
         axis=1,
-    ).reshape(ranks, -1, width)
+    ).reshape(ranks, shard, -1)
+    rest = jax.vmap(fold)(rest)
     turned = t_dot(deal_m, d_x.astype(BF)).astype(BF).reshape(ranks, -1, width)
     came = lax.all_to_all(
         jnp.concatenate([turned, rest], axis=1), "dp", split_axis=0, concat_axis=0, tiled=True
     )
     output = line_gather(t_dot(send_m, result_back).astype(BF), 8, True)
     came, output = together(came, output)
-    seats = count // ranks
     grad_tokens = t_dot(send_m, came[:, :seats].reshape(count, width)).astype(BF)
-    share_rest = jnp.sum(came[:, seats:].astype(F32), axis=0).reshape(shard, -1)
+    share_rest = unfold(jnp.sum(came[:, seats:].astype(F32), axis=0), 128)
     s_small = share_rest
     s_vectors = s_small[:, slots : slots + 4].T
 

time: 736 us -> 747 us (1.015)
  Pallas kernels: 447 us -> 438 us
  waiting for transfers between devices: 17.9 us -> 26.3 us
  other arithmetic: 44.5 us -> 52 us
    all_to_all x3, waiting for transfers between devices: 0.01 us -> 18.4 us  [exchange(): return lax.all_to_all(v, 'dp', split_axis=0, concat_axis=0, tiled=True)]
    all_gather x5 -> x4, waiting for transfers between devices: 15 us -> 0.08 us  [gather_whole(): lax.all_gather(jnp.concatenate(parts, axis=1), 'dp', axis=0, tiled=True)]
    pallas_call x11, Pallas kernels: 389 us -> 380 us  [chain_sum(): pl.pallas_call(functools.partial(chain_sum_kernel, pieces, layout), out_s...]
    unnamed x255 -> x272, local copies, waits for them, and re-layouts: 38 us -> 36.6 us
  transfers between devices with their start and end apart: 13 -> 12, of which waited for: 2 -> 2; matrix products, arithmetic and copies ran while one was open for 23% -> 24% of each run, Pallas kernels for 57% -> 55%
where the time goes in v6:
time: 747 us; the launch traced here: 738 us
  Pallas kernels  438 us (59%)
  matrix products  123 us (16%)
  local copies, waits for them, and re-layouts  57.9 us (8%)
  other arithmetic  52 us (7%)
  waiting for transfers between devices  26.3 us (4%)
  starting transfers between devices  24.1 us (3%)
  between operations  16.5 us (2%)
    pallas_call x11, Pallas kernels, chain_sum(): pl.pallas_call(functools.partial(chain_sum_kernel, pieces, layout), out_s...  380 us
    dot_general x18, matrix products, dot(): lax.dot_general(left, right, (((1,), (0,)), ((), ())), preferred_element_...  64.5 us
    pallas_call x2, Pallas kernels, line_gather(): pl.pallas_call(functools.partial(line_gather_kernel, pieces, side), out_s...  51.4 us
    dot_general x16, matrix products, dot_t(): lax.dot_general(left, right, (((1,), (1,)), ((), ())), preferred_element_...  41 us
    unnamed x272, local copies, waits for them, and re-layouts  36.6 us
    all_to_all x3, starting transfers between devices, exchange(): return lax.all_to_all(v, 'dp', split_axis=0, concat_axis=0, tiled=True)  19 us
    all_to_all x3, waiting for transfers between devices, exchange(): return lax.all_to_all(v, 'dp', split_axis=0, concat_axis=0, tiled=True)  18.4 us
  transfers between devices with their start and end apart: 12, of which 2 were waited for; matrix products, arithmetic and copies ran while one was open for 24% of the time, Pallas kernels for 55%

profile of v6, /device:TPU:0, one launch (start us, length us, event | category | flops | bytes accessed | tf_op | source)
XLA Modules:
  0.0 737.9 jit_solution(12639827615532937714)
XLA Ops:
  14.3 5.3 all-to-all-start
  20.1 26.6 %line_gather.2 = bf16[1536,384]{1,0:T(8,128)(2,1)S(1)} custom-call(bf16[384,384]{1,0:T(8,128)(2,1)S(1)} %pad_maximum_fusion.9.x_ref), custom_call_target="tpu_custom_call" | custom-call | bytes 50000000 | tf_op jit(solution)/shard_map/line_gather/pallas_call | solution.py:294
  47.5 18.4 %all-to-all-done = bf16[8,112,1536]{2,1,0:T(8,128)(2,1)} async-done(((bf16[8,112,1536]{2,1,0:T(8,128)(2,1)}), bf16[8,112,1536]{2,1,0:T(8,128)(2,1)}, u32[]{:S(2)}, u32[]{:S(2)}) %all-to-all-start) | async-done | bytes 2752544 | tf_op jit(solution)/shard_map/all_to_all | solution.py:498
  81.1 34.7 %chain_sum.11.refs_2_ = bf16[384,1536]{1,0:T(8,128)(2,1)S(1)} custom-call(bf16[384,1536]{1,0:T(8,128)(2,1)S(1)} %convolution_convert_fusion.10.x_ref), custom_call_target="tpu_custom_call" | custom-call | bytes 100000000 | tf_op jit(solution)/shard_map/chain_sum/pallas_call | solution.py:190
  121.4 6.1 multiply_convert_fusion.4
  129.7 31.5 %chain_sum.12 = bf16[384,1536]{1,0:T(8,128)(2,1)S(1)} custom-call(bf16[384,1536]{1,0:T(8,128)(2,1)S(1)} %convolution_convert_fusion.1.x_ref), custom_call_target="tpu_custom_call" | custom-call | bytes 100000000 | tf_op jit(solution)/shard_map/chain_sum/pallas_call | solution.py:190
  174.0 9.7 %all-to-all-start.1 = ((bf16[8,48,1536]{2,1,0:T(8,128)(2,1)}), bf16[8,48,1536]{2,1,0:T(8,128)(2,1)}, u32[]{:S(2)}, u32[]{:S(2)}) async-start(bf16[8,48,1536]{2,1,0:T(8,128)(2,1)} %bitcast.16), calls=%async_computation.1 | async-start | bytes 2359296 | tf_op jit(solution)/shard_map/all_to_all | solution.py:498
  185.9 37.3 %chain_sum.13 = bf16[384,1536]{1,0:T(8,128)(2,1)S(1)} custom-call(bf16[384,1536]{1,0:T(8,128)(2,1)S(1)} %convolution_convert_fusion.9.x_ref), custom_call_target="tpu_custom_call" | custom-call | bytes 100000000 | tf_op jit(solution)/shard_map/chain_sum/pallas_call | solution.py:190
  235.9 5.0 multiply_convert_fusion.3
  246.4 35.8 %chain_sum.14 = bf16[384,1536]{1,0:T(8,128)(2,1)S(1)} custom-call(bf16[384,1536]{1,0:T(8,128)(2,1)S(1)} %fusion.34.x_ref), custom_call_target="tpu_custom_call" | custom-call | bytes 100000000 | tf_op jit(solution)/shard_map/chain_sum/pallas_call | solution.py:190
  292.7 34.8 %chain_sum.15 = bf16[384,1536]{1,0:T(8,128)(2,1)S(1)} custom-call(bf16[384,1536]{1,0:T(8,128)(2,1)S(1)} %fusion.39.x_ref), custom_call_target="tpu_custom_call" | custom-call | bytes 100000000 | tf_op jit(solution)/shard_map/chain_sum/pallas_call | solution.py:190
  346.7 33.7 %chain_sum.16 = (bf16[384,1536]{1,0:T(8,128)(2,1)S(1)}, bf16[1536,3072]{1,0:T(8,128)(2,1)S(1)}) custom-call(bf16[384,1536]{1,0:T(8,128)(2,1)S(1)} %fusion.30.x_ref, bf16[384,1536]{1,0:T(8,128)(2,1)S(1)} %convolution_convert_fusion.7.refs_0_, bf16[384,1024]{1,0:T(8,128)(2,1)S(1)} %get-tuple-element.198.refs_1_, ...), custom_call_target="tpu_custom_call" | custom-call | bytes 100000000 | tf_op jit(solution)/shard_map/chain_sum/pallas_call | solution.py:190
  397.4 6.8 fusion.38
  409.9 32.8 %chain_sum.17 = bf16[384,1536]{1,0:T(8,128)(2,1)S(1)} custom-call(bf16[384,1536]{1,0:T(8,128)(2,1)S(1)} %fusion.40.x_ref), custom_call_target="tpu_custom_call" | custom-call | bytes 100000000 | tf_op jit(solution)/shard_map/chain_sum/pallas_call | solution.py:190
  455.2 32.0 %chain_sum.18 = (bf16[384,1536]{1,0:T(8,128)(2,1)S(1)}, bf16[1536,1536]{1,0:T(8,128)(2,1)S(1)}) custom-call(bf16[384,1536]{1,0:T(8,128)(2,1)S(1)} %fusion.42.x_ref, bf16[384,1536]{1,0:T(8,128)(2,1)S(1)} %fusion.133.refs_0_, bf16[384,1536]{1,0:T(8,128)(2,1)S(1)} %copy-done.7, bf16[384,1536]{1,0:T(8,128)(2,1)S(1)} %copy-done.5, ...), custom_call_target="tpu_custom_call" | custom-call | bytes 100000000 | tf_op jit(solution)/shard_map/chain_sum/pallas_call | solution.py:190
  494.7 4.8 fusion.134
  499.6 7.2 multiply_reduce_fusion.1
  523.3 32.6 %chain_sum.19 = (bf16[384,1536]{1,0:T(8,128)(2,1)S(1)}, bf16[1536,2304]{1,0:T(8,128)(2,1)S(1)}) custom-call(bf16[384,1536]{1,0:T(8,128)(2,1)S(1)} %convolution_convert_fusion.5.x_ref, bf16[384,1536]{1,0:T(8,128)(2,1)S(1)} %copy-done.36, bf16[384,384]{1,0:T(8,128)(2,1)S(1)} %copy-done.33, bf16[384,1536]{1,0:T(8,128)(2,1)S(1)} %copy-done.11, ...), custom_call_target="tpu_custom_call" | custom-call | bytes 100000000 | tf_op jit(solution)/shard_map/chain_sum/pallas_call | solution.py:190
  561.3 5.4 fusion.46.refs_3_
  566.8 5.4 fusion.31.x_ref
  573.1 32.6 %chain_sum.20 = (bf16[384,1536]{1,0:T(8,128)(2,1)S(1)}, bf16[1536,3456]{1,0:T(8,128)(2,1)}) custom-call(bf16[384,1536]{1,0:T(8,128)(2,1)S(1)} %fusion.31.x_ref, bf16[384,1536]{1,0:T(8,128)(2,1)S(1)} %copy-done.14, bf16[384,1536]{1,0:T(8,128)(2,1)S(1)} %copy-done.44, bf16[384,1536]{1,0:T(8,128)(2,1)S(1)} %copy-done.32, bf16[384,1536]{1,0:T(8,128)(2,1)S(1)} %fusion.46.refs_3_, ...), custom_call_target="tpu_custom_call" | custom-call | bytes 100000000 | tf_op jit(solution)/shard_map/chain_sum/pallas_call | solution.py:190
  628.5 41.7 %chain_sum.21 = bf16[448,1536]{1,0:T(8,128)(2,1)S(1)} custom-call(bf16[448,1536]{1,0:T(8,128)(2,1)S(1)} %pad_maximum_fusion.4.x_ref), custom_call_target="tpu_custom_call" | custom-call | bytes 100000000 | tf_op jit(solution)/shard_map/chain_sum/pallas_call | solution.py:190
  684.7 24.8 %line_gather.3 = bf16[384,1536]{1,0:T(8,128)(2,1)S(1)} custom-call(bf16[384,384]{1,0:T(8,128)(2,1)S(1)} %convolution_convert_fusion.14.x_ref), custom_call_target="tpu_custom_call" | custom-call | bytes 50000000 | tf_op jit(solution)/shard_map/line_gather/pallas_call | solution.py:294
  717.5 7.6 %reduce-scatter.11.cloned.1.call-done = bf16[192,3456]{1,0:T(8,128)(2,1)} async-done(((bf16[1536,3456]{1,0:T(8,128)(2,1)}), bf16[192,3456]{1,0:T(8,128)(2,1)}) %reduce-scatter.11.cloned.1.call-update) | async-done | bytes 1327120 | tf_op jit(solution)/shard_map/reduce_scatter | solution.py:697
  (439 shorter events, 208.7 us)
Async XLA Ops:
  7.3 114.1 %all-gather.5.cloned.1.call-start = ((), (), s32[]{:S(2)}) async-start(), calls=%async_computation.8 | async-start | bytes 10616832 | tf_op jit(solution)/shard_map/all_gather | solution.py:480
  14.3 51.7 %all-to-all-start = ((bf16[8,112,1536]{2,1,0:T(8,128)(2,1)}), bf16[8,112,1536]{2,1,0:T(8,128)(2,1)}, u32[]{:S(2)}, u32[]{:S(2)}) async-start(bf16[8,112,1536]{2,1,0:T(8,128)(2,1)} %pad_maximum_fusion), calls=%async_computation | async-start | bytes 5505024 | tf_op jit(solution)/shard_map/all_to_all | solution.py:498
  19.6 141.7 %all-gather.7.cloned.1.call-start = ((), (), s32[]{:S(2)}) async-start(), calls=%async_computation.9 | async-start | bytes 5308416 | tf_op jit(solution)/shard_map/all_gather | solution.py:480
  75.7 153.0 %all-gather.9.cloned.1.call-start = ((), (), s32[]{:S(2)}) async-start(), calls=%async_computation.10 | async-start | bytes 10616832 | tf_op jit(solution)/shard_map/all_gather | solution.py:480
  120.2 212.4 %all-gather.11.cloned.1.call-start = ((), (), s32[]{:S(2)}) async-start(), calls=%async_computation.11 | async-start | bytes 10616832 | tf_op jit(solution)/shard_map/all_gather | solution.py:480
  121.1 46.3 %copy-start.25 = (f32[3,128,320]{2,1,0:T(8,128)}, f32[3,128,320]{2,1,0:T(8,128)S(1)}, u32[]{:S(2)}) copy-start(f32[3,128,320]{2,1,0:T(8,128)S(1)} %pad_maximum_fusion.8.mask_ref) | copy-start | bytes 1474564
  174.0 49.2 %all-to-all-start.1 = ((bf16[8,48,1536]{2,1,0:T(8,128)(2,1)}), bf16[8,48,1536]{2,1,0:T(8,128)(2,1)}, u32[]{:S(2)}, u32[]{:S(2)}) async-start(bf16[8,48,1536]{2,1,0:T(8,128)(2,1)} %bitcast.16), calls=%async_computation.1 | async-start | bytes 2359296 | tf_op jit(solution)/shard_map/all_to_all | solution.py:498
  183.6 39.6 %copy-start.49 = (bf16[384,1536]{1,0:T(8,128)(2,1)S(1)}, bf16[384,1536]{1,0:T(8,128)(2,1)}, u32[]{:S(2)}) copy-start(bf16[384,1536]{1,0:T(8,128)(2,1)} %copy-done.48) | copy-start | bytes 3538948
  183.6 323.7 %reduce-scatter.7.cloned.1.call-start = ((), (), s32[]{:S(2)}) async-start(), calls=%async_computation.12 | async-start | bytes 10616832 | tf_op jit(solution)/shard_map/reduce_scatter | solution.py:635
  185.9 37.8 %copy-start.88 = (f32[1536]{0:T(1024)S(1)}, f32[1536]{0:T(1024)}, u32[]{:S(2)}) copy-start(f32[1536]{0:T(1024)} %get-tuple-element.183) | copy-start | bytes 18436
  235.8 46.4 %copy-start.12 = (bf16[384,1536]{1,0:T(8,128)(2,1)}, bf16[384,1536]{1,0:T(8,128)(2,1)S(1)}, u32[]{:S(2)}) copy-start(bf16[384,1536]{1,0:T(8,128)(2,1)S(1)} %fusion.35.refs_0_) | copy-start | bytes 3538948
  240.9 46.5 %copy-start.54 = (f32[384,1536]{1,0:T(8,128)}, f32[384,1536]{1,0:T(8,128)S(1)}, u32[]{:S(2)}) copy-start(f32[384,1536]{1,0:T(8,128)S(1)} %get-tuple-element.228) | copy-start | bytes 7077892
  240.9 48.7 %copy-start.28 = (bf16[384,1536]{1,0:T(8,128)(2,1)}, bf16[384,1536]{1,0:T(8,128)(2,1)S(1)}, u32[]{:S(2)}) copy-start(bf16[384,1536]{1,0:T(8,128)(2,1)S(1)} %get-tuple-element.227.refs_5_) | copy-start | bytes 3538948
  246.4 35.8 %copy-start.84 = (pred[128,128]{1,0:T(8,128)(4,1)S(1)}, pred[128,128]{1,0:T(8,128)(4,1)}, u32[]{:S(2)}) copy-start(pred[128,128]{1,0:T(8,128)(4,1)} %copy-done.83) | copy-start | bytes 49156
  246.4 35.8 %copy-start.98 = (s32[3,128]{1,0:T(4,128)S(1)}, s32[3,128]{1,0:T(4,128)}, u32[]{:S(2)}) copy-start(s32[3,128]{1,0:T(4,128)} %copy-done.97) | copy-start | bytes 4612
  246.4 36.3 %copy-start.105 = (f32[384]{0:T(512)S(1)}, f32[384]{0:T(512)}, u32[]{:S(2)}) copy-start(f32[384]{0:T(512)} %broadcast_multiply_fusion) | copy-start | bytes 4612
  385.0 175.0 %reduce-scatter.13.cloned.1.call-start = ((), (), s32[]{:S(2)}) async-start(), calls=%async_computation.15 | async-start | bytes 1474560
  494.1 132.8 %reduce-scatter.9.cloned.1.call-start = ((), (), s32[]{:S(2)}) async-start(), calls=%async_computation.13 | async-start | bytes 7962624 | tf_op jit(solution)/shard_map/reduce_scatter | solution.py:681
  559.8 165.4 %reduce-scatter.11.cloned.1.call-start = ((), (), s32[]{:S(2)}) async-start(), calls=%async_computation.14 | async-start | bytes 11943936 | tf_op jit(solution)/shard_map/reduce_scatter | solution.py:697
  619.7 51.7 %all-to-all-start.2 = ((bf16[8,48,384]{2,1,0:T(8,128)(2,1)}), bf16[8,48,384]{2,1,0:T(8,128)(2,1)S(1)}, u32[]{:S(2)}, u32[]{:S(2)}) async-start(bf16[8,48,384]{2,1,0:T(8,128)(2,1)} %bitcast.36), calls=%async_computation.4 | async-start | bytes 589824 | tf_op jit(solution)/shard_map/all_to_all | solution.py:498
  626.9 44.5 %copy-start.51 = (bf16[384,1536]{1,0:T(8,128)(2,1)S(1)}, bf16[384,1536]{1,0:T(8,128)(2,1)}, u32[]{:S(2)}) copy-start(bf16[384,1536]{1,0:T(8,128)(2,1)} %copy-done.48) | copy-start | bytes 3538948
  626.9 44.5 %copy-start.82 = (f32[1536]{0:T(1024)S(1)}, f32[1536]{0:T(1024)}, u32[]{:S(2)}) copy-start(f32[1536]{0:T(1024)} %copy-done.81) | copy-start | bytes 18436
  626.9 44.5 %copy-start.104 = (f32[384]{0:T(512)S(1)}, f32[384]{0:T(512)}, u32[]{:S(2)}) copy-start(f32[384]{0:T(512)} %copy-done.103) | copy-start | bytes 4612
  679.1 32.4 %all-to-all-start.3 = ((bf16[8,64,1536]{2,1,0:T(8,128)(2,1)}), bf16[8,64,1536]{2,1,0:T(8,128)(2,1)S(1)}, u32[]{:S(2)}, u32[]{:S(2)}) async-start(bf16[8,64,1536]{2,1,0:T(8,128)(2,1)} %pad_maximum_fusion.3), calls=%async_computation.5 | async-start | bytes 3145728 | tf_op jit(solution)/shard_map/all_to_all | solution.py:724
  (121 other events, 588.1 us)
Sparse Core Ops, SparseCore 0:
  10.5 88.2 all-gather.4
  101.3 38.7 all-gather.6
  142.0 69.9 all-gather.8
  214.3 60.1 all-gather.10
  385.1 76.6 reduce-scatter.6
  494.2 31.6 reduce-scatter.12
  559.9 66.1 reduce-scatter.8
  629.5 95.5 reduce-scatter.10

commit v7 on v5

--- a/solution.py
+++ b/solution.py
@@ -64,8 +64,7 @@
         stage, put_sem = refs[8], refs[9]
         rows = pl.ds(pl.multiple_of(tile * TILE, TILE), TILE)
         slot = lax.rem(tile, 2)
-        target = g_ref.at[rows, pl.ds(0, stage.shape[2])]
-        return pltpu.make_async_copy(stage.at[slot], target, put_sem.at[slot])
+        return pltpu.make_async_copy(stage.at[slot], g_ref.at[rows], put_sem.at[slot])
 
     def fill(tile):
         stage = refs[8]
@@ -168,7 +167,7 @@
             down(p).wait_send()
 
 
-def chain_sum(x, call_id=1, products=(), room=0):
+def chain_sum(x, call_id=1, products=(), near=False):
     rows, cols = x.shape
     pieces = rows // 16
     dma = pltpu.SemaphoreType.DMA
@@ -183,8 +182,8 @@
     grant = 3 * rows * cols * 2 + GRANT
     if products:
         width, high = sum(w for w, _ in layout), products[0][0][0].shape[1]
-        out_shape.append(jax.ShapeDtypeStruct((high, width + room), BF))
-        out_specs.append(pl.BlockSpec(memory_space=pl.ANY))
+        out_shape.append(jax.ShapeDtypeStruct((high, width), BF))
+        out_specs.append(pl.BlockSpec(memory_space=pl.ANY if near else pltpu.HBM))
         scratch += [pltpu.VMEM((2, TILE, width), BF), dma((2,))]
         grant += 2 * TILE * width * 2 + 4 * GRANT
     out = pl.pallas_call(
@@ -546,22 +545,21 @@
     memory, w_attn = together(memory, w_attn)
     w_qkv, wo_t = cut_apart(w_attn, 3 * inner, inner)
     w_kv = w_attn[:, inner : 3 * inner]
-    all_rows = jnp.concatenate([persistent, memory, n1], axis=0)
+    (all_rows,) = together(jnp.concatenate([persistent, memory, n1], axis=0))
     qkv = dot(all_rows, w_qkv).astype(BF)
     allowed = jnp.concatenate(
         [jnp.ones((batches, rows, slots), F32), causal.astype(F32), causal.astype(F32)], axis=2
     )
     mixed = local_call(functools.partial(attend_kernel, slots), (count, inner), qkv, allowed)
-    mixed, late_gate, late_up, late_down, later = together(mixed, w_gate, w_up, w_down, cotangent)
-    cotangent_arrived = exchange(dot(send_m, later).astype(BF))
+    mixed, late_gate, late_up, late_down = together(mixed, w_gate, w_up, w_down)
     wg, wu, wd_t = gather(late_gate, late_up, late_down.T)
-    attended, cotangent_arrived = together(chain_sum(dot_t(mixed, wo_t)), cotangent_arrived)
-    after_attn = x + attended.astype(F32)
-    d_out_low = dot(deal_m, cotangent_arrived).astype(BF)
+    after_attn = x + chain_sum(dot_t(mixed, wo_t)).astype(F32)
 
     r2 = rms(after_attn)
     n2 = after_attn * r2 * g_mem
     rate_s = jax.nn.sigmoid(jnp.sum(n2 * rate_w, axis=1, keepdims=True))
+    rate_s, later = together(rate_s, cotangent)
+    cotangent_arrived = exchange(dot(send_m, later).astype(BF))
     rate = RATE_SCALE * rate_s
     n2_low = n2.astype(BF)
     n2_own = own(n2_low)
@@ -570,7 +568,11 @@
     key_hidden = dot(key_mem, w_in)
     key_s, key_silu, key_slope = silu_parts(key_hidden)
     key_act = key_silu.astype(BF)
-    miss = chain_sum(dot_t(key_act, w_out_t) - value_part).astype(F32)
+    miss, cotangent_arrived = together(
+        chain_sum(dot_t(key_act, w_out_t) - value_part), cotangent_arrived
+    )
+    miss = miss.astype(F32)
+    d_out_low = dot(deal_m, cotangent_arrived).astype(BF)
     error = (rate * miss).astype(BF)
     back_pre = dot(error, w_out_t)
     back_hidden = (back_pre * key_slope).astype(BF)
@@ -591,7 +593,7 @@
 
     d_ffn = dot(d_out_low, wd_t)
     d_gate = (d_ffn * up * gate_slope).astype(BF)
-    d_up = (d_ffn * gate_silu).astype(BF)
+    d_up, ffn_part = together((d_ffn * gate_silu).astype(BF), ffn_part)
     d_n3, gw_ffn = chain_sum(
         dot_t(d_gate, wg) + dot_t(d_up, wu),
         2,
@@ -629,7 +631,7 @@
         + batch_dot("bij,bik->bjk", d_gram, split(key_mem))
     )
     d_key, gw_out_early = chain_sum(
-        d_key_part, 6, [[(d_update, new_act), (error, d_back_pre)]]
+        d_key_part, 6, [[(d_update, new_act), (error, d_back_pre)]], True
     )
     d_key, ffn_part = together(d_key, ffn_part)
     ffn_own = lax.psum_scatter(ffn_part, "tensor", scatter_dimension=1, tiled=True)
@@ -646,13 +648,9 @@
     d_qkv = local_call(
         functools.partial(attend_back_kernel, slots), qkv.shape, qkv, allowed, d_mixed
     )
-    d_persist_rows, d_memory_rows, d_rows = (
-        d_qkv[:slots],
-        d_qkv[slots : slots + count],
-        d_qkv[slots + count :],
-    )
-    d_memory, gw_attn = chain_sum(
-        dot_t(d_memory_rows[:, inner:], w_kv),
+    d_rows = d_qkv[slots + count :]
+    d_context, gw_attn = chain_sum(
+        dot_t(d_qkv[: slots + count, inner:], w_kv),
         3,
         [
             [(d_key, n2_own)],
@@ -662,12 +660,12 @@
         ],
     )
     d_n1_part = dot_t(d_rows, w_qkv)
-    d_persist_part = dot_t(d_persist_rows[:, inner:], w_kv)
 
     share_attn = lax.psum_scatter(gw_attn, "dp", scatter_dimension=0, tiled=True)
-    d_memory, ffn_own = together(d_memory, ffn_own)
+    d_context, ffn_own = together(d_context, ffn_own)
+    g_persist, d_memory = d_context[:slots], d_context[slots:]
     result_own = (own(after_mem) + ffn_own.astype(F32)).astype(BF)
-    result_back = exchange(t_dot(deal_m, result_own).astype(BF))
+    turned_result = t_dot(deal_m, result_own).astype(BF)
     d_read = (dot(d_memory, w_out_t) * read_slope).astype(BF)
     d_query_mem, gw_mem = chain_sum(
         dot_t(d_read, w_in),
@@ -676,17 +674,20 @@
             [(key_mem, d_key_hidden), (query_mem, d_read)],
             [(d_miss, key_act), (d_memory, read_low), (gw_out_early,)],
         ],
-        inner,
-    )
-    gw_query_mem = t_dot(d_query_mem, n1_own).astype(BF)
-    gw_mem = lax.dynamic_update_slice(gw_mem, gw_query_mem, (0, 2 * hidden))
+    )
     share_mem = lax.psum_scatter(gw_mem, "dp", scatter_dimension=0, tiled=True)
-    d_n1_part = d_n1_part + in_own(dot(d_query_mem, wqm_t))
-    d_persist_part, share_attn = together(d_persist_part.astype(BF), share_attn)
-    last = chain_sum(jnp.concatenate([d_n1_part.astype(BF), d_persist_part], axis=0), 5)
+    seats = count // ranks
+    gw_query_mem = t_dot(d_query_mem, n1_own).astype(BF).reshape(ranks, shard, inner)
+    result_back = exchange(
+        jnp.concatenate([turned_result.reshape(ranks, seats, inner), gw_query_mem], axis=1)
+    )
+    late_wqm_t, share_attn = together(wqm_t, share_attn)
+    d_n1_part = d_n1_part + in_own(dot(d_query_mem, late_wqm_t))
+    last = chain_sum(d_n1_part)
     last, result_back = together(last, result_back)
-    d_n1 = last[:count].astype(F32)
-    g_persist = last[count:]
+    d_n1 = last.astype(F32)
+    s_query_mem = jnp.sum(result_back[:, seats:].astype(F32), axis=0)
+    result_back = result_back[:, :seats].reshape(count, inner)
     gg_attn = jnp.sum(d_n1 * x * r1, axis=0)
     d_x = d_after_attn + rms_back(x, r1, g_attn, d_n1)
 
@@ -695,7 +696,7 @@
 
     s_down, s_gate, s_up = cut(share_ffn, *[w_gate.shape[1]] * 3)
     s_key_mem, s_value_mem, s_output, s_query, s_key, s_value = cut(share_attn, *[inner] * 6)
-    s_in, s_out, s_query_mem = cut(share_mem, hidden, hidden, inner)
+    s_in, s_out = cut(share_mem, hidden, hidden)
     grad_vectors = jnp.stack([gg_attn, gg_mem, gg_ffn, gg_rate], axis=1)
     rest = jnp.concatenate(
         [
@@ -711,7 +712,6 @@
     )
     output = line_gather(t_dot(send_m, result_back).astype(BF), 8, True)
     came, output = together(came, output)
-    seats = count // ranks
     grad_tokens = t_dot(send_m, came[:, :seats].reshape(count, width)).astype(BF)
     share_rest = jnp.sum(came[:, seats:].astype(F32), axis=0).reshape(shard, -1)
     s_small = share_rest

time: 736 us -> 750 us (1.019)
    dot_general x16 -> x15, matrix products: 46.1 us -> 42.9 us  [dot_t(): lax.dot_general(left, right, (((1,), (1,)), ((), ())), preferred_element_...]
    unnamed x255 -> x265, local copies, waits for them, and re-layouts: 38 us -> 36.2 us
  transfers between devices with their start and end apart: 13 -> 13, of which waited for: 2 -> 2; matrix products, arithmetic and copies ran while one was open for 23% -> 24% of each run, Pallas kernels for 57% -> 56%
where the time goes in v7:
time: 750 us; the launch traced here: 739 us
  Pallas kernels  452 us (60%)
  matrix products  129 us (17%)
  local copies, waits for them, and re-layouts  60.5 us (8%)
  other arithmetic  44.6 us (6%)
  starting transfers between devices  20 us (3%)
  waiting for transfers between devices  16.5 us (2%)
  between operations  16.1 us (2%)
    pallas_call x11, Pallas kernels, chain_sum(): pl.pallas_call(functools.partial(chain_sum_kernel, pieces, layout), out_s...  394 us
    dot_general x18, matrix products, dot(): lax.dot_general(left, right, (((1,), (0,)), ((), ())), preferred_element_...  71.3 us
    pallas_call x2, Pallas kernels, line_gather(): pl.pallas_call(functools.partial(line_gather_kernel, pieces, side), out_s...  50.7 us
    dot_general x15, matrix products, dot_t(): lax.dot_general(left, right, (((1,), (1,)), ((), ())), preferred_element_...  42.9 us
    unnamed x265, local copies, waits for them, and re-layouts  36.2 us
    all_gather x5, waiting for transfers between devices, gather_whole(): lax.all_gather(jnp.concatenate(parts, axis=1), 'dp', axis=0, tiled=True)  15.3 us
  transfers between devices with their start and end apart: 13, of which 2 were waited for; matrix products, arithmetic and copies ran while one was open for 24% of the time, Pallas kernels for 56%

profile of v7, /device:TPU:0, one launch (start us, length us, event | category | flops | bytes accessed | tf_op | source)
XLA Modules:
  0.0 738.7 jit_solution(8751752549339901124)
XLA Ops:
  18.4 5.3 all-to-all-start
  24.2 25.8 %line_gather.2 = bf16[1536,384]{1,0:T(8,128)(2,1)S(1)} custom-call(bf16[384,384]{1,0:T(8,128)(2,1)S(1)} %pad_maximum_fusion.8.x_ref), custom_call_target="tpu_custom_call" | custom-call | bytes 50000000 | tf_op jit(solution)/shard_map/line_gather/pallas_call | solution.py:293
  56.2 35.2 %chain_sum.11.refs_2_ = bf16[384,1536]{1,0:T(8,128)(2,1)S(1)} custom-call(bf16[384,1536]{1,0:T(8,128)(2,1)S(1)} %convolution_convert_fusion.10.x_ref), custom_call_target="tpu_custom_call" | custom-call | bytes 100000000 | tf_op jit(solution)/shard_map/chain_sum/pallas_call | solution.py:189
  92.6 15.3 %all-gather.8.cloned.1.call-done = bf16[1536,3072]{1,0:T(8,128)(2,1)} async-done(((bf16[192,3072]{1,0:T(8,128)(2,1)}), bf16[1536,3072]{1,0:T(8,128)(2,1)}) %all-gather.8.cloned.1.call-update) | async-done | bytes 9437200 | tf_op jit(solution)/shard_map/all_gather | solution.py:479
  107.8 6.3 multiply_convert_fusion.4
  122.2 38.5 %chain_sum.12 = bf16[384,1536]{1,0:T(8,128)(2,1)S(1)} custom-call(bf16[384,1536]{1,0:T(8,128)(2,1)S(1)} %convolution_convert_fusion.2.x_ref), custom_call_target="tpu_custom_call" | custom-call | bytes 100000000 | tf_op jit(solution)/shard_map/chain_sum/pallas_call | solution.py:189
  173.2 35.9 %chain_sum.13 = bf16[384,1536]{1,0:T(8,128)(2,1)S(1)} custom-call(bf16[384,1536]{1,0:T(8,128)(2,1)S(1)} %convolution_convert_fusion.9.x_ref), custom_call_target="tpu_custom_call" | custom-call | bytes 100000000 | tf_op jit(solution)/shard_map/chain_sum/pallas_call | solution.py:189
  217.8 5.1 fusion.35.refs_0_
  222.9 6.3 multiply_convert_fusion.3
  233.4 36.8 %chain_sum.14 = bf16[384,1536]{1,0:T(8,128)(2,1)S(1)} custom-call(bf16[384,1536]{1,0:T(8,128)(2,1)S(1)} %fusion.34.x_ref), custom_call_target="tpu_custom_call" | custom-call | bytes 100000000 | tf_op jit(solution)/shard_map/chain_sum/pallas_call | solution.py:189
  272.4 6.0 multiply_convert_fusion.2
  285.3 36.4 %chain_sum.15 = bf16[384,1536]{1,0:T(8,128)(2,1)S(1)} custom-call(bf16[384,1536]{1,0:T(8,128)(2,1)S(1)} %fusion.39.x_ref), custom_call_target="tpu_custom_call" | custom-call | bytes 100000000 | tf_op jit(solution)/shard_map/chain_sum/pallas_call | solution.py:189
  339.8 34.7 %chain_sum.16 = (bf16[384,1536]{1,0:T(8,128)(2,1)S(1)}, bf16[1536,3072]{1,0:T(8,128)(2,1)S(1)}) custom-call(bf16[384,1536]{1,0:T(8,128)(2,1)S(1)} %fusion.30.x_ref, bf16[384,1536]{1,0:T(8,128)(2,1)S(1)} %convolution_convert_fusion.7.refs_0_, bf16[384,1024]{1,0:T(8,128)(2,1)S(1)} %get-tuple-element.225.refs_1_, ...), custom_call_target="tpu_custom_call" | custom-call | bytes 100000000 | tf_op jit(solution)/shard_map/chain_sum/pallas_call | solution.py:189
  389.9 5.7 fusion.38
  404.0 33.6 %chain_sum.17 = bf16[384,1536]{1,0:T(8,128)(2,1)S(1)} custom-call(bf16[384,1536]{1,0:T(8,128)(2,1)S(1)} %fusion.40.x_ref), custom_call_target="tpu_custom_call" | custom-call | bytes 100000000 | tf_op jit(solution)/shard_map/chain_sum/pallas_call | solution.py:189
  450.0 33.4 %chain_sum.18 = (bf16[384,1536]{1,0:T(8,128)(2,1)S(1)}, bf16[1536,1536]{1,0:T(8,128)(2,1)S(1)}) custom-call(bf16[384,1536]{1,0:T(8,128)(2,1)S(1)} %fusion.42.x_ref, bf16[384,1536]{1,0:T(8,128)(2,1)S(1)} %fusion.131.refs_0_, bf16[384,1536]{1,0:T(8,128)(2,1)S(1)} %copy-done.7, bf16[384,1536]{1,0:T(8,128)(2,1)S(1)} %copy-done.5, ...), custom_call_target="tpu_custom_call" | custom-call | bytes 100000000 | tf_op jit(solution)/shard_map/chain_sum/pallas_call | solution.py:189
  495.6 7.2 multiply_reduce_fusion.1
  518.7 38.5 %chain_sum.19 = (bf16[448,1536]{1,0:T(8,128)(2,1)S(1)}, bf16[1536,2304]{1,0:T(8,128)(2,1)S(1)}) custom-call(bf16[448,1536]{1,0:T(8,128)(2,1)S(1)} %convolution_convert_fusion.1.x_ref, bf16[384,1536]{1,0:T(8,128)(2,1)S(1)} %copy-done.36, bf16[384,384]{1,0:T(8,128)(2,1)S(1)} %copy-done.31, bf16[384,1536]{1,0:T(8,128)(2,1)S(1)} %copy-done.11, ...), custom_call_target="tpu_custom_call" | custom-call | bytes 100000000 | tf_op jit(solution)/shard_map/chain_sum/pallas_call | solution.py:189
  564.4 5.8 fusion.46.refs_3_
  570.3 5.4 fusion.31.x_ref
  576.1 34.1 %chain_sum.20 = (bf16[384,1536]{1,0:T(8,128)(2,1)S(1)}, bf16[1536,3072]{1,0:T(8,128)(2,1)S(1)}) custom-call(bf16[384,1536]{1,0:T(8,128)(2,1)S(1)} %fusion.31.x_ref, bf16[384,1536]{1,0:T(8,128)(2,1)S(1)} %copy-done.14, bf16[384,1536]{1,0:T(8,128)(2,1)S(1)} %copy-done.44, bf16[384,1536]{1,0:T(8,128)(2,1)S(1)} %copy-done.30, ...), custom_call_target="tpu_custom_call" | custom-call | bytes 100000000 | tf_op jit(solution)/shard_map/chain_sum/pallas_call | solution.py:189
  628.5 5.1 fusion.4
  640.4 36.8 %chain_sum.21 = bf16[384,1536]{1,0:T(8,128)(2,1)S(1)} custom-call(bf16[384,1536]{1,0:T(8,128)(2,1)S(1)} %convert_element_type.287.x_ref), custom_call_target="tpu_custom_call" | custom-call | bytes 100000000 | tf_op jit(solution)/shard_map/chain_sum/pallas_call | solution.py:189
  692.0 24.9 %line_gather.3 = bf16[384,1536]{1,0:T(8,128)(2,1)S(1)} custom-call(bf16[384,384]{1,0:T(8,128)(2,1)S(1)} %convolution_convert_fusion.13.x_ref), custom_call_target="tpu_custom_call" | custom-call | bytes 50000000 | tf_op jit(solution)/shard_map/line_gather/pallas_call | solution.py:293
  (430 shorter events, 204.4 us)
Async XLA Ops:
  7.2 44.7 %all-gather.6.cloned.1.call-start = ((), (), s32[]{:S(2)}) async-start(), calls=%async_computation.8 | async-start | bytes 1769472 | tf_op jit(solution)/shard_map/all_gather | solution.py:479
  13.1 94.7 %all-gather.8.cloned.1.call-start = ((), (), s32[]{:S(2)}) async-start(), calls=%async_computation.9 | async-start | bytes 10616832 | tf_op jit(solution)/shard_map/all_gather | solution.py:479
  18.4 31.9 %all-to-all-start = ((bf16[8,48,1536]{2,1,0:T(8,128)(2,1)}), bf16[8,48,1536]{2,1,0:T(8,128)(2,1)S(1)}, u32[]{:S(2)}, u32[]{:S(2)}) async-start(bf16[8,48,1536]{2,1,0:T(8,128)(2,1)} %bitcast), calls=%async_computation | async-start | bytes 2359296 | tf_op jit(solution)/shard_map/all_to_all | solution.py:501
  23.7 137.0 %all-gather.10.cloned.1.call-start = ((), (), s32[]{:S(2)}) async-start(), calls=%async_computation.10 | async-start | bytes 5308416 | tf_op jit(solution)/shard_map/all_gather | solution.py:479
  55.4 36.1 %copy-start.75 = (bf16[192,384]{1,0:T(8,128)(2,1)S(1)}, bf16[192,384]{1,0:T(8,128)(2,1)}, u32[]{:S(2)}) copy-start(bf16[192,384]{1,0:T(8,128)(2,1)} %param.33) | copy-start | bytes 442372
  92.5 125.3 %all-gather.12.cloned.1.call-start = ((), (), s32[]{:S(2)}) async-start(), calls=%async_computation.11 | async-start | bytes 10616832 | tf_op jit(solution)/shard_map/all_gather | solution.py:479
  116.3 209.5 %all-gather.14.cloned.1.call-start = ((), (), s32[]{:S(2)}) async-start(), calls=%async_computation.12 | async-start | bytes 10616832 | tf_op jit(solution)/shard_map/all_gather | solution.py:479
  117.0 50.0 %copy-start.22 = (f32[3,128,320]{2,1,0:T(8,128)}, f32[3,128,320]{2,1,0:T(8,128)S(1)}, u32[]{:S(2)}) copy-start(f32[3,128,320]{2,1,0:T(8,128)S(1)} %pad_maximum_fusion.7.mask_ref) | copy-start | bytes 1474564
  170.9 38.1 %copy-start.48 = (bf16[384,1536]{1,0:T(8,128)(2,1)S(1)}, bf16[384,1536]{1,0:T(8,128)(2,1)}, u32[]{:S(2)}) copy-start(bf16[384,1536]{1,0:T(8,128)(2,1)} %copy-done.47) | copy-start | bytes 3538948
  173.1 36.4 %copy-start.86 = (f32[1536]{0:T(1024)S(1)}, f32[1536]{0:T(1024)}, u32[]{:S(2)}) copy-start(f32[1536]{0:T(1024)} %get-tuple-element.210) | copy-start | bytes 18436
  212.6 57.6 %all-to-all-start.1 = ((bf16[8,48,1536]{2,1,0:T(8,128)(2,1)}), bf16[8,48,1536]{2,1,0:T(8,128)(2,1)}, u32[]{:S(2)}, u32[]{:S(2)}) async-start(bf16[8,48,1536]{2,1,0:T(8,128)(2,1)} %bitcast.10), calls=%async_computation.1 | async-start | bytes 2359296 | tf_op jit(solution)/shard_map/all_to_all | solution.py:501
  216.9 286.6 %reduce-scatter.7.cloned.1.call-start = ((), (), s32[]{:S(2)}) async-start(), calls=%async_computation.13 | async-start | bytes 10616832 | tf_op jit(solution)/shard_map/reduce_scatter | solution.py:623
  222.9 47.4 %copy-start.12 = (bf16[384,1536]{1,0:T(8,128)(2,1)}, bf16[384,1536]{1,0:T(8,128)(2,1)S(1)}, u32[]{:S(2)}) copy-start(bf16[384,1536]{1,0:T(8,128)(2,1)S(1)} %fusion.35.refs_0_) | copy-start | bytes 3538948
  285.3 36.4 %copy-start.49 = (bf16[384,1536]{1,0:T(8,128)(2,1)S(1)}, bf16[384,1536]{1,0:T(8,128)(2,1)}, u32[]{:S(2)}) copy-start(bf16[384,1536]{1,0:T(8,128)(2,1)} %copy-done.47) | copy-start | bytes 3538948
  379.2 182.4 %reduce-scatter.13.cloned.1.call-start = ((), (), s32[]{:S(2)}) async-start(), calls=%async_computation.16 | async-start | bytes 1474560
  399.4 38.2 %copy-start.60 = (bf16[384,1536]{1,0:T(8,128)(2,1)S(1)}, bf16[384,1536]{1,0:T(8,128)(2,1)}, u32[]{:S(2)}) copy-start(bf16[384,1536]{1,0:T(8,128)(2,1)} %copy-done.59) | copy-start | bytes 3538948
  399.4 42.7 %slice-start.10 = ((s8[9437184]{0:T(1024)(128)(4,1)}), s8[4194304]{0:T(1024)(128)(4,1)S(1)}, s32[]{:S(2)}) async-start(s8[9437184]{0:T(1024)(128)(4,1)} %bitcast.156), calls=%async_computation.27 | async-start | bytes 8388608
  399.4 42.7 %slice-start.11 = ((s8[9437184]{0:T(1024)(128)(4,1)}), s8[4194304]{0:T(1024)(128)(4,1)S(1)}, s32[]{:S(2)}) async-start(s8[9437184]{0:T(1024)(128)(4,1)} %bitcast.156), calls=%async_computation.28 | async-start | bytes 8388608
  490.3 145.0 %reduce-scatter.9.cloned.1.call-start = ((), (), s32[]{:S(2)}) async-start(), calls=%async_computation.14 | async-start | bytes 7962624 | tf_op jit(solution)/shard_map/reduce_scatter | solution.py:664
  561.3 166.7 %reduce-scatter.11.cloned.1.call-start = ((), (), s32[]{:S(2)}) async-start(), calls=%async_computation.15 | async-start | bytes 10616832 | tf_op jit(solution)/shard_map/reduce_scatter | solution.py:678
  620.4 56.8 %all-to-all-start.2 = ((bf16[8,240,384]{2,1,0:T(8,128)(2,1)}), bf16[8,240,384]{2,1,0:T(8,128)(2,1)}, u32[]{:S(2)}, u32[]{:S(2)}) async-start(bf16[8,240,384]{2,1,0:T(8,128)(2,1)} %pad_maximum_fusion.3), calls=%async_computation.4 | async-start | bytes 2949120 | tf_op jit(solution)/shard_map/all_to_all | solution.py:501
  638.4 38.8 %copy-start.51 = (bf16[384,1536]{1,0:T(8,128)(2,1)S(1)}, bf16[384,1536]{1,0:T(8,128)(2,1)}, u32[]{:S(2)}) copy-start(bf16[384,1536]{1,0:T(8,128)(2,1)} %copy-done.47) | copy-start | bytes 3538948
  638.4 38.8 %copy-start.80 = (f32[1536]{0:T(1024)S(1)}, f32[1536]{0:T(1024)}, u32[]{:S(2)}) copy-start(f32[1536]{0:T(1024)} %copy-done.79) | copy-start | bytes 18436
  684.3 37.7 %all-to-all-start.3 = ((bf16[8,64,1536]{2,1,0:T(8,128)(2,1)}), bf16[8,64,1536]{2,1,0:T(8,128)(2,1)}, u32[]{:S(2)}, u32[]{:S(2)}) async-start(bf16[8,64,1536]{2,1,0:T(8,128)(2,1)} %pad_maximum_fusion.2), calls=%async_computation.5 | async-start | bytes 3145728 | tf_op jit(solution)/shard_map/all_to_all | solution.py:710
  (120 other events, 721.1 us)
Sparse Core Ops, SparseCore 0:
  13.2 34.1 all-gather.5
  49.9 57.8 all-gather.7
  110.3 38.7 all-gather.9
  151.4 58.6 all-gather.11
  211.9 67.6 all-gather.13
  379.3 78.0 reduce-scatter.6
  490.4 31.7 reduce-scatter.12
  561.4 66.3 reduce-scatter.8
  631.3 91.7 reduce-scatter.10

commit v8 on v5

--- a/solution.py
+++ b/solution.py
@@ -532,21 +532,21 @@
         )
 
     r1 = rms(x)
-    n1 = (x * r1 * g_attn).astype(BF)
+    n1, late_query, late_key, late_value, late_output = together(
+        (x * r1 * g_attn).astype(BF), w_query, w_key, w_value, w_output
+    )
+    w_attn = gather_whole(late_query, late_key, late_value, late_output.T)
     n1_own = own(n1)
     query_mem = chain_sum(dot_t(n1_own, wqm_t))
-    query_mem, late_query, late_key, late_value, late_output = together(
-        query_mem, w_query, w_key, w_value, w_output
-    )
-    w_attn = gather_whole(late_query, late_key, late_value, late_output.T)
+    query_mem, tall = together(query_mem, tall)
+    wkm_t, wvm_t = gather(tall[:, :shard].T, tall[:, shard:].T)
     read_s, read_act, read_slope = silu_parts(dot(query_mem, w_in))
-    read_low, tall = together(read_act.astype(BF), tall)
-    wkm_t, wvm_t = gather(tall[:, :shard].T, tall[:, shard:].T)
+    read_low = read_act.astype(BF)
     memory = chain_sum(dot_t(read_low, w_out_t))
     memory, w_attn = together(memory, w_attn)
     w_qkv, wo_t = cut_apart(w_attn, 3 * inner, inner)
     w_kv = w_attn[:, inner : 3 * inner]
-    all_rows = jnp.concatenate([persistent, memory, n1], axis=0)
+    (all_rows,) = together(jnp.concatenate([persistent, memory, n1], axis=0))
     qkv = dot(all_rows, w_qkv).astype(BF)
     allowed = jnp.concatenate(
         [jnp.ones((batches, rows, slots), F32), causal.astype(F32), causal.astype(F32)], axis=2
@@ -646,13 +646,11 @@
     d_qkv = local_call(
         functools.partial(attend_back_kernel, slots), qkv.shape, qkv, allowed, d_mixed
     )
-    d_persist_rows, d_memory_rows, d_rows = (
-        d_qkv[:slots],
-        d_qkv[slots : slots + count],
-        d_qkv[slots + count :],
-    )
+    d_rows = d_qkv[slots + count :]
+    d_context = dot_t(d_qkv[: slots + count, inner:], w_kv).astype(BF)
+    d_persist_part = d_context[:slots]
     d_memory, gw_attn = chain_sum(
-        dot_t(d_memory_rows[:, inner:], w_kv),
+        d_context[slots:],
         3,
         [
             [(d_key, n2_own)],
@@ -662,7 +660,6 @@
         ],
     )
     d_n1_part = dot_t(d_rows, w_qkv)
-    d_persist_part = dot_t(d_persist_rows[:, inner:], w_kv)
 
     share_attn = lax.psum_scatter(gw_attn, "dp", scatter_dimension=0, tiled=True)
     d_memory, ffn_own = together(d_memory, ffn_own)

time: 736 us -> 741 us (level)
  matrix products: 127 us -> 119 us
  waiting for transfers between devices: 17.9 us -> 25.4 us
    reduce_scatter x1, waiting for transfers between devices: 2.71 us -> 14.6 us  [per_device(): share_mem = lax.psum_scatter(gw_mem, 'dp', scatter_dimension=0, tiled=True)]
    dot_general x16 -> x15, matrix products: 46.1 us -> 41.4 us  [dot_t(): lax.dot_general(left, right, (((1,), (1,)), ((), ())), preferred_element_...]
    unnamed x255 -> x253, local copies, waits for them, and re-layouts: 38 us -> 40 us
  transfers between devices with their start and end apart: 13 -> 13, of which waited for: 2 -> 4; matrix products, arithmetic and copies ran while one was open for 23% -> 22% of each run, Pallas kernels for 57% -> 57%
where the time goes in v8:
time: 741 us; the launch traced here: 731 us
  Pallas kernels  449 us (61%)
  matrix products  119 us (16%)
  local copies, waits for them, and re-layouts  60.8 us (8%)
  other arithmetic  42.4 us (6%)
  waiting for transfers between devices  25.4 us (3%)
  starting transfers between devices  18.2 us (2%)
  between operations  16 us (2%)
    pallas_call x11, Pallas kernels, chain_sum(): pl.pallas_call(functools.partial(chain_sum_kernel, pieces, layout), out_s...  392 us
    dot_general x18, matrix products, dot(): lax.dot_general(left, right, (((1,), (0,)), ((), ())), preferred_element_...  61.7 us
    pallas_call x2, Pallas kernels, line_gather(): pl.pallas_call(functools.partial(line_gather_kernel, pieces, side), out_s...  50.7 us
    dot_general x15, matrix products, dot_t(): lax.dot_general(left, right, (((1,), (1,)), ((), ())), preferred_element_...  41.4 us
    unnamed x253, local copies, waits for them, and re-layouts  40 us
  transfers between devices with their start and end apart: 13, of which 4 were waited for; matrix products, arithmetic and copies ran while one was open for 22% of the time, Pallas kernels for 57%

profile of v8, /device:TPU:0, one launch (start us, length us, event | category | flops | bytes accessed | tf_op | source)
XLA Modules:
  0.0 731.3 jit_solution(15539726668672460570)
XLA Ops:
  18.4 5.3 all-to-all-start
  24.2 25.9 %line_gather.2 = bf16[1536,384]{1,0:T(8,128)(2,1)S(1)} custom-call(bf16[384,384]{1,0:T(8,128)(2,1)S(1)} %pad_maximum_fusion.8.x_ref), custom_call_target="tpu_custom_call" | custom-call | bytes 50000000 | tf_op jit(solution)/shard_map/line_gather/pallas_call | solution.py:294
  59.1 35.3 %chain_sum.11.refs_2_ = bf16[384,1536]{1,0:T(8,128)(2,1)S(1)} custom-call(bf16[384,1536]{1,0:T(8,128)(2,1)S(1)} %convolution_convert_fusion.10.x_ref), custom_call_target="tpu_custom_call" | custom-call | bytes 100000000 | tf_op jit(solution)/shard_map/chain_sum/pallas_call | solution.py:190
  102.6 5.2 all-gather.8.cloned.1.call-done
  107.8 6.0 multiply_convert_fusion.4
  115.9 38.5 %chain_sum.12 = bf16[384,1536]{1,0:T(8,128)(2,1)S(1)} custom-call(bf16[384,1536]{1,0:T(8,128)(2,1)S(1)} %convolution_convert_fusion.2.x_ref), custom_call_target="tpu_custom_call" | custom-call | bytes 100000000 | tf_op jit(solution)/shard_map/chain_sum/pallas_call | solution.py:190
  172.6 37.0 %chain_sum.13 = bf16[384,1536]{1,0:T(8,128)(2,1)S(1)} custom-call(bf16[384,1536]{1,0:T(8,128)(2,1)S(1)} %convolution_convert_fusion.9.x_ref), custom_call_target="tpu_custom_call" | custom-call | bytes 100000000 | tf_op jit(solution)/shard_map/chain_sum/pallas_call | solution.py:190
  234.8 38.9 %chain_sum.14 = bf16[384,1536]{1,0:T(8,128)(2,1)S(1)} custom-call(bf16[384,1536]{1,0:T(8,128)(2,1)S(1)} %fusion.34.x_ref), custom_call_target="tpu_custom_call" | custom-call | bytes 100000000 | tf_op jit(solution)/shard_map/chain_sum/pallas_call | solution.py:190
  284.2 35.9 %chain_sum.15 = bf16[384,1536]{1,0:T(8,128)(2,1)S(1)} custom-call(bf16[384,1536]{1,0:T(8,128)(2,1)S(1)} %fusion.39.x_ref), custom_call_target="tpu_custom_call" | custom-call | bytes 100000000 | tf_op jit(solution)/shard_map/chain_sum/pallas_call | solution.py:190
  334.3 34.8 %chain_sum.16 = (bf16[384,1536]{1,0:T(8,128)(2,1)S(1)}, bf16[1536,3072]{1,0:T(8,128)(2,1)S(1)}) custom-call(bf16[384,1536]{1,0:T(8,128)(2,1)S(1)} %fusion.30.x_ref, bf16[384,1536]{1,0:T(8,128)(2,1)S(1)} %convolution_convert_fusion.7.refs_0_, bf16[384,1024]{1,0:T(8,128)(2,1)S(1)} %get-tuple-element.219.refs_1_, ...), custom_call_target="tpu_custom_call" | custom-call | bytes 100000000 | tf_op jit(solution)/shard_map/chain_sum/pallas_call | solution.py:190
  385.0 6.9 fusion.38
  397.5 33.9 %chain_sum.17 = bf16[384,1536]{1,0:T(8,128)(2,1)S(1)} custom-call(bf16[384,1536]{1,0:T(8,128)(2,1)S(1)} %fusion.40.x_ref), custom_call_target="tpu_custom_call" | custom-call | bytes 100000000 | tf_op jit(solution)/shard_map/chain_sum/pallas_call | solution.py:190
  443.7 32.6 %chain_sum.18 = (bf16[384,1536]{1,0:T(8,128)(2,1)S(1)}, bf16[1536,1536]{1,0:T(8,128)(2,1)S(1)}) custom-call(bf16[384,1536]{1,0:T(8,128)(2,1)S(1)} %fusion.42.x_ref, bf16[384,1536]{1,0:T(8,128)(2,1)S(1)} %fusion.133.refs_0_, bf16[384,1536]{1,0:T(8,128)(2,1)S(1)} %copy-done.7, bf16[384,1536]{1,0:T(8,128)(2,1)S(1)} %copy-done.5, ...), custom_call_target="tpu_custom_call" | custom-call | bytes 100000000 | tf_op jit(solution)/shard_map/chain_sum/pallas_call | solution.py:190
  476.3 6.5 convolution_convert_fusion.6
  487.0 4.8 fusion.134
  491.9 7.0 multiply_reduce_fusion.1
  500.2 4.7 fusion.137
  516.5 32.3 %chain_sum.19 = (bf16[384,1536]{1,0:T(8,128)(2,1)S(1)}, bf16[1536,2304]{1,0:T(8,128)(2,1)S(1)}) custom-call(bf16[384,1536]{1,0:T(8,128)(2,1)S(1)} %slice.199.x_ref, bf16[384,1536]{1,0:T(8,128)(2,1)S(1)} %copy-done.33, bf16[384,384]{1,0:T(8,128)(2,1)S(1)} %copy-done.30, bf16[384,1536]{1,0:T(8,128)(2,1)S(1)} %copy-done.11, bf16[384,384]{1,0:T(8,128)(2,1)S(1)} %copy-done.30, ...), custom_call_target="tpu_custom_call" | custom-call | bytes 100000000 | tf_op jit(solution)/shard_map/chain_sum/pallas_call | solution.py:190
  554.1 5.9 fusion.46.refs_3_
  560.0 5.4 fusion.31.x_ref
  568.9 31.0 %chain_sum.20 = (bf16[384,1536]{1,0:T(8,128)(2,1)S(1)}, bf16[1536,3456]{1,0:T(8,128)(2,1)}) custom-call(bf16[384,1536]{1,0:T(8,128)(2,1)S(1)} %fusion.31.x_ref, bf16[384,1536]{1,0:T(8,128)(2,1)S(1)} %copy-done.14, bf16[384,1536]{1,0:T(8,128)(2,1)S(1)} %copy-done.39, bf16[384,1536]{1,0:T(8,128)(2,1)S(1)} %copy-done.29, bf16[384,1536]{1,0:T(8,128)(2,1)S(1)} %fusion.46.refs_3_, ...), custom_call_target="tpu_custom_call" | custom-call | bytes 100000000 | tf_op jit(solution)/shard_map/chain_sum/pallas_call | solution.py:190
  617.5 41.6 %chain_sum.21 = bf16[448,1536]{1,0:T(8,128)(2,1)S(1)} custom-call(bf16[448,1536]{1,0:T(8,128)(2,1)S(1)} %pad_maximum_fusion.3.x_ref), custom_call_target="tpu_custom_call" | custom-call | bytes 100000000 | tf_op jit(solution)/shard_map/chain_sum/pallas_call | solution.py:190
  671.6 24.8 %line_gather.3 = bf16[384,1536]{1,0:T(8,128)(2,1)S(1)} custom-call(bf16[384,384]{1,0:T(8,128)(2,1)S(1)} %convolution_convert_fusion.13.x_ref), custom_call_target="tpu_custom_call" | custom-call | bytes 50000000 | tf_op jit(solution)/shard_map/line_gather/pallas_call | solution.py:294
  704.3 14.6 %reduce-scatter.11.cloned.1.call-done = bf16[192,3456]{1,0:T(8,128)(2,1)} async-done(((bf16[1536,3456]{1,0:T(8,128)(2,1)}), bf16[192,3456]{1,0:T(8,128)(2,1)}) %reduce-scatter.11.cloned.1.call-update) | async-done | bytes 1327120 | tf_op jit(solution)/shard_map/reduce_scatter | solution.py:680
  (412 shorter events, 200.7 us)
Async XLA Ops:
  7.2 44.6 %all-gather.6.cloned.1.call-start = ((), (), s32[]{:S(2)}) async-start(), calls=%async_computation.8 | async-start | bytes 1769472 | tf_op jit(solution)/shard_map/all_gather | solution.py:480
  13.1 94.7 %all-gather.8.cloned.1.call-start = ((), (), s32[]{:S(2)}) async-start(), calls=%async_computation.9 | async-start | bytes 10616832 | tf_op jit(solution)/shard_map/all_gather | solution.py:480
  18.4 32.0 %all-to-all-start = ((bf16[8,48,1536]{2,1,0:T(8,128)(2,1)}), bf16[8,48,1536]{2,1,0:T(8,128)(2,1)S(1)}, u32[]{:S(2)}, u32[]{:S(2)}) async-start(bf16[8,48,1536]{2,1,0:T(8,128)(2,1)} %bitcast.3), calls=%async_computation | async-start | bytes 2359296 | tf_op jit(solution)/shard_map/all_to_all | solution.py:502
  23.7 130.7 %all-gather.10.cloned.1.call-start = ((), (), s32[]{:S(2)}) async-start(), calls=%async_computation.10 | async-start | bytes 5308416 | tf_op jit(solution)/shard_map/all_gather | solution.py:480
  51.2 268.9 %copy-start.48 = (bf16[384,1536]{1,0:T(8,128)(2,1)}, bf16[384,1536]{1,0:T(8,128)(2,1)S(1)}, u32[]{:S(2)}) copy-start(bf16[384,1536]{1,0:T(8,128)(2,1)S(1)} %get-tuple-element.243) | copy-start | bytes 3538948
  56.8 162.4 %all-gather.12.cloned.1.call-start = ((), (), s32[]{:S(2)}) async-start(), calls=%async_computation.11 | async-start | bytes 10616832 | tf_op jit(solution)/shard_map/all_gather | solution.py:480
  98.7 223.9 %all-gather.14.cloned.1.call-start = ((), (), s32[]{:S(2)}) async-start(), calls=%async_computation.12 | async-start | bytes 10616832 | tf_op jit(solution)/shard_map/all_gather | solution.py:480
  99.4 61.1 %copy-start.21 = (f32[3,128,320]{2,1,0:T(8,128)}, f32[3,128,320]{2,1,0:T(8,128)S(1)}, u32[]{:S(2)}) copy-start(f32[3,128,320]{2,1,0:T(8,128)S(1)} %pad_maximum_fusion.7.mask_ref) | copy-start | bytes 1474564
  166.9 42.8 %all-to-all-start.1 = ((bf16[8,48,1536]{2,1,0:T(8,128)(2,1)}), bf16[8,48,1536]{2,1,0:T(8,128)(2,1)S(1)}, u32[]{:S(2)}, u32[]{:S(2)}) async-start(bf16[8,48,1536]{2,1,0:T(8,128)(2,1)} %bitcast.128), calls=%async_computation.1 | async-start | bytes 2359296 | tf_op jit(solution)/shard_map/all_to_all | solution.py:502
  170.5 329.1 %reduce-scatter.7.cloned.1.call-start = ((), (), s32[]{:S(2)}) async-start(), calls=%async_computation.13 | async-start | bytes 10616832 | tf_op jit(solution)/shard_map/reduce_scatter | solution.py:621
  227.0 46.7 %copy-start.12 = (bf16[384,1536]{1,0:T(8,128)(2,1)}, bf16[384,1536]{1,0:T(8,128)(2,1)S(1)}, u32[]{:S(2)}) copy-start(bf16[384,1536]{1,0:T(8,128)(2,1)S(1)} %fusion.35.refs_0_) | copy-start | bytes 3538948
  229.2 49.7 %copy-start.51 = (f32[384,1536]{1,0:T(8,128)}, f32[384,1536]{1,0:T(8,128)S(1)}, u32[]{:S(2)}) copy-start(f32[384,1536]{1,0:T(8,128)S(1)} %get-tuple-element.247) | copy-start | bytes 7077892
  229.2 51.8 %copy-start.25 = (bf16[384,1536]{1,0:T(8,128)(2,1)}, bf16[384,1536]{1,0:T(8,128)(2,1)S(1)}, u32[]{:S(2)}) copy-start(bf16[384,1536]{1,0:T(8,128)(2,1)S(1)} %get-tuple-element.246.refs_5_) | copy-start | bytes 3538948
  234.8 38.9 %copy-start.84 = (pred[128,128]{1,0:T(8,128)(4,1)S(1)}, pred[128,128]{1,0:T(8,128)(4,1)}, u32[]{:S(2)}) copy-start(pred[128,128]{1,0:T(8,128)(4,1)} %copy-done.83) | copy-start | bytes 49156
  234.8 38.9 %copy-start.97 = (s32[3,128]{1,0:T(4,128)S(1)}, s32[3,128]{1,0:T(4,128)}, u32[]{:S(2)}) copy-start(s32[3,128]{1,0:T(4,128)} %copy-done.96) | copy-start | bytes 4612
  234.8 39.4 %copy-start.104 = (f32[384]{0:T(512)S(1)}, f32[384]{0:T(512)}, u32[]{:S(2)}) copy-start(f32[384]{0:T(512)} %broadcast_multiply_fusion) | copy-start | bytes 4612
  373.7 179.2 %reduce-scatter.13.cloned.1.call-start = ((), (), s32[]{:S(2)}) async-start(), calls=%async_computation.16 | async-start | bytes 1474560
  486.4 130.9 %reduce-scatter.9.cloned.1.call-start = ((), (), s32[]{:S(2)}) async-start(), calls=%async_computation.14 | async-start | bytes 7962624 | tf_op jit(solution)/shard_map/reduce_scatter | solution.py:664
  552.7 166.2 %reduce-scatter.11.cloned.1.call-start = ((), (), s32[]{:S(2)}) async-start(), calls=%async_computation.15 | async-start | bytes 11943936 | tf_op jit(solution)/shard_map/reduce_scatter | solution.py:680
  612.3 46.8 %all-to-all-start.2 = ((bf16[8,48,384]{2,1,0:T(8,128)(2,1)}), bf16[8,48,384]{2,1,0:T(8,128)(2,1)S(1)}, u32[]{:S(2)}, u32[]{:S(2)}) async-start(bf16[8,48,384]{2,1,0:T(8,128)(2,1)} %bitcast.28), calls=%async_computation.4 | async-start | bytes 589824 | tf_op jit(solution)/shard_map/all_to_all | solution.py:502
  615.9 43.2 %copy-start.50 = (bf16[384,1536]{1,0:T(8,128)(2,1)S(1)}, bf16[384,1536]{1,0:T(8,128)(2,1)}, u32[]{:S(2)}) copy-start(bf16[384,1536]{1,0:T(8,128)(2,1)} %copy-done.48) | copy-start | bytes 3538948
  615.9 43.2 %copy-start.82 = (f32[1536]{0:T(1024)S(1)}, f32[1536]{0:T(1024)}, u32[]{:S(2)}) copy-start(f32[1536]{0:T(1024)} %copy-done.81) | copy-start | bytes 18436
  616.0 43.2 %copy-start.103 = (f32[384]{0:T(512)S(1)}, f32[384]{0:T(512)}, u32[]{:S(2)}) copy-start(f32[384]{0:T(512)} %get-tuple-element.239) | copy-start | bytes 4612
  665.3 33.0 %all-to-all-start.3 = ((bf16[8,64,1536]{2,1,0:T(8,128)(2,1)}), bf16[8,64,1536]{2,1,0:T(8,128)(2,1)}, u32[]{:S(2)}, u32[]{:S(2)}) async-start(bf16[8,64,1536]{2,1,0:T(8,128)(2,1)} %pad_maximum_fusion.2), calls=%async_computation.5 | async-start | bytes 3145728 | tf_op jit(solution)/shard_map/all_to_all | solution.py:706
  (114 other events, 636.7 us)
Sparse Core Ops, SparseCore 0:
  13.2 34.1 all-gather.5
  49.9 57.8 all-gather.7
  110.3 38.7 all-gather.9
  151.4 67.8 all-gather.11
  221.6 58.6 all-gather.13
  373.9 76.0 reduce-scatter.6
  486.6 28.4 reduce-scatter.12
  552.8 64.5 reduce-scatter.8
  620.9 97.9 reduce-scatter.10
